TPU v7x, 512 devices: a whole 4x8x8 slice. The times are simulated.
512 devices in a mesh: shot: 128 (over z, y, core), tm: 4 (over x).
Axes of the slice: x: 4, y: 8, z: 8, core: 2. Of those that a mesh axis runs over, the one named last changes fastest.
Arguments:
- records: bfloat16 [128, 4, 256, 512], P('shot', None, None, 'tm'), may hold values from -6 to 6
- fan_taps: bfloat16 [4, 15, 15], replicated, may hold values from -0.29882812 to 0.29882812
- dip_taps: bfloat16 [15, 15], replicated, may hold values from -0.29882812 to 0.29882812
- live_mask: int32 [128, 256], P('shot'), may hold values from 0 to 1, as said below
- node_place: int32 [256], replicated, may hold values from 0 to 255, as said below
- shot_place: int32 [128], replicated, may hold values from 0 to 127, as said below
Outputs:
- node_gathers: bfloat16 [128, 4, 256, 512], P(None, None, 'shot', 'tm')
Inputs may be any that keep to these rules, and one draw needn't show every extreme that they name: `live_mask`: A trace is live only where the node lies within 128 positions of the shot's point on the receiver line; some traces inside that band are dead too. `node_place`: A permutation: every position once. `shot_place`: A permutation: every position once.
All inputs are finite; a program needn't handle non-finite values.
Results may differ from a plain program's by a relative error of at most 0.0049.
Values may be sent and summed in bfloat16 or wider, within the bound.
No kernel may reach another device: no remote copies, remote signals or barrier semaphores. Data moves between devices by JAX's collectives and lax.ppermute only.
A program may use at most 64 MiB of HBM per device.

v0:
```python
import jax
import jax.numpy as jnp
from jax import lax
from jax.sharding import PartitionSpec as P


def with_halo(block, sides, width):
    for axis, dim in sides:
        count = lax.axis_size(axis)
        forward = [(i, i + 1) for i in range(count - 1)]
        backward = [(target, source) for source, target in forward]
        low = lax.ppermute(
            lax.slice_in_dim(block, block.shape[dim] - width, None, axis=dim), axis, forward
        )
        high = lax.ppermute(lax.slice_in_dim(block, 0, width, axis=dim), axis, backward)
        block = jnp.concatenate([low, block, high], axis=dim)
    return block


def tap_tables(tap_set, out_width):
    tap_count = tap_set.shape[1]
    extent = out_width + tap_count - 1
    row_iota = lax.broadcasted_iota(jnp.int32, (extent, out_width, tap_count), 0)
    col_iota = lax.broadcasted_iota(jnp.int32, (extent, out_width, tap_count), 1)
    tap_iota = lax.broadcasted_iota(jnp.int32, (extent, out_width, tap_count), 2)
    onehot = (row_iota - col_iota == tap_iota).astype(jnp.bfloat16)
    tables = jnp.einsum(
        "gab,jtb->gjat", tap_set, onehot, preferred_element_type=jnp.float32
    ).astype(jnp.bfloat16)
    return tables.reshape(tap_set.shape[0], extent, tap_count * out_width)


def shifted_total(products, along, tap_count, out_width):
    tap_reach = (tap_count - 1) // 2
    length = products.shape[along]
    split = products.reshape(products.shape[:-1] + (tap_count, out_width))
    widths = [(0, 0)] * split.ndim
    widths[along] = (tap_reach, tap_reach)
    padded = jnp.pad(split, widths)
    total = lax.slice_in_dim(padded, 0, length, axis=along)[..., 0, :]
    for offset in range(1, tap_count):
        total = (
            total + lax.slice_in_dim(padded, offset, offset + length, axis=along)[..., offset, :]
        )
    return total


def on_device(records, fan_taps, dip_taps, live_mask, node_place, shot_place):
    samples = records.shape[3]
    tap_count = fan_taps.shape[1]
    tap_reach = (tap_count - 1) // 2
    node_order = jnp.argsort(node_place)
    shot_order = jnp.argsort(shot_place)
    extended = with_halo(records, (("tm", 3),), tap_reach)
    ordered = jnp.take(extended, node_order, axis=2)
    fan_table = tap_tables(fan_taps, samples)
    fan_products = jnp.einsum(
        "scnj,cjk->scnk", ordered, fan_table, preferred_element_type=jnp.float32
    )
    fan_field = shifted_total(fan_products, 2, tap_count, samples)
    keep_mask = jnp.take(live_mask, node_order, axis=1).astype(jnp.float32)[:, None, :, None]
    fanned = (fan_field * keep_mask).astype(jnp.bfloat16)
    dip_table = tap_tables(dip_taps[None], samples)[0]
    arranged = jnp.take(
        lax.all_to_all(fanned, "shot", split_axis=2, concat_axis=0, tiled=True), shot_order, axis=0
    )
    widened = with_halo(arranged, (("tm", 3),), tap_reach)
    dip_products = jnp.dot(widened, dip_table, preferred_element_type=jnp.float32)
    result = shifted_total(dip_products, 0, tap_count, samples)
    return result.astype(jnp.bfloat16)


def solution(mesh):
    return jax.shard_map(
        on_device,
        mesh=mesh,
        in_specs=(P("shot", None, None, "tm"), P(), P(), P("shot", None), P(), P()),
        out_specs=P(None, None, "shot", "tm"),
        check_vma=False,
    )
```

profile of v0, /device:TPU:1, one launch (start us, length us, event | category | flops | bytes accessed | tf_op | source)
XLA Modules:
  0.0 88.4 jit_solution(13589727429361229150)
XLA Ops:
  0.0 0.0 copy-start
  0.0 0.0 copy-start.1
  0.0 1.2 %copy.25 = bf16[1,4,256,128]{3,1,2,0:T(4,128)(2,1)S(1)} copy(bf16[1,4,256,128]{3,2,1,0:T(8,128)(2,1)} %param.6) | data formatting | bytes 524288 | tf_op args[0]
  1.2 0.9 %fusion.45 = (bf16[1,4,256,7]{3,1,2,0:T(4,128)(2,1)}, bf16[1,4,256,7]{3,1,2,0:T(4,128)(2,1)S(1)}) fusion(bf16[1,4,256,128]{3,1,2,0:T(4,128)(2,1)S(1)} %copy.25), kind=kLoop, calls=%fused_computation.87 | loop fusion | bytes 57344 | tf_op jit(solution)/shard_map/slice | solution.py:13
  2.1 3.9 %collective-permute-start = (bf16[1,4,256,7]{3,1,2,0:T(4,128)(2,1)}, bf16[1,4,256,7]{3,1,2,0:T(4,128)(2,1)S(1)}, u32[]{:S(2)}, u32[]{:S(2)}) collective-permute-start(bf16[1,4,256,7]{3,1,2,0:T(4,128)(2,1)} %get-tuple-element.13), channel_id=1, source_target_pairs={{0,1},{1,2},{2,3},{4,5},{5,6},{6,7},{8,9},{9,10},{10,11},{12,13},{... | collective-permute-start | bytes 43016 | tf_op jit(solution)/shard_map/ppermute | solution.py:12
  6.1 1.3 %collective-permute-start.1 = (bf16[1,4,256,7]{3,1,2,0:T(4,128)(2,1)S(1)}, bf16[1,4,256,7]{3,1,2,0:T(4,128)(2,1)S(1)}, u32[]{:S(2)}, u32[]{:S(2)}) collective-permute-start(bf16[1,4,256,7]{3,1,2,0:T(4,128)(2,1)S(1)} %get-tuple-element.14), channel_id=1, source_target_pairs={{1,0},{2,1},{3,2},{5,4},{6,5},{7,6},{9,8},{10,9},{11,10},{13,12},{... | collective-permute-start | bytes 43016 | tf_op jit(solution)/shard_map/ppermute | solution.py:15
  7.4 3.9 %sort.35 = (s32[256]{0:T(256)}, s32[256]{0:T(256)S(1)}) sort(s32[256]{0:T(256)} %param.10, s32[256]{0:T(256)S(1)} %iota.39), dimensions={0}, to_apply=%region_1.2 | sort | flops 2048 | bytes 4096 | tf_op jit(solution)/shard_map/jit(argsort)/sort | solution.py:52
  11.2 1.5 %convert_bitcast_fusion = bf16[4,142,15,128]{3,2,0,1:T(8,128)(2,1)S(1)} fusion(bf16[4,15,15]{2,0,1:T(4,128)(2,1)} %param.7), kind=kOutput, calls=%fused_computation.17 | convolution fusion | flops 34352640 | bytes 2182920 | tf_op jit(solution)/shard_map/gab,jtb->gjat/dot_general | solution.py:27
  12.7 0.0 copy-done.1
  12.7 1.9 %gather_fusion.1 = s32[256]{0:T(256)S(1)} fusion(s32[256]{0:T(256)S(1)} %bitcast.54, s32[1024]{0:T(1024)S(1)} %pad_clamp_fusion.1), kind=kCustom, calls=%fused_computation.1 | custom fusion | bytes 3072 | tf_op jit(solution)/shard_map/jit(_take)/gather | solution.py:61
  14.7 0.0 copy-start.3
  14.7 2.8 %reshape.295 = bf16[4,142,1920]{2,0,1:T(4,128)(2,1)} reshape(bf16[4,142,15,128]{3,2,0,1:T(8,128)(2,1)S(1)} %convert_bitcast_fusion) | data formatting | bytes 4362240 | tf_op jit(solution)/shard_map/reshape | solution.py:30
  17.5 0.0 copy-start.2
  17.5 0.0 copy-done.3
  17.6 2.5 %sort.34 = (s32[128]{0:T(128)}, s32[128]{0:T(128)S(1)}) sort(s32[128]{0:T(128)S(1)} %copy-done.3, s32[128]{0:T(128)S(1)} %iota.35), dimensions={0}, to_apply=%region_0.0 | sort | flops 896 | bytes 2048 | tf_op jit(solution)/shard_map/jit(argsort)/sort | solution.py:53
  20.1 0.0 collective-permute-done
  20.1 0.0 collective-permute-done.1
  20.1 0.7 maximum_bitcast_fusion
  20.8 1.2 %gather_fusion = bf16[256,4,142]{2,1,0:T(4,128)(2,1)S(1)} fusion(bf16[4,256,142]{2,0,1:T(4,128)(2,1)S(1)} %maximum_bitcast_fusion, s32[1024]{0:T(1024)S(1)} %pad_clamp_fusion.1), kind=kCustom, calls=%fused_computation | custom fusion | bytes 582656 | tf_op jit(solution)/shard_map/jit(_take)/gather | solution.py:55
  22.0 0.9 %select_bitcast_fusion = bf16[4,256,142]{2,0,1:T(4,128)(2,1)S(1)} fusion(bf16[256,4,142]{2,1,0:T(4,128)(2,1)S(1)} %gather_fusion, pred[256]{0:T(512)(128)(4,1)S(1)} %get-tuple-element.10), kind=kLoop, calls=%fused_computation.52 | loop fusion | flops 145408 | bytes 581888 | tf_op jit(solution)/shard_map/jit(_take)/select_n | solution.py:55
  22.9 0.0 copy-done.2
  22.9 4.8 %fusion = f32[4,1920,256]{2,1,0:T(8,128)} fusion(bf16[4,142,1920]{2,0,1:T(4,128)(2,1)S(1)} %copy-done.2, bf16[4,256,142]{2,0,1:T(4,128)(2,1)S(1)} %select_bitcast_fusion), kind=kOutput, calls=%fused_computation.18 | convolution fusion | flops 558366720 | bytes 10336256 | tf_op jit(solution)/shard_map/scnj,cjk->scnk/dot_general | solution.py:57
  27.7 9.7 %copy.29 = f32[1,4,256,15,128]{4,1,2,3,0:T(4,128)} copy(f32[1,4,256,15,128]{2,4,3,1,0:T(8,128)} %bitcast.55) | data formatting | bytes 15728640 | tf_op jit(solution)/shard_map/reshape | solution.py:36
  37.4 4.7 %fusion.28 = bf16[1,4,256,128]{3,1,0,2:T(4,128)(2,1)} fusion(f32[1,4,256,15,128]{4,1,2,3,0:T(4,128)} %copy.29, f32[256]{0:T(256)S(1)} %get-tuple-element.9), kind=kLoop, calls=%fused_computation.50 | loop fusion | flops 2097152 | bytes 8651776 | tf_op jit(solution)/shard_map/convert_element_type | solution.py:62
  42.1 17.9 %all-to-all-start = ((bf16[1,4,256,128]{3,1,0,2:T(4,128)(2,1)}), bf16[1,4,256,128]{3,1,0,2:T(4,128)(2,1)S(1)}, u32[]{:S(2)}, u32[]{:S(2)}) async-start(bf16[1,4,256,128]{3,1,0,2:T(4,128)(2,1)} %fusion.28), calls=%async_computation | async-start | bytes 524288 | tf_op jit(solution)/shard_map/all_to_all | solution.py:65
  60.0 15.2 %all-to-all-done = bf16[1,4,256,128]{3,1,0,2:T(4,128)(2,1)S(1)} async-done(((bf16[1,4,256,128]{3,1,0,2:T(4,128)(2,1)}), bf16[1,4,256,128]{3,1,0,2:T(4,128)(2,1)S(1)}, u32[]{:S(2)}, u32[]{:S(2)}) %all-to-all-start) | async-done | bytes 262176 | tf_op jit(solution)/shard_map/all_to_all | solution.py:65
  75.2 0.8 gather_fusion.2
  76.1 0.2 copy.33
  76.4 4.3 %collective-permute-start.2 = (bf16[128,4,2,7]{0,3,2,1:T(8,128)(2,1)S(1)}, bf16[128,4,2,7]{0,3,2,1:T(8,128)(2,1)S(1)}, u32[]{:S(2)}, u32[]{:S(2)}) collective-permute-start(bf16[128,4,2,7]{0,3,2,1:T(8,128)(2,1)S(1)} %get-tuple-element.11), channel_id=1, source_target_pairs={{0,1},{1,2},{2,3},{4,5},{5,6},{6,7},{8,9},{9,10},{10,11},{12,13},{... | collective-permute-start | bytes 43016 | tf_op jit(solution)/shard_map/ppermute | solution.py:12
  80.6 1.5 %collective-permute-start.3 = (bf16[128,4,2,7]{0,3,2,1:T(8,128)(2,1)S(1)}, bf16[128,4,2,7]{0,3,2,1:T(8,128)(2,1)S(1)}, u32[]{:S(2)}, u32[]{:S(2)}) collective-permute-start(bf16[128,4,2,7]{0,3,2,1:T(8,128)(2,1)S(1)} %get-tuple-element.12), channel_id=1, source_target_pairs={{1,0},{2,1},{3,2},{5,4},{6,5},{7,6},{9,8},{10,9},{11,10},{13,12},{... | collective-permute-start | bytes 43016 | tf_op jit(solution)/shard_map/ppermute | solution.py:15
  82.1 0.0 copy-done
  82.1 0.4 fusion.2
  82.5 0.1 pad.19
  82.6 0.2 copy.43
  82.8 0.4 dot_general.23
  83.3 0.0 collective-permute-done.2
  83.3 1.8 %collective-permute-done.3 = bf16[128,4,2,7]{0,3,2,1:T(8,128)(2,1)S(1)} collective-permute-done((bf16[128,4,2,7]{0,3,2,1:T(8,128)(2,1)S(1)}, bf16[128,4,2,7]{0,3,2,1:T(8,128)(2,1)S(1)}, u32[]{:S(2)}, u32[]{:S(2)}) %collective-permute-start.3) | collective-permute-done | bytes 14368 | tf_op jit(solution)/shard_map/ppermute | solution.py:15
  85.1 1.3 %fusion.5 = f32[128,4,2,15,128]{4,0,3,2,1:T(8,128)S(1)} fusion(bf16[15,128,142,1,1]{1,0,2,4,3:T(8,128)(2,1)S(1)} %bitcast.57, bf16[128,4,2,7]{0,3,2,1:T(8,128)(2,1)S(1)} %collective-permute-done.3, bf16[128,4,2,128]{0,3,2,1:T(8,128)(2,1)S(1)} %broadcast_select_fusion, bf16[128,4,2,7]{0,3,2,1:T(8,128)(2,1)S(1)} %collective-permute-done.2), kind=kOutput, calls=%fused_computation.24 | convolution fusion | flops 559239168 | bytes 8700416 | tf_op jit(solution)/shard_map/dot_general | solution.py:68
  86.4 1.0 %fusion.39 = bf16[128,4,2,128]{3,0,2,1:T(8,128)(2,1)S(1)} fusion(f32[128,4,2,15,128]{4,0,3,2,1:T(8,128)S(1)} %fusion.5), kind=kLoop, calls=%fused_computation.74 | loop fusion | flops 1966080 | bytes 8650752 | tf_op jit(solution)/shard_map/convert_element_type | solution.py:70
  87.4 1.0 %copy.35 = bf16[128,4,2,128]{3,2,1,0:T(2,128)(2,1)} copy(bf16[128,4,2,128]{3,0,2,1:T(8,128)(2,1)S(1)} %fusion.39) | data formatting | bytes 524288 | tf_op jit(solution)/shard_map/convert_element_type | solution.py:70
  (10 shorter events, 0.1 us)
Async XLA Ops:
  0.0 82.1 %copy-start = (bf16[15,15]{1,0:T(8,128)(2,1)S(1)}, bf16[15,15]{1,0:T(8,128)(2,1)}, u32[]{:S(2)}) copy-start(bf16[15,15]{1,0:T(8,128)(2,1)} %param.8) | copy-start | bytes 1354
  0.0 12.7 %copy-start.1 = (s32[1,256]{1,0:T(1,128)S(1)}, s32[1,256]{1,0:T(1,128)}, u32[]{:S(2)}) copy-start(s32[1,256]{1,0:T(1,128)} %param.9) | copy-start | bytes 3076
  2.1 18.0 %collective-permute-start = (bf16[1,4,256,7]{3,1,2,0:T(4,128)(2,1)}, bf16[1,4,256,7]{3,1,2,0:T(4,128)(2,1)S(1)}, u32[]{:S(2)}, u32[]{:S(2)}) collective-permute-start(bf16[1,4,256,7]{3,1,2,0:T(4,128)(2,1)} %get-tuple-element.13), channel_id=1, source_target_pairs={{0,1},{1,2},{2,3},{4,5},{5,6},{6,7},{8,9},{9,10},{10,11},{12,13},{... | collective-permute-start | bytes 43016 | tf_op jit(solution)/shard_map/ppermute | solution.py:12
  6.1 14.0 %collective-permute-start.1 = (bf16[1,4,256,7]{3,1,2,0:T(4,128)(2,1)S(1)}, bf16[1,4,256,7]{3,1,2,0:T(4,128)(2,1)S(1)}, u32[]{:S(2)}, u32[]{:S(2)}) collective-permute-start(bf16[1,4,256,7]{3,1,2,0:T(4,128)(2,1)S(1)} %get-tuple-element.14), channel_id=1, source_target_pairs={{1,0},{2,1},{3,2},{5,4},{6,5},{7,6},{9,8},{10,9},{11,10},{13,12},{... | collective-permute-start | bytes 43016 | tf_op jit(solution)/shard_map/ppermute | solution.py:15
  14.7 2.8 %copy-start.3 = (s32[128]{0:T(128)S(1)}, s32[128]{0:T(128)}, u32[]{:S(2)}) copy-start(s32[128]{0:T(128)} %param.11) | copy-start | bytes 1540
  17.5 5.4 %copy-start.2 = (bf16[4,142,1920]{2,0,1:T(4,128)(2,1)S(1)}, bf16[4,142,1920]{2,0,1:T(4,128)(2,1)}, u32[]{:S(2)}) copy-start(bf16[4,142,1920]{2,0,1:T(4,128)(2,1)} %reshape.295) | copy-start | bytes 6543364
  42.1 33.1 %all-to-all-start = ((bf16[1,4,256,128]{3,1,0,2:T(4,128)(2,1)}), bf16[1,4,256,128]{3,1,0,2:T(4,128)(2,1)S(1)}, u32[]{:S(2)}, u32[]{:S(2)}) async-start(bf16[1,4,256,128]{3,1,0,2:T(4,128)(2,1)} %fusion.28), calls=%async_computation | async-start | bytes 524288 | tf_op jit(solution)/shard_map/all_to_all | solution.py:65
  76.4 6.9 %collective-permute-start.2 = (bf16[128,4,2,7]{0,3,2,1:T(8,128)(2,1)S(1)}, bf16[128,4,2,7]{0,3,2,1:T(8,128)(2,1)S(1)}, u32[]{:S(2)}, u32[]{:S(2)}) collective-permute-start(bf16[128,4,2,7]{0,3,2,1:T(8,128)(2,1)S(1)} %get-tuple-element.11), channel_id=1, source_target_pairs={{0,1},{1,2},{2,3},{4,5},{5,6},{6,7},{8,9},{9,10},{10,11},{12,13},{... | collective-permute-start | bytes 43016 | tf_op jit(solution)/shard_map/ppermute | solution.py:12
  80.6 4.5 %collective-permute-start.3 = (bf16[128,4,2,7]{0,3,2,1:T(8,128)(2,1)S(1)}, bf16[128,4,2,7]{0,3,2,1:T(8,128)(2,1)S(1)}, u32[]{:S(2)}, u32[]{:S(2)}) collective-permute-start(bf16[128,4,2,7]{0,3,2,1:T(8,128)(2,1)S(1)} %get-tuple-element.12), channel_id=1, source_target_pairs={{1,0},{2,1},{3,2},{5,4},{6,5},{7,6},{9,8},{10,9},{11,10},{13,12},{... | collective-permute-start | bytes 43016 | tf_op jit(solution)/shard_map/ppermute | solution.py:15
where the time goes:
time: 89.2 us; the launch traced here: 88.4 us
  starting transfers between devices  28.9 us (32%)
  local copies, waits for them, and re-layouts  20.5 us (23%)
  waiting for transfers between devices  17.1 us (19%)
  other arithmetic  13.8 us (15%)
  matrix products  7.92 us (9%)
    all_to_all x1, starting transfers between devices, on_device(): lax.all_to_all(fanned, 'shot', split_axis=2, concat_axis=0, tiled=True)  17.9 us
    all_to_all x1, waiting for transfers between devices, on_device(): lax.all_to_all(fanned, 'shot', split_axis=2, concat_axis=0, tiled=True)  15.2 us
    reshape x1, local copies, waits for them, and re-layouts, shifted_total(): split = products.reshape(products.shape[:-1] + (tap_count, out_width))  9.71 us
    ppermute x2, starting transfers between devices, with_halo(): lax.ppermute(lax.slice_in_dim(block, block.shape[dim] - width, None, axis...  8.21 us
    dot_general x1, matrix products, on_device(): jnp.einsum('scnj,cjk->scnk', ordered, fan_table, preferred_element_type=j...  4.75 us
    convert_element_type x1, other arithmetic, on_device(): fanned = (fan_field * keep_mask).astype(jnp.bfloat16)  4.68 us
    sort x1, other arithmetic, on_device(): node_order = jnp.argsort(node_place)  3.87 us
    reshape x1, local copies, waits for them, and re-layouts, tap_tables(): return tables.reshape(tap_set.shape[0], extent, tap_count * out_width)  2.83 us
  transfers between devices with their start and end apart: 5, of which 2 were waited for; matrix products, arithmetic and copies ran while one was open for 16% of the time, Pallas kernels for 0%

commit v1 on v0

v1 whole, which is shorter than its diff:
```python
import functools

import jax
import jax.numpy as jnp
from jax import lax
from jax.experimental import pallas as pl
from jax.experimental.pallas import tpu as pltpu
from jax.sharding import PartitionSpec as P

LANES = 128
EXT = 256


def time_halo(block, axis, width):
    count = lax.axis_size(axis)
    forward = [(i, i + 1) for i in range(count - 1)]
    backward = [(target, source) for source, target in forward]
    samples = block.shape[-1]
    low = lax.ppermute(lax.slice_in_dim(block, samples - width, None, axis=-1), axis, forward)
    high = lax.ppermute(lax.slice_in_dim(block, 0, width, axis=-1), axis, backward)
    return low, high


def extend(block, low, high, extra=None):
    parts = [block, low, high]
    if extra is not None:
        parts.append(extra)
    used = sum(p.shape[-1] for p in parts)
    pad = jnp.zeros(block.shape[:-1] + (EXT - used,), block.dtype)
    return jnp.concatenate(parts + [pad], axis=-1)


def toeplitz(tap_set, samples, width):
    taps = tap_set.shape[-1]
    j = jnp.arange(EXT, dtype=jnp.int32)
    time_of = jnp.where(
        j < samples,
        j,
        jnp.where(j < samples + width, j - samples - width, jnp.where(j < samples + 2 * width, j - width, 1 << 20)),
    )
    t = jnp.arange(samples, dtype=jnp.int32)
    b = time_of[:, None] - t[None, :] + width
    onehot = (b[:, :, None] == jnp.arange(taps, dtype=jnp.int32)[None, None, :]).astype(jnp.bfloat16)
    tables = jnp.einsum("gab,jtb->gajt", tap_set, onehot, preferred_element_type=jnp.float32)
    return tables.astype(jnp.bfloat16)


def fan_kernel(place_ref, ext_ref, table_ref, out_ref, scr_ref, *, taps, live_col):
    rows = ext_ref.shape[1]
    reach = (taps - 1) // 2
    place = place_ref[...]
    select = (lax.broadcasted_iota(jnp.int32, (rows, rows), 0) == place).astype(jnp.bfloat16)
    ordered = jnp.dot(select, ext_ref[0], preferred_element_type=jnp.float32)
    keep = ordered[:, live_col:live_col + 1]
    ordered = ordered.astype(jnp.bfloat16)
    scr_ref[0:8, :] = jnp.zeros((8, LANES), jnp.float32)
    scr_ref[rows + 8:rows + 16, :] = jnp.zeros((8, LANES), jnp.float32)
    acc = jnp.zeros((rows, LANES), jnp.float32)
    for a in range(taps):
        part = jnp.dot(ordered, table_ref[0, a], preferred_element_type=jnp.float32)
        scr_ref[8:rows + 8, :] = part
        acc = acc + scr_ref[pl.ds(a + 8 - reach, rows), :]
    out_ref[0] = (acc * keep).astype(out_ref.dtype)


def dip_kernel(target_ref, ext_ref, table_ref, out_ref, scr_ref, *, taps, group):
    rows = ext_ref.shape[1]
    reach = (taps - 1) // 2
    pad = group * 8
    target = target_ref[...]
    select = (lax.broadcasted_iota(jnp.int32, (rows, rows), 0) == target).astype(jnp.bfloat16)
    ordered = jnp.dot(select, ext_ref[0], preferred_element_type=jnp.float32).astype(jnp.bfloat16)
    scr_ref[0:pad, :] = jnp.zeros((pad, LANES), jnp.float32)
    scr_ref[rows + pad:rows + 2 * pad, :] = jnp.zeros((pad, LANES), jnp.float32)
    acc = jnp.zeros((rows, LANES), jnp.float32)
    for a in range(taps):
        part = jnp.dot(ordered, table_ref[a], preferred_element_type=jnp.float32)
        scr_ref[pad:rows + pad, :] = part
        acc = acc + scr_ref[pl.ds(pad + group * (a - reach), rows), :]
    out_ref[0] = acc.astype(out_ref.dtype)


def fan_call(place, ext, tables):
    comps, rows, _ = ext.shape
    taps = tables.shape[1]
    samples = tables.shape[3]
    kernel = functools.partial(fan_kernel, taps=taps, live_col=samples + taps - 1)
    return pl.pallas_call(
        kernel,
        grid=(comps,),
        in_specs=[
            pl.BlockSpec((1, rows), lambda c: (0, 0)),
            pl.BlockSpec((1, rows, EXT), lambda c: (c, 0, 0)),
            pl.BlockSpec((1, taps, EXT, samples), lambda c: (c, 0, 0, 0)),
        ],
        out_specs=pl.BlockSpec((1, rows, samples), lambda c: (c, 0, 0)),
        out_shape=jax.ShapeDtypeStruct((comps, rows, samples), jnp.bfloat16),
        scratch_shapes=[pltpu.VMEM((rows + 16, LANES), jnp.float32)],
    )(place, ext, tables)


def dip_call(target, ext, tables, group):
    comps, rows, _ = ext.shape
    taps = tables.shape[0]
    samples = tables.shape[2]
    kernel = functools.partial(dip_kernel, taps=taps, group=group)
    return pl.pallas_call(
        kernel,
        grid=(comps,),
        in_specs=[
            pl.BlockSpec((1, rows), lambda c: (0, 0)),
            pl.BlockSpec((1, rows, EXT), lambda c: (c, 0, 0)),
            pl.BlockSpec((taps, EXT, samples), lambda c: (0, 0, 0)),
        ],
        out_specs=pl.BlockSpec((1, rows, samples), lambda c: (c, 0, 0)),
        out_shape=jax.ShapeDtypeStruct((comps, rows, samples), jnp.bfloat16),
        scratch_shapes=[pltpu.VMEM((rows + 16 * group, LANES), jnp.float32)],
    )(target, ext, tables)


def on_device(records, fan_taps, dip_taps, live_mask, node_place, shot_place):
    _, comps, nodes, samples = records.shape
    taps = fan_taps.shape[1]
    reach = (taps - 1) // 2
    devices = lax.axis_size("shot")
    group = nodes // devices

    block = records[0]
    low, high = time_halo(block, "tm", reach)
    live = jnp.broadcast_to(live_mask[0].astype(jnp.bfloat16)[None, :, None], (comps, nodes, 1))
    ext = extend(block, low, high, live)
    fanned = fan_call(node_place[None, :], ext, toeplitz(fan_taps, samples, reach))

    sent = fanned.reshape(comps, devices, group, samples).transpose(1, 0, 2, 3)
    arrived = lax.all_to_all(sent, "shot", split_axis=0, concat_axis=0, tiled=True)
    lines = arrived.transpose(1, 0, 2, 3)
    low, high = time_halo(lines, "tm", reach)
    ext2 = extend(lines, low, high).reshape(comps, devices * group, EXT)
    target = (jnp.repeat(shot_place, group) * group + jnp.tile(jnp.arange(group, dtype=jnp.int32), devices))[None, :]
    tables = toeplitz(dip_taps[None], samples, reach)[0]
    out = dip_call(target, ext2, tables, group)
    return out.reshape(comps, devices, group, samples).transpose(1, 0, 2, 3)


def solution(mesh):
    return jax.shard_map(
        on_device,
        mesh=mesh,
        in_specs=(P("shot", None, None, "tm"), P(), P(), P("shot", None), P(), P()),
        out_specs=P(None, None, "shot", "tm"),
        check_vma=False,
    )
```

time: 89.2 us -> 81.1 us (0.909)
  other arithmetic: 13.8 us -> 1.25 us
  Pallas kernels: 0 us -> 12.4 us
  local copies, waits for them, and re-layouts: 20.5 us -> 14.6 us
  matrix products: 7.92 us -> 2.59 us
  waiting for transfers between devices: 17.1 us -> 20.1 us
    pallas_call x0 -> x2, Pallas kernels: none -> 12.4 us  [the longest x1 6.42 us: fan_call(): pl.pallas_call(kernel, grid=(comps,), in_specs=[pl.BlockSpec((1, rows), l...]
    reshape x2 -> x3, local copies, waits for them, and re-layouts: 12.5 us -> 4.66 us  [the longest x1 1.83 us: on_device(): return out.reshape(comps, devices, group, samples).transpose(1, 0, 2, 3)]
    sort x2 -> x0, other arithmetic: 6.4 us -> none  [the longest x1 3.87 us: on_device(): node_order = jnp.argsort(node_place)]
    convert_element_type x3 -> x1, other arithmetic: 5.65 us -> 0.02 us  [on_device(): live_mask[0].astype(jnp.bfloat16)[None, :, None]]
    dot_general x4 -> x2, matrix products: 7.92 us -> 2.59 us  [toeplitz(): jnp.einsum('gab,jtb->gajt', tap_set, onehot, preferred_element_type=jnp.f...]
    dot_general x1 -> x2, local copies, waits for them, and re-layouts: 0.45 us -> 5.74 us  [toeplitz(): jnp.einsum('gab,jtb->gajt', tap_set, onehot, preferred_element_type=jnp.f...]
    gather x4 -> x0, local copies, waits for them, and re-layouts: 4.17 us -> none  [the longest x1 1.95 us: on_device(): jnp.take(live_mask, node_order, axis=1).astype(jnp.float32)]
    ppermute x4, waiting for transfers between devices: 1.85 us -> 5.54 us  [the longest x2 3.81 us: time_halo(): lax.ppermute(lax.slice_in_dim(block, 0, width, axis=-1), axis, backward)]
  transfers between devices with their start and end apart: 5 -> 5, of which waited for: 2 -> 3; matrix products, arithmetic and copies ran while one was open for 16% -> 12% of each run, Pallas kernels for 0% -> 0%
where the time goes in v1:
time: 81.1 us; the launch traced here: 80.6 us
  starting transfers between devices  29.4 us (36%)
  waiting for transfers between devices  20.1 us (25%)
  local copies, waits for them, and re-layouts  14.6 us (18%)
  Pallas kernels  12.4 us (15%)
  matrix products  2.59 us (3%)
  other arithmetic  1.25 us (2%)
    all_to_all x1, starting transfers between devices, on_device(): lax.all_to_all(sent, 'shot', split_axis=0, concat_axis=0, tiled=True)  19.6 us
    all_to_all x1, waiting for transfers between devices, on_device(): lax.all_to_all(sent, 'shot', split_axis=0, concat_axis=0, tiled=True)  14.6 us
    ppermute x2, starting transfers between devices, time_halo(): lax.ppermute(lax.slice_in_dim(block, samples - width, None, axis=-1), axi...  7.08 us
    pallas_call x1, Pallas kernels, fan_call(): pl.pallas_call(kernel, grid=(comps,), in_specs=[pl.BlockSpec((1, rows), l...  6.42 us
    pallas_call x1, Pallas kernels, dip_call(): pl.pallas_call(kernel, grid=(comps,), in_specs=[pl.BlockSpec((1, rows), l...  5.96 us
    dot_general x2, local copies, waits for them, and re-layouts, toeplitz(): jnp.einsum('gab,jtb->gajt', tap_set, onehot, preferred_element_type=jnp.f...  5.74 us
    ppermute x2, waiting for transfers between devices, time_halo(): lax.ppermute(lax.slice_in_dim(block, 0, width, axis=-1), axis, backward)  3.81 us
    ppermute x2, starting transfers between devices, time_halo(): lax.ppermute(lax.slice_in_dim(block, 0, width, axis=-1), axis, backward)  2.76 us
  transfers between devices with their start and end apart: 5, of which 3 were waited for; matrix products, arithmetic and copies ran while one was open for 12% of the time, Pallas kernels for 0%

profile of v1, /device:TPU:1, one launch (start us, length us, event | category | flops | bytes accessed | tf_op | source)
XLA Modules:
  0.0 80.6 jit_solution(8517345767392636433)
XLA Ops:
  0.0 0.0 copy-start
  0.0 1.2 %fusion.14 = (bf16[4,256,7]{2,1,0:T(8,128)(2,1)S(1)}, bf16[4,256,7]{2,1,0:T(8,128)(2,1)S(1)}) fusion(bf16[4,256,128]{2,1,0:T(8,128)(2,1)} %bitcast.32), kind=kLoop, calls=%fused_computation.28 | loop fusion | bytes 57344 | tf_op jit(solution)/shard_map/slice | solution.py:20
  1.2 4.0 %collective-permute-start = (bf16[4,256,7]{2,1,0:T(8,128)(2,1)S(1)}, bf16[4,256,7]{2,1,0:T(8,128)(2,1)S(1)}, u32[]{:S(2)}, u32[]{:S(2)}) collective-permute-start(bf16[4,256,7]{2,1,0:T(8,128)(2,1)S(1)} %get-tuple-element.8), channel_id=1, source_target_pairs={{0,1},{1,2},{2,3},{4,5},{5,6},{6,7},{8,9},{9,10},{10,11},{12,13},{... | collective-permute-start | bytes 43016 | tf_op jit(solution)/shard_map/ppermute | solution.py:19
  5.2 1.3 %collective-permute-start.1 = (bf16[4,256,7]{2,1,0:T(8,128)(2,1)S(1)}, bf16[4,256,7]{2,1,0:T(8,128)(2,1)S(1)}, u32[]{:S(2)}, u32[]{:S(2)}) collective-permute-start(bf16[4,256,7]{2,1,0:T(8,128)(2,1)S(1)} %get-tuple-element.7), channel_id=1, source_target_pairs={{1,0},{2,1},{3,2},{5,4},{6,5},{7,6},{9,8},{10,9},{11,10},{13,12},{... | collective-permute-start | bytes 43016 | tf_op jit(solution)/shard_map/ppermute | solution.py:20
  6.5 0.1 subtract_add_fusion
  6.6 0.0 copy-start.2
  6.6 2.0 %fusion.3 = bf16[256,128,4,15]{1,3,2,0:T(8,128)(2,1)S(1)} fusion(s32[256,128]{1,0:T(8,128)S(1)} %subtract_add_fusion, bf16[4,15,15]{2,0,1:T(4,128)(2,1)} %param.7), kind=kOutput, calls=%fused_computation.5 | convolution fusion | flops 59473920 | bytes 4065032 | tf_op jit(solution)/shard_map/gab,jtb->gajt/dot_general | solution.py:44
  8.6 0.0 copy-done.2
  8.6 0.0 copy-start.1
  8.6 4.5 %copy.34 = bf16[256,128,4,15]{1,0,3,2:T(8,128)(2,1)} copy(bf16[256,128,4,15]{1,3,2,0:T(8,128)(2,1)S(1)} %fusion.3) | data formatting | bytes 7864320 | tf_op jit(solution)/shard_map/gab,jtb->gajt/dot_general | solution.py:44
  13.1 0.0 collective-permute-done
  13.1 0.0 collective-permute-done.1
  13.1 0.1 broadcast_in_dim.17
  13.3 0.0 copy-done.1
  13.3 1.3 %concatenate.6.ext_ref = bf16[4,256,256]{2,1,0:T(8,128)(2,1)} concatenate(bf16[4,256,128]{2,1,0:T(8,128)(2,1)S(1)} %bitcast.33, bf16[4,256,7]{2,1,0:T(8,128)(2,1)S(1)} %collective-permute-done, bf16[4,256,7]{2,1,0:T(8,128)(2,1)S(1)} %collective-permute-done.1, bf16[4,256,1]{2,1,0:T(8,128)(2,1)S(1)} %broadcast_in_dim.17, bf16[4,256,113]{2,1,0:T(8,128)(2,1)S(1)} %broadcast_in_dim.18), dimensions={2} | concatenate | bytes 1048576 | tf_op jit(solution)/shard_map/concatenate | solution.py:30
  14.6 0.0 copy-start.3
  14.6 6.4 %shard_map.64 = bf16[4,256,128]{2,1,0:T(8,128)(2,1)} custom-call(s32[1,256]{1,0:T(1,128)} %bitcast.36, bf16[4,256,256]{2,1,0:T(8,128)(2,1)} %concatenate.6.ext_ref, bf16[4,15,256,128]{3,2,1,0:T(8,128)(2,1)} %bitcast.28), custom_call_target="tpu_custom_call" | custom-call | tf_op jit(solution)/shard_map/pallas_call | solution.py:88
  21.0 1.8 %copy.37 = bf16[4,128,2,128]{3,2,0,1:T(2,128)(2,1)} copy(bf16[4,128,2,128]{3,2,1,0:T(2,128)(2,1)} %bitcast.34) | data formatting | bytes 524288 | tf_op jit(solution)/shard_map/reshape | solution.py:134
  22.8 19.6 %all-to-all-start = ((bf16[128,4,2,128]{3,2,1,0:T(2,128)(2,1)}), bf16[128,4,2,128]{3,2,1,0:T(2,128)(2,1)S(1)}, u32[]{:S(2)}, u32[]{:S(2)}) async-start(bf16[128,4,2,128]{3,2,1,0:T(2,128)(2,1)} %bitcast.27), calls=%async_computation | async-start | bytes 524288 | tf_op jit(solution)/shard_map/all_to_all | solution.py:135
  42.4 0.0 copy-done.3
  42.4 0.0 copy-done
  42.4 0.6 fusion.1
  43.0 14.6 %all-to-all-done = bf16[128,4,2,128]{3,2,1,0:T(2,128)(2,1)S(1)} async-done(((bf16[128,4,2,128]{3,2,1,0:T(2,128)(2,1)}), bf16[128,4,2,128]{3,2,1,0:T(2,128)(2,1)S(1)}, u32[]{:S(2)}, u32[]{:S(2)}) %all-to-all-start) | async-done | bytes 262176 | tf_op jit(solution)/shard_map/all_to_all | solution.py:135
  57.6 0.5 fusion.13
  58.1 3.1 %collective-permute-start.2 = (bf16[4,128,2,7]{3,2,0,1:T(2,128)(2,1)S(1)}, bf16[4,128,2,7]{3,2,0,1:T(2,128)(2,1)S(1)}, u32[]{:S(2)}, u32[]{:S(2)}) collective-permute-start(bf16[4,128,2,7]{3,2,0,1:T(2,128)(2,1)S(1)} %get-tuple-element.5), channel_id=1, source_target_pairs={{0,1},{1,2},{2,3},{4,5},{5,6},{6,7},{8,9},{9,10},{10,11},{12,13},{... | collective-permute-start | bytes 43016 | tf_op jit(solution)/shard_map/ppermute | solution.py:19
  61.3 1.5 %collective-permute-start.3 = (bf16[4,128,2,7]{3,2,0,1:T(2,128)(2,1)S(1)}, bf16[4,128,2,7]{3,2,0,1:T(2,128)(2,1)S(1)}, u32[]{:S(2)}, u32[]{:S(2)}) collective-permute-start(bf16[4,128,2,7]{3,2,0,1:T(2,128)(2,1)S(1)} %get-tuple-element.6), channel_id=1, source_target_pairs={{1,0},{2,1},{3,2},{5,4},{6,5},{7,6},{9,8},{10,9},{11,10},{13,12},{... | collective-permute-start | bytes 43016 | tf_op jit(solution)/shard_map/ppermute | solution.py:20
  62.7 0.1 iota_add_fusion
  62.8 1.2 %copy.35 = bf16[256,128,15]{1,0,2:T(8,128)(2,1)} copy(bf16[256,128,15]{1,2,0:T(8,128)(2,1)S(1)} %fusion.1) | data formatting | bytes 1966080 | tf_op jit(solution)/shard_map/gab,jtb->gajt/dot_general | solution.py:44
  64.0 0.7 add.38.target_ref
  64.7 0.1 pad.3.clone
  64.8 1.7 %collective-permute-done.2 = bf16[4,128,2,7]{3,2,0,1:T(2,128)(2,1)S(1)} collective-permute-done((bf16[4,128,2,7]{3,2,0,1:T(2,128)(2,1)S(1)}, bf16[4,128,2,7]{3,2,0,1:T(2,128)(2,1)S(1)}, u32[]{:S(2)}, u32[]{:S(2)}) %collective-permute-start.2) | collective-permute-done | bytes 14368 | tf_op jit(solution)/shard_map/ppermute | solution.py:19
  66.5 3.8 %collective-permute-done.3 = bf16[4,128,2,7]{3,2,0,1:T(2,128)(2,1)S(1)} collective-permute-done((bf16[4,128,2,7]{3,2,0,1:T(2,128)(2,1)S(1)}, bf16[4,128,2,7]{3,2,0,1:T(2,128)(2,1)S(1)}, u32[]{:S(2)}, u32[]{:S(2)}) %collective-permute-start.3) | collective-permute-done | bytes 14368 | tf_op jit(solution)/shard_map/ppermute | solution.py:20
  70.4 1.1 %maximum_maximum_fusion = bf16[4,128,2,256]{3,2,0,1:T(2,128)(2,1)S(1)} fusion(bf16[4,128,2,7]{3,2,0,1:T(2,128)(2,1)S(1)} %collective-permute-done.3, bf16[4,128,2,7]{3,2,0,1:T(2,128)(2,1)S(1)} %collective-permute-done.2, bf16[4,128,2,128]{3,2,0,1:T(2,128)(2,1)S(1)} %bitcast.30, bf16[256]{0:T(256)(128)(2,1)S(1)} %pad.3.clone), kind=kLoop, calls=%fused_computation.10 | loop fusion | flops 2097152 | bytes 815616 | tf_op jit(solution)/shard_map/concatenate | solution.py:30
  71.4 0.4 copy.18
  71.8 1.0 %reshape.84.ext_ref = bf16[4,256,256]{2,1,0:T(8,128)(2,1)} reshape(bf16[4,128,2,256]{3,2,1,0:T(2,128)(2,1)S(1)} %copy.18) | data formatting | bytes 1048576 | tf_op jit(solution)/shard_map/reshape | solution.py:138
  72.8 6.0 %shard_map.65 = bf16[4,256,128]{2,1,0:T(8,128)(2,1)} custom-call(s32[1,256]{1,0:T(1,128)} %add.38.target_ref, bf16[4,256,256]{2,1,0:T(8,128)(2,1)} %reshape.84.ext_ref, bf16[15,256,128]{2,1,0:T(8,128)(2,1)} %bitcast.31), custom_call_target="tpu_custom_call" | custom-call | tf_op jit(solution)/shard_map/pallas_call | solution.py:107
  78.7 1.8 %copy.36 = bf16[4,128,2,128]{3,2,0,1:T(2,128)(2,1)} copy(bf16[4,128,2,128]{3,2,1,0:T(2,128)(2,1)} %bitcast.35) | data formatting | bytes 524288 | tf_op jit(solution)/shard_map/reshape | solution.py:142
  (5 shorter events, 0.1 us)
Async XLA Ops:
  0.0 42.4 %copy-start = (bf16[15,15]{1,0:T(8,128)(2,1)S(1)}, bf16[15,15]{1,0:T(8,128)(2,1)}, u32[]{:S(2)}) copy-start(bf16[15,15]{1,0:T(8,128)(2,1)} %param.8) | copy-start | bytes 1354
  1.2 11.9 %collective-permute-start = (bf16[4,256,7]{2,1,0:T(8,128)(2,1)S(1)}, bf16[4,256,7]{2,1,0:T(8,128)(2,1)S(1)}, u32[]{:S(2)}, u32[]{:S(2)}) collective-permute-start(bf16[4,256,7]{2,1,0:T(8,128)(2,1)S(1)} %get-tuple-element.8), channel_id=1, source_target_pairs={{0,1},{1,2},{2,3},{4,5},{5,6},{6,7},{8,9},{9,10},{10,11},{12,13},{... | collective-permute-start | bytes 43016 | tf_op jit(solution)/shard_map/ppermute | solution.py:19
  5.2 8.0 %collective-permute-start.1 = (bf16[4,256,7]{2,1,0:T(8,128)(2,1)S(1)}, bf16[4,256,7]{2,1,0:T(8,128)(2,1)S(1)}, u32[]{:S(2)}, u32[]{:S(2)}) collective-permute-start(bf16[4,256,7]{2,1,0:T(8,128)(2,1)S(1)} %get-tuple-element.7), channel_id=1, source_target_pairs={{1,0},{2,1},{3,2},{5,4},{6,5},{7,6},{9,8},{10,9},{11,10},{13,12},{... | collective-permute-start | bytes 43016 | tf_op jit(solution)/shard_map/ppermute | solution.py:20
  6.6 2.0 %copy-start.2 = (s32[1,256]{1,0:T(1,128)S(1)}, s32[1,256]{1,0:T(1,128)}, u32[]{:S(2)}) copy-start(s32[1,256]{1,0:T(1,128)} %param.9) | copy-start | bytes 3076
  8.6 4.7 %copy-start.1 = (bf16[1,4,256,128]{3,2,1,0:T(8,128)(2,1)S(1)}, bf16[1,4,256,128]{3,2,1,0:T(8,128)(2,1)}, u32[]{:S(2)}) copy-start(bf16[1,4,256,128]{3,2,1,0:T(8,128)(2,1)} %param.6) | copy-start | bytes 786436
  14.6 27.8 %copy-start.3 = (s32[128]{0:T(128)S(1)}, s32[128]{0:T(128)}, u32[]{:S(2)}) copy-start(s32[128]{0:T(128)} %param.11) | copy-start | bytes 1540
  22.8 34.8 %all-to-all-start = ((bf16[128,4,2,128]{3,2,1,0:T(2,128)(2,1)}), bf16[128,4,2,128]{3,2,1,0:T(2,128)(2,1)S(1)}, u32[]{:S(2)}, u32[]{:S(2)}) async-start(bf16[128,4,2,128]{3,2,1,0:T(2,128)(2,1)} %bitcast.27), calls=%async_computation | async-start | bytes 524288 | tf_op jit(solution)/shard_map/all_to_all | solution.py:135
  58.1 8.4 %collective-permute-start.2 = (bf16[4,128,2,7]{3,2,0,1:T(2,128)(2,1)S(1)}, bf16[4,128,2,7]{3,2,0,1:T(2,128)(2,1)S(1)}, u32[]{:S(2)}, u32[]{:S(2)}) collective-permute-start(bf16[4,128,2,7]{3,2,0,1:T(2,128)(2,1)S(1)} %get-tuple-element.5), channel_id=1, source_target_pairs={{0,1},{1,2},{2,3},{4,5},{5,6},{6,7},{8,9},{9,10},{10,11},{12,13},{... | collective-permute-start | bytes 43016 | tf_op jit(solution)/shard_map/ppermute | solution.py:19
  61.3 9.1 %collective-permute-start.3 = (bf16[4,128,2,7]{3,2,0,1:T(2,128)(2,1)S(1)}, bf16[4,128,2,7]{3,2,0,1:T(2,128)(2,1)S(1)}, u32[]{:S(2)}, u32[]{:S(2)}) collective-permute-start(bf16[4,128,2,7]{3,2,0,1:T(2,128)(2,1)S(1)} %get-tuple-element.6), channel_id=1, source_target_pairs={{1,0},{2,1},{3,2},{5,4},{6,5},{7,6},{9,8},{10,9},{11,10},{13,12},{... | collective-permute-start | bytes 43016 | tf_op jit(solution)/shard_map/ppermute | solution.py:20

commit v2 on v1

v2 whole, which is shorter than its diff:
```python
import functools

import jax
import jax.numpy as jnp
from jax import lax
from jax.experimental import pallas as pl
from jax.experimental.pallas import tpu as pltpu
from jax.sharding import PartitionSpec as P

LANES = 128
EXT = 256


def time_halo(block, axis, width):
    count = lax.axis_size(axis)
    forward = [(i, i + 1) for i in range(count - 1)]
    backward = [(target, source) for source, target in forward]
    samples = block.shape[-1]
    low = lax.ppermute(lax.slice_in_dim(block, samples - width, None, axis=-1), axis, forward)
    high = lax.ppermute(lax.slice_in_dim(block, 0, width, axis=-1), axis, backward)
    return low, high


def extend(block, low, high, extra=None):
    parts = [block, low, high]
    if extra is not None:
        parts.append(extra)
    used = sum(p.shape[-1] for p in parts)
    pad = jnp.zeros(block.shape[:-1] + (EXT - used,), block.dtype)
    return jnp.concatenate(parts + [pad], axis=-1)


def toeplitz(tap_set, samples, width):
    taps = tap_set.shape[-1]
    j = jnp.arange(EXT, dtype=jnp.int32)
    time_of = jnp.where(
        j < samples,
        j,
        jnp.where(j < samples + width, j - samples - width, jnp.where(j < samples + 2 * width, j - width, 1 << 20)),
    )
    t = jnp.arange(samples, dtype=jnp.int32)
    b = time_of[:, None] - t[None, :] + width
    onehot = (b[:, :, None] == jnp.arange(taps, dtype=jnp.int32)[None, None, :]).astype(jnp.bfloat16)
    tables = jnp.einsum("gab,jtb->gajt", tap_set, onehot, preferred_element_type=jnp.float32)
    return tables.astype(jnp.bfloat16)


def fan_tables(fan_taps, samples, reach):
    comps, _, taps = fan_taps.shape
    wide = 2 * reach
    j = jnp.arange(EXT, dtype=jnp.int32)
    time_of = jnp.where(
        j < samples,
        j,
        jnp.where(j < samples + wide, j - samples - wide, jnp.where(j < samples + 2 * wide, j - wide, 1 << 20)),
    )
    col = jnp.arange(EXT, dtype=jnp.int32)
    k = col - samples
    owner = k // wide
    r = k % wide
    halo_t = jnp.where(r < reach, r - reach, samples - reach + r)
    c = jnp.arange(comps, dtype=jnp.int32)[:, None]
    t_of = jnp.where(col[None, :] < samples, col[None, :], jnp.where((owner[None, :] == c) & (k[None, :] < comps * wide), halo_t[None, :], -(1 << 20)))
    b = time_of[None, :, None] - t_of[:, None, :] + reach
    onehot = (b[..., None] == jnp.arange(taps, dtype=jnp.int32)).astype(jnp.bfloat16)
    tables = jnp.einsum("gab,gjtb->gajt", fan_taps, onehot, preferred_element_type=jnp.float32)
    return tables.astype(jnp.bfloat16)


def fan_kernel(place_ref, edge_ref, ext_ref, table_ref, out_ref, scr_ref, halo_ref, *, taps, live_col):
    c = pl.program_id(0)
    rows = ext_ref.shape[1]
    samples = LANES
    place = place_ref[...]
    select = (lax.broadcasted_iota(jnp.int32, (rows, rows), 0) == place).astype(jnp.bfloat16)
    ordered = jnp.dot(select, ext_ref[0], preferred_element_type=jnp.float32)
    keep = ordered[:, live_col:live_col + 1]
    ordered = ordered.astype(jnp.bfloat16)
    scr_ref[0:8, :] = jnp.zeros((8, EXT), jnp.float32)
    scr_ref[rows + 8:rows + 16, :] = jnp.zeros((8, EXT), jnp.float32)
    acc = jnp.zeros((rows, EXT), jnp.float32)
    for a in range(taps):
        part = jnp.dot(ordered, table_ref[0, a], preferred_element_type=jnp.float32)
        scr_ref[8:rows + 8, :] = part
        acc = acc + scr_ref[pl.ds(a + 1, rows), :]
    out_ref[:, pl.ds(pl.multiple_of(c * samples, samples), samples)] = (acc[:, :samples] * keep).astype(out_ref.dtype)

    @pl.when(c == 0)
    def _():
        halo_ref[...] = acc[:, samples:]

    @pl.when(c > 0)
    def _():
        halo_ref[...] += acc[:, samples:]

    @pl.when(c == pl.num_programs(0) - 1)
    def _():
        out_ref[:, pl.ds(pl.num_programs(0) * samples, samples)] = (halo_ref[...] * keep * edge_ref[...]).astype(out_ref.dtype)


def dip_kernel(target_ref, data_ref, table_ref, out_ref, scr_ref, *, taps, group, comps, reach):
    rows = data_ref.shape[0]
    samples = LANES
    pad = group * 8
    target = target_ref[...]
    select = (lax.broadcasted_iota(jnp.int32, (rows, rows), 0) == target).astype(jnp.bfloat16)
    halo = jnp.dot(select, data_ref[:, comps * samples:(comps + 1) * samples], preferred_element_type=jnp.float32)
    scr_ref[0:pad, :] = jnp.zeros((pad, LANES), jnp.float32)
    scr_ref[rows + pad:rows + 2 * pad, :] = jnp.zeros((pad, LANES), jnp.float32)
    for c in range(comps):
        main = jnp.dot(select, data_ref[:, c * samples:(c + 1) * samples], preferred_element_type=jnp.float32)
        mine = halo if c == 0 else pltpu.roll(halo, samples - 2 * reach * c, 1)
        ordered = jnp.concatenate([main, mine], axis=1).astype(jnp.bfloat16)
        acc = jnp.zeros((rows, LANES), jnp.float32)
        for a in range(taps):
            part = jnp.dot(ordered, table_ref[a], preferred_element_type=jnp.float32)
            scr_ref[pad:rows + pad, :] = part
            acc = acc + scr_ref[pl.ds(pad + group * (a - reach), rows), :]
        out_ref[c] = acc.astype(out_ref.dtype)


def fan_call(place, edge, ext, tables):
    comps, rows, _ = ext.shape
    taps = tables.shape[1]
    kernel = functools.partial(fan_kernel, taps=taps, live_col=LANES + 2 * (taps - 1))
    return pl.pallas_call(
        kernel,
        grid=(comps,),
        in_specs=[
            pl.BlockSpec((1, rows), lambda c: (0, 0)),
            pl.BlockSpec((1, LANES), lambda c: (0, 0)),
            pl.BlockSpec((1, rows, EXT), lambda c: (c, 0, 0)),
            pl.BlockSpec((1, taps, EXT, EXT), lambda c: (c, 0, 0, 0)),
        ],
        out_specs=pl.BlockSpec((rows, (comps + 1) * LANES), lambda c: (0, 0)),
        out_shape=jax.ShapeDtypeStruct((rows, (comps + 1) * LANES), jnp.bfloat16),
        scratch_shapes=[pltpu.VMEM((rows + 16, EXT), jnp.float32), pltpu.VMEM((rows, LANES), jnp.float32)],
    )(place, edge, ext, tables)


def dip_call(target, data, tables, group, comps, reach):
    rows = data.shape[0]
    taps = tables.shape[0]
    kernel = functools.partial(dip_kernel, taps=taps, group=group, comps=comps, reach=reach)
    return pl.pallas_call(
        kernel,
        out_shape=jax.ShapeDtypeStruct((comps, rows, LANES), jnp.bfloat16),
        scratch_shapes=[pltpu.VMEM((rows + 16 * group, LANES), jnp.float32)],
    )(target, data, tables)


def on_device(records, fan_taps, dip_taps, live_mask, node_place, shot_place):
    _, comps, nodes, samples = records.shape
    taps = fan_taps.shape[1]
    reach = (taps - 1) // 2
    devices = lax.axis_size("shot")
    group = nodes // devices

    block = records[0]
    low, high = time_halo(block, "tm", 2 * reach)
    live = jnp.broadcast_to(live_mask[0].astype(jnp.bfloat16)[None, :, None], (comps, nodes, 1))
    ext = extend(block, low, high, live)
    place = lax.axis_index("tm")
    lane = jnp.arange(LANES, dtype=jnp.int32) % (2 * reach)
    edge = jnp.where(lane < reach, place > 0, place < lax.axis_size("tm") - 1).astype(jnp.float32)[None, :]
    packed = fan_call(node_place[None, :], edge, ext, fan_tables(fan_taps, samples, reach))

    sent = packed.reshape(devices, group, packed.shape[-1])
    arrived = lax.all_to_all(sent, "shot", split_axis=0, concat_axis=0, tiled=True)
    data = arrived.reshape(devices * group, packed.shape[-1])
    target = (jnp.repeat(shot_place, group) * group + jnp.tile(jnp.arange(group, dtype=jnp.int32), devices))[None, :]
    tables = toeplitz(dip_taps[None], samples, reach)[0]
    out = dip_call(target, data, tables, group, comps, reach)
    return out.reshape(comps, devices, group, samples).transpose(1, 0, 2, 3)


def solution(mesh):
    return jax.shard_map(
        on_device,
        mesh=mesh,
        in_specs=(P("shot", None, None, "tm"), P(), P(), P("shot", None), P(), P()),
        out_specs=P(None, None, "shot", "tm"),
        check_vma=False,
    )
```

time: 81.1 us -> 77.3 us (0.953)
  starting transfers between devices: 29.4 us -> 23.1 us
  waiting for transfers between devices: 20.1 us -> 13.9 us
  matrix products: 2.59 us -> 6.96 us
  local copies, waits for them, and re-layouts: 14.6 us -> 18.7 us
    dot_general x0 -> x1, local copies, waits for them, and re-layouts: none -> 9.62 us  [fan_tables(): jnp.einsum('gab,gjtb->gajt', fan_taps, onehot, preferred_element_type=jnp...]
    dot_general x0 -> x1, matrix products: none -> 6.33 us  [fan_tables(): jnp.einsum('gab,gjtb->gajt', fan_taps, onehot, preferred_element_type=jnp...]
    dot_general x2 -> x1, local copies, waits for them, and re-layouts: 5.74 us -> 1.21 us  [toeplitz(): jnp.einsum('gab,jtb->gajt', tap_set, onehot, preferred_element_type=jnp.f...]
    ppermute x2 -> x1, waiting for transfers between devices: 3.81 us -> 0.01 us  [time_halo(): lax.ppermute(lax.slice_in_dim(block, 0, width, axis=-1), axis, backward)]
    ppermute x2 -> x1, starting transfers between devices: 7.08 us -> 3.96 us  [time_halo(): lax.ppermute(lax.slice_in_dim(block, samples - width, None, axis=-1), axi...]
    dot_general x2 -> x1, matrix products: 2.59 us -> 0.63 us  [toeplitz(): jnp.einsum('gab,jtb->gajt', tap_set, onehot, preferred_element_type=jnp.f...]
    ppermute x2 -> x1, waiting for transfers between devices: 1.72 us -> 0.01 us  [time_halo(): lax.ppermute(lax.slice_in_dim(block, samples - width, None, axis=-1), axi...]
    all_to_all x1, starting transfers between devices: 19.6 us -> 17.9 us  [on_device(): lax.all_to_all(sent, 'shot', split_axis=0, concat_axis=0, tiled=True)]
  transfers between devices with their start and end apart: 5 -> 3, of which waited for: 3 -> 1; matrix products, arithmetic and copies ran while one was open for 12% -> 26% of each run, Pallas kernels for 0% -> 0%
where the time goes in v2:
time: 77.3 us; the launch traced here: 76.6 us
  starting transfers between devices  23.1 us (30%)
  local copies, waits for them, and re-layouts  18.7 us (24%)
  waiting for transfers between devices  13.9 us (18%)
  Pallas kernels  12.2 us (16%)
  matrix products  6.96 us (9%)
  other arithmetic  1.58 us (2%)
    all_to_all x1, starting transfers between devices, on_device(): lax.all_to_all(sent, 'shot', split_axis=0, concat_axis=0, tiled=True)  17.9 us
    all_to_all x1, waiting for transfers between devices, on_device(): lax.all_to_all(sent, 'shot', split_axis=0, concat_axis=0, tiled=True)  13.9 us
    dot_general x1, local copies, waits for them, and re-layouts, fan_tables(): jnp.einsum('gab,gjtb->gajt', fan_taps, onehot, preferred_element_type=jnp...  9.62 us
    pallas_call x1, Pallas kernels, fan_call(): pl.pallas_call(kernel, grid=(comps,), in_specs=[pl.BlockSpec((1, rows), l...  6.78 us
    dot_general x1, matrix products, fan_tables(): jnp.einsum('gab,gjtb->gajt', fan_taps, onehot, preferred_element_type=jnp...  6.33 us
    pallas_call x1, Pallas kernels, dip_call(): pl.pallas_call(kernel, out_shape=jax.ShapeDtypeStruct((comps, rows, LANES...  5.46 us
    ppermute x1, starting transfers between devices, time_halo(): lax.ppermute(lax.slice_in_dim(block, samples - width, None, axis=-1), axi...  3.96 us
    reshape x1, local copies, waits for them, and re-layouts, on_device(): return out.reshape(comps, devices, group, samples).transpose(1, 0, 2, 3)  1.83 us
  transfers between devices with their start and end apart: 3, of which 1 were waited for; matrix products, arithmetic and copies ran while one was open for 26% of the time, Pallas kernels for 0%

profile of v2, /device:TPU:1, one launch (start us, length us, event | category | flops | bytes accessed | tf_op | source)
XLA Modules:
  0.0 76.6 jit_solution(2833296472388543130)
XLA Ops:
  0.0 0.0 copy-start
  0.0 1.2 %fusion.16 = (bf16[4,256,14]{2,1,0:T(8,128)(2,1)S(1)}, bf16[4,256,14]{2,1,0:T(8,128)(2,1)S(1)}) fusion(bf16[4,256,128]{2,1,0:T(8,128)(2,1)} %bitcast.19), kind=kLoop, calls=%fused_computation.43 | loop fusion | bytes 114688 | tf_op jit(solution)/shard_map/slice | solution.py:20
  1.2 4.0 %collective-permute-start = (bf16[4,256,14]{2,1,0:T(8,128)(2,1)S(1)}, bf16[4,256,14]{2,1,0:T(8,128)(2,1)S(1)}, u32[]{:S(2)}, u32[]{:S(2)}) collective-permute-start(bf16[4,256,14]{2,1,0:T(8,128)(2,1)S(1)} %get-tuple-element.6), channel_id=1, source_target_pairs={{0,1},{1,2},{2,3},{4,5},{5,6},{6,7},{8,9},{9,10},{10,11},{12,13},{... | collective-permute-start | bytes 86024 | tf_op jit(solution)/shard_map/ppermute | solution.py:19
  5.2 1.3 %collective-permute-start.1 = (bf16[4,256,14]{2,1,0:T(8,128)(2,1)S(1)}, bf16[4,256,14]{2,1,0:T(8,128)(2,1)S(1)}, u32[]{:S(2)}, u32[]{:S(2)}) collective-permute-start(bf16[4,256,14]{2,1,0:T(8,128)(2,1)S(1)} %get-tuple-element.5), channel_id=1, source_target_pairs={{1,0},{2,1},{3,2},{5,4},{6,5},{7,6},{9,8},{10,9},{11,10},{13,12},{... | collective-permute-start | bytes 86024 | tf_op jit(solution)/shard_map/ppermute | solution.py:20
  6.5 0.7 convert_reduce_fusion
  7.2 0.1 subtract_add_fusion.1
  7.3 0.1 subtract_add_fusion
  7.5 0.0 copy-done
  7.5 6.3 %fusion = bf16[4,256,256,15]{2,3,1,0:T(8,128)(2,1)} fusion(s32[4,256,256]{2,1,0:T(8,128)S(1)} %subtract_add_fusion, bf16[4,15,15,1]{2,0,1,3:T(4,128)(2,1)S(1)} %bitcast.16), kind=kOutput, calls=%fused_computation.1 | convolution fusion | flops 121896960 | bytes 8914696 | tf_op jit(solution)/shard_map/gab,gjtb->gajt/dot_general | solution.py:66
  13.8 0.5 select_convert_fusion.edge_ref
  14.3 0.0 copy-start.1
  14.3 9.6 %copy.27 = bf16[4,256,256,15]{2,1,3,0:T(8,128)(2,1)} copy(bf16[4,256,256,15]{2,3,1,0:T(8,128)(2,1)} %fusion) | data formatting | bytes 15728640 | tf_op jit(solution)/shard_map/gab,gjtb->gajt/dot_general | solution.py:66
  24.0 0.0 copy-start.2
  24.0 0.0 copy-start.3
  24.0 0.0 collective-permute-done
  24.0 0.0 collective-permute-done.1
  24.0 0.1 broadcast_in_dim.77
  24.1 0.0 copy-done.1
  24.2 1.3 %concatenate.3.ext_ref = bf16[4,256,256]{2,1,0:T(8,128)(2,1)} concatenate(bf16[4,256,128]{2,1,0:T(8,128)(2,1)S(1)} %bitcast.20, bf16[4,256,14]{2,1,0:T(8,128)(2,1)S(1)} %collective-permute-done, bf16[4,256,14]{2,1,0:T(8,128)(2,1)S(1)} %collective-permute-done.1, bf16[4,256,1]{2,1,0:T(8,128)(2,1)S(1)} %broadcast_in_dim.77, bf16[4,256,99]{2,1,0:T(8,128)(2,1)S(1)} %broadcast_in_dim.78), dimensions={2} | concatenate | bytes 1048576 | tf_op jit(solution)/shard_map/concatenate | solution.py:30
  25.4 6.8 %shard_map.64 = bf16[256,640]{1,0:T(8,128)(2,1)} custom-call(s32[1,256]{1,0:T(1,128)} %bitcast.22, f32[1,128]{1,0:T(1,128)} %select_convert_fusion.edge_ref, bf16[4,256,256]{2,1,0:T(8,128)(2,1)} %concatenate.3.ext_ref, bf16[4,15,256,256]{3,2,1,0:T(8,128)(2,1)} %bitcast.17), custom_call_target="tpu_custom_call" | custom-call | tf_op jit(solution)/shard_map/pallas_call | solution.py:126
  32.2 1.8 %reshape.223 = bf16[128,2,640]{2,1,0:T(2,128)(2,1)} reshape(bf16[256,640]{1,0:T(8,128)(2,1)} %shard_map.64) | data formatting | bytes 655360 | tf_op jit(solution)/shard_map/reshape | solution.py:168
  34.0 17.9 %all-to-all-start = ((bf16[128,2,640]{2,1,0:T(2,128)(2,1)}), bf16[128,2,640]{2,1,0:T(2,128)(2,1)S(1)}, u32[]{:S(2)}, u32[]{:S(2)}) async-start(bf16[128,2,640]{2,1,0:T(2,128)(2,1)} %reshape.223), calls=%async_computation | async-start | bytes 655360 | tf_op jit(solution)/shard_map/all_to_all | solution.py:169
  51.9 0.0 copy-done.2
  51.9 0.6 fusion.3
  52.6 1.2 %copy.28 = bf16[256,128,15]{1,0,2:T(8,128)(2,1)} copy(bf16[256,128,15]{1,2,0:T(8,128)(2,1)S(1)} %fusion.3) | data formatting | bytes 1966080 | tf_op jit(solution)/shard_map/gab,jtb->gajt/dot_general | solution.py:44
  53.8 0.0 copy-done.3
  53.8 0.1 iota_add_fusion
  53.9 0.7 add.114.target_ref
  54.6 13.9 %all-to-all-done = bf16[128,2,640]{2,1,0:T(2,128)(2,1)S(1)} async-done(((bf16[128,2,640]{2,1,0:T(2,128)(2,1)}), bf16[128,2,640]{2,1,0:T(2,128)(2,1)S(1)}, u32[]{:S(2)}, u32[]{:S(2)}) %all-to-all-start) | async-done | bytes 327712 | tf_op jit(solution)/shard_map/all_to_all | solution.py:169
  68.5 0.9 %reshape.224.data_ref = bf16[256,640]{1,0:T(8,128)(2,1)} reshape(bf16[128,2,640]{2,1,0:T(2,128)(2,1)S(1)} %all-to-all-done) | data formatting | bytes 655360 | tf_op jit(solution)/shard_map/reshape | solution.py:170
  69.3 5.5 %shard_map.65 = bf16[4,256,128]{2,1,0:T(8,128)(2,1)} custom-call(s32[1,256]{1,0:T(1,128)} %add.114.target_ref, bf16[256,640]{1,0:T(8,128)(2,1)} %reshape.224.data_ref, bf16[15,256,128]{2,1,0:T(8,128)(2,1)} %bitcast.18), custom_call_target="tpu_custom_call" | custom-call | tf_op jit(solution)/shard_map/pallas_call | solution.py:145
  74.8 1.8 %copy.29 = bf16[4,128,2,128]{3,2,0,1:T(2,128)(2,1)} copy(bf16[4,128,2,128]{3,2,1,0:T(2,128)(2,1)} %bitcast.21) | data formatting | bytes 524288 | tf_op jit(solution)/shard_map/reshape | solution.py:174
  (7 shorter events, 0.1 us)
Async XLA Ops:
  0.0 7.5 %copy-start = (bf16[4,15,15]{2,0,1:T(4,128)(2,1)S(1)}, bf16[4,15,15]{2,0,1:T(4,128)(2,1)}, u32[]{:S(2)}) copy-start(bf16[4,15,15]{2,0,1:T(4,128)(2,1)} %param.7) | copy-start | bytes 5404
  1.2 22.8 %collective-permute-start = (bf16[4,256,14]{2,1,0:T(8,128)(2,1)S(1)}, bf16[4,256,14]{2,1,0:T(8,128)(2,1)S(1)}, u32[]{:S(2)}, u32[]{:S(2)}) collective-permute-start(bf16[4,256,14]{2,1,0:T(8,128)(2,1)S(1)} %get-tuple-element.6), channel_id=1, source_target_pairs={{0,1},{1,2},{2,3},{4,5},{5,6},{6,7},{8,9},{9,10},{10,11},{12,13},{... | collective-permute-start | bytes 86024 | tf_op jit(solution)/shard_map/ppermute | solution.py:19
  5.2 18.8 %collective-permute-start.1 = (bf16[4,256,14]{2,1,0:T(8,128)(2,1)S(1)}, bf16[4,256,14]{2,1,0:T(8,128)(2,1)S(1)}, u32[]{:S(2)}, u32[]{:S(2)}) collective-permute-start(bf16[4,256,14]{2,1,0:T(8,128)(2,1)S(1)} %get-tuple-element.5), channel_id=1, source_target_pairs={{1,0},{2,1},{3,2},{5,4},{6,5},{7,6},{9,8},{10,9},{11,10},{13,12},{... | collective-permute-start | bytes 86024 | tf_op jit(solution)/shard_map/ppermute | solution.py:20
  14.3 9.8 %copy-start.1 = (bf16[1,4,256,128]{3,2,1,0:T(8,128)(2,1)S(1)}, bf16[1,4,256,128]{3,2,1,0:T(8,128)(2,1)}, u32[]{:S(2)}) copy-start(bf16[1,4,256,128]{3,2,1,0:T(8,128)(2,1)} %param.6) | copy-start | bytes 786436
  24.0 27.9 %copy-start.2 = (bf16[15,15]{1,0:T(8,128)(2,1)S(1)}, bf16[15,15]{1,0:T(8,128)(2,1)}, u32[]{:S(2)}) copy-start(bf16[15,15]{1,0:T(8,128)(2,1)} %param.8) | copy-start | bytes 1354
  24.0 29.8 %copy-start.3 = (s32[128]{0:T(128)S(1)}, s32[128]{0:T(128)}, u32[]{:S(2)}) copy-start(s32[128]{0:T(128)} %param.11) | copy-start | bytes 1540
  34.0 34.5 %all-to-all-start = ((bf16[128,2,640]{2,1,0:T(2,128)(2,1)}), bf16[128,2,640]{2,1,0:T(2,128)(2,1)S(1)}, u32[]{:S(2)}, u32[]{:S(2)}) async-start(bf16[128,2,640]{2,1,0:T(2,128)(2,1)} %reshape.223), calls=%async_computation | async-start | bytes 655360 | tf_op jit(solution)/shard_map/all_to_all | solution.py:169

commit v3 on v2

v3 whole, which is shorter than its diff:
```python
import functools

import jax
import jax.numpy as jnp
from jax import lax
from jax.experimental import pallas as pl
from jax.experimental.pallas import tpu as pltpu
from jax.sharding import PartitionSpec as P

LANES = 128
EXT = 256


def time_halo(block, axis, width):
    count = lax.axis_size(axis)
    forward = [(i, i + 1) for i in range(count - 1)]
    backward = [(target, source) for source, target in forward]
    samples = block.shape[-1]
    low = lax.ppermute(lax.slice_in_dim(block, samples - width, None, axis=-1), axis, forward)
    high = lax.ppermute(lax.slice_in_dim(block, 0, width, axis=-1), axis, backward)
    return low, high


def circulant(tap_set, samples):
    taps = tap_set.shape[-1]
    reach = (taps - 1) // 2
    j = jnp.arange(EXT, dtype=jnp.int32)
    t = jnp.arange(samples, dtype=jnp.int32)
    b = (j[:, None] - t[None, :] + reach) % EXT
    onehot = (b[:, :, None] == jnp.arange(taps, dtype=jnp.int32)[None, None, :]).astype(jnp.bfloat16)
    tables = jnp.einsum("gab,jtb->gajt", tap_set, onehot, preferred_element_type=jnp.float32)
    return tables.astype(jnp.bfloat16)


def fan_kernel(place_ref, edge_ref, ext_ref, table_ref, out_ref, scr_ref, halo_ref, *, taps, live_col, comps):
    c = pl.program_id(0)
    rows = ext_ref.shape[1]
    samples = LANES
    reach = (taps - 1) // 2
    place = place_ref[...]
    select = (lax.broadcasted_iota(jnp.int32, (rows, rows), 0) == place).astype(jnp.bfloat16)
    ordered = jnp.dot(select, ext_ref[0], preferred_element_type=jnp.float32)
    keep = ordered[:, live_col:live_col + 1]
    ordered = ordered.astype(jnp.bfloat16)
    swapped = jnp.concatenate([ordered[:, samples:], ordered[:, :samples]], axis=1)
    second = rows + 16
    zeros = jnp.zeros((8, LANES), jnp.float32)
    scr_ref[0:8, :] = zeros
    scr_ref[rows + 8:rows + 16, :] = zeros
    scr_ref[second + rows:second + rows + 8, :] = zeros
    acc = jnp.zeros((rows, LANES), jnp.float32)
    acc_h = jnp.zeros((rows, LANES), jnp.float32)
    for a in range(taps):
        table = table_ref[0, a]
        scr_ref[8:rows + 8, :] = jnp.dot(ordered, table, preferred_element_type=jnp.float32)
        scr_ref[second:second + rows, :] = jnp.dot(swapped, table, preferred_element_type=jnp.float32)
        acc = acc + scr_ref[pl.ds(a + 8 - reach, rows), :]
        acc_h = acc_h + scr_ref[pl.ds(second + a - reach, rows), :]
    out_ref[:, pl.ds(pl.multiple_of(c * samples, samples), samples)] = (acc * keep).astype(out_ref.dtype)
    lane = lax.broadcasted_iota(jnp.int32, (rows, LANES), 1)
    for k in range(comps):
        @pl.when(c == k)
        def _():
            moved = pltpu.roll(acc_h, reach + 2 * reach * k, 1)
            mine = jnp.where((lane >= 2 * reach * k) & (lane < 2 * reach * (k + 1)), moved, 0.0)
            if k == 0:
                halo_ref[...] = mine
            else:
                halo_ref[...] += mine

    @pl.when(c == comps - 1)
    def _():
        out_ref[:, comps * samples:(comps + 1) * samples] = (halo_ref[...] * keep * edge_ref[...]).astype(out_ref.dtype)


def dip_kernel(target_ref, data_ref, table_ref, out_ref, scr_ref, *, taps, group, comps):
    rows = data_ref.shape[0]
    samples = LANES
    reach = (taps - 1) // 2
    pad = group * 8
    target = target_ref[...]
    select = (lax.broadcasted_iota(jnp.int32, (rows, rows), 0) == target).astype(jnp.bfloat16)
    halo = jnp.dot(select, data_ref[:, comps * samples:(comps + 1) * samples], preferred_element_type=jnp.float32)
    scr_ref[0:pad, :] = jnp.zeros((pad, LANES), jnp.float32)
    scr_ref[rows + pad:rows + 2 * pad, :] = jnp.zeros((pad, LANES), jnp.float32)
    for c in range(comps):
        main = jnp.dot(select, data_ref[:, c * samples:(c + 1) * samples], preferred_element_type=jnp.float32)
        mine = pltpu.roll(halo, (samples - reach - 2 * reach * c) % samples, 1)
        ordered = jnp.concatenate([main, mine], axis=1).astype(jnp.bfloat16)
        acc = jnp.zeros((rows, LANES), jnp.float32)
        for a in range(taps):
            part = jnp.dot(ordered, table_ref[0, a], preferred_element_type=jnp.float32)
            scr_ref[pad:rows + pad, :] = part
            acc = acc + scr_ref[pl.ds(pad + group * (a - reach), rows), :]
        out_ref[c] = acc.astype(out_ref.dtype)


def fan_call(place, edge, ext, tables, live_col):
    comps, rows, _ = ext.shape
    taps = tables.shape[1]
    kernel = functools.partial(fan_kernel, taps=taps, live_col=live_col, comps=comps)
    return pl.pallas_call(
        kernel,
        grid=(comps,),
        in_specs=[
            pl.BlockSpec((1, rows), lambda c: (0, 0)),
            pl.BlockSpec((1, LANES), lambda c: (0, 0)),
            pl.BlockSpec((1, rows, EXT), lambda c: (c, 0, 0)),
            pl.BlockSpec((1, taps, EXT, LANES), lambda c: (c, 0, 0, 0)),
        ],
        out_specs=pl.BlockSpec((rows, (comps + 1) * LANES), lambda c: (0, 0)),
        out_shape=jax.ShapeDtypeStruct((rows, (comps + 1) * LANES), jnp.bfloat16),
        scratch_shapes=[pltpu.VMEM((2 * rows + 24, LANES), jnp.float32), pltpu.VMEM((rows, LANES), jnp.float32)],
    )(place, edge, ext, tables)


def dip_call(target, data, tables, group, comps):
    rows = data.shape[0]
    taps = tables.shape[1]
    kernel = functools.partial(dip_kernel, taps=taps, group=group, comps=comps)
    return pl.pallas_call(
        kernel,
        out_shape=jax.ShapeDtypeStruct((comps, rows, LANES), jnp.bfloat16),
        scratch_shapes=[pltpu.VMEM((rows + 16 * group, LANES), jnp.float32)],
    )(target, data, tables)


def on_device(records, fan_taps, dip_taps, live_mask, node_place, shot_place):
    _, comps, nodes, samples = records.shape
    taps = fan_taps.shape[1]
    reach = (taps - 1) // 2
    wide = 2 * reach
    devices = lax.axis_size("shot")
    group = nodes // devices

    block = records[0]
    low, high = time_halo(block, "tm", wide)
    live_col = samples + 32
    live = jnp.broadcast_to(live_mask[0].astype(jnp.bfloat16)[None, :, None], (comps, nodes, 1))
    gap1 = jnp.zeros((comps, nodes, live_col - samples - wide), jnp.bfloat16)
    gap2 = jnp.zeros((comps, nodes, EXT - wide - live_col - 1), jnp.bfloat16)
    ext = jnp.concatenate([block, high, gap1, live, gap2, low], axis=-1)
    place = lax.axis_index("tm")
    lane = jnp.arange(LANES, dtype=jnp.int32) % wide
    edge = jnp.where(lane < reach, place > 0, place < lax.axis_size("tm") - 1).astype(jnp.float32)[None, :]
    packed = fan_call(node_place[None, :], edge, ext, circulant(fan_taps, samples), live_col)

    sent = packed.reshape(devices, group, packed.shape[-1])
    arrived = lax.all_to_all(sent, "shot", split_axis=0, concat_axis=0, tiled=True)
    data = arrived.reshape(devices * group, packed.shape[-1])
    target = (jnp.repeat(shot_place, group) * group + jnp.tile(jnp.arange(group, dtype=jnp.int32), devices))[None, :]
    out = dip_call(target, data, circulant(dip_taps[None], samples), group, comps)
    return out.reshape(comps, devices, group, samples).transpose(1, 0, 2, 3)


def solution(mesh):
    return jax.shard_map(
        on_device,
        mesh=mesh,
        in_specs=(P("shot", None, None, "tm"), P(), P(), P("shot", None), P(), P()),
        out_specs=P(None, None, "shot", "tm"),
        check_vma=False,
    )
```

time: 77.3 us -> 70.3 us (0.909)
  local copies, waits for them, and re-layouts: 18.7 us -> 13.6 us
  matrix products: 6.96 us -> 2.58 us
  Pallas kernels: 12.2 us -> 13.8 us
  starting transfers between devices: 23.1 us -> 24.4 us
    dot_general x2, local copies, waits for them, and re-layouts: 10.8 us -> 5.75 us  [circulant(): jnp.einsum('gab,jtb->gajt', tap_set, onehot, preferred_element_type=jnp.f...]
    dot_general x2, matrix products: 6.96 us -> 2.58 us  [circulant(): jnp.einsum('gab,jtb->gajt', tap_set, onehot, preferred_element_type=jnp.f...]
    pallas_call x1, Pallas kernels: 6.78 us -> 8.34 us  [fan_call(): pl.pallas_call(kernel, grid=(comps,), in_specs=[pl.BlockSpec((1, rows), l...]
  transfers between devices with their start and end apart: 3 -> 3, of which waited for: 1 -> 1; matrix products, arithmetic and copies ran while one was open for 26% -> 15% of each run, Pallas kernels for 0% -> 0%
where the time goes in v3:
time: 70.3 us; the launch traced here: 69.9 us
  starting transfers between devices  24.4 us (35%)
  waiting for transfers between devices  13.9 us (20%)
  Pallas kernels  13.8 us (20%)
  local copies, waits for them, and re-layouts  13.6 us (19%)
  matrix products  2.58 us (4%)
  other arithmetic  1.37 us (2%)
    all_to_all x1, starting transfers between devices, on_device(): lax.all_to_all(sent, 'shot', split_axis=0, concat_axis=0, tiled=True)  18.5 us
    all_to_all x1, waiting for transfers between devices, on_device(): lax.all_to_all(sent, 'shot', split_axis=0, concat_axis=0, tiled=True)  13.9 us
    pallas_call x1, Pallas kernels, fan_call(): pl.pallas_call(kernel, grid=(comps,), in_specs=[pl.BlockSpec((1, rows), l...  8.34 us
    dot_general x2, local copies, waits for them, and re-layouts, circulant(): jnp.einsum('gab,jtb->gajt', tap_set, onehot, preferred_element_type=jnp.f...  5.75 us
    pallas_call x1, Pallas kernels, dip_call(): pl.pallas_call(kernel, out_shape=jax.ShapeDtypeStruct((comps, rows, LANES...  5.49 us
    ppermute x1, starting transfers between devices, time_halo(): lax.ppermute(lax.slice_in_dim(block, samples - width, None, axis=-1), axi...  4.59 us
    dot_general x2, matrix products, circulant(): jnp.einsum('gab,jtb->gajt', tap_set, onehot, preferred_element_type=jnp.f...  2.58 us
    reshape x1, local copies, waits for them, and re-layouts, on_device(): return out.reshape(comps, devices, group, samples).transpose(1, 0, 2, 3)  1.83 us
  transfers between devices with their start and end apart: 3, of which 1 were waited for; matrix products, arithmetic and copies ran while one was open for 15% of the time, Pallas kernels for 0%

profile of v3, /device:TPU:1, one launch (start us, length us, event | category | flops | bytes accessed | tf_op | source)
XLA Modules:
  0.0 69.9 jit_solution(3468322855650816788)
XLA Ops:
  0.0 0.0 copy-start
  0.0 1.2 %fusion.12 = (bf16[4,256,14]{2,1,0:T(8,128)(2,1)S(1)}, bf16[4,256,14]{2,1,0:T(8,128)(2,1)S(1)}) fusion(bf16[4,256,128]{2,1,0:T(8,128)(2,1)} %bitcast.27), kind=kLoop, calls=%fused_computation.23 | loop fusion | bytes 114688 | tf_op jit(solution)/shard_map/slice | solution.py:19
  1.2 1.3 %collective-permute-start = (bf16[4,256,14]{2,1,0:T(8,128)(2,1)S(1)}, bf16[4,256,14]{2,1,0:T(8,128)(2,1)S(1)}, u32[]{:S(2)}, u32[]{:S(2)}) collective-permute-start(bf16[4,256,14]{2,1,0:T(8,128)(2,1)S(1)} %get-tuple-element.6), channel_id=1, source_target_pairs={{1,0},{2,1},{3,2},{5,4},{6,5},{7,6},{9,8},{10,9},{11,10},{13,12},{... | collective-permute-start | bytes 86024 | tf_op jit(solution)/shard_map/ppermute | solution.py:20
  2.5 4.6 %collective-permute-start.1 = (bf16[4,256,14]{2,1,0:T(8,128)(2,1)S(1)}, bf16[4,256,14]{2,1,0:T(8,128)(2,1)S(1)}, u32[]{:S(2)}, u32[]{:S(2)}) collective-permute-start(bf16[4,256,14]{2,1,0:T(8,128)(2,1)S(1)} %get-tuple-element.5), channel_id=1, source_target_pairs={{0,1},{1,2},{2,3},{4,5},{5,6},{6,7},{8,9},{9,10},{10,11},{12,13},{... | collective-permute-start | bytes 86024 | tf_op jit(solution)/shard_map/ppermute | solution.py:19
  7.1 0.1 add_select_fusion
  7.1 0.7 %convert_reduce_fusion = bf16[256]{0:T(256)(128)(2,1)S(1)} fusion(s32[1,256]{1,0:T(1,128)} %param.9), kind=kLoop, calls=%fused_computation.21 | loop fusion | flops 256 | bytes 1536 | tf_op jit(solution)/shard_map/convert_element_type | solution.py:139
  7.8 2.0 %fusion.3 = bf16[256,128,4,15]{1,3,2,0:T(8,128)(2,1)S(1)} fusion(s32[256,128]{1,0:T(8,128)S(1)} %add_select_fusion, bf16[4,15,15]{2,0,1:T(4,128)(2,1)} %param.7), kind=kOutput, calls=%fused_computation.5 | convolution fusion | flops 59473920 | bytes 4065032 | tf_op jit(solution)/shard_map/gab,jtb->gajt/dot_general | solution.py:31
  9.8 0.5 select_convert_fusion.edge_ref
  10.3 0.0 copy-start.1
  10.3 4.5 %copy.27 = bf16[256,128,4,15]{1,0,3,2:T(8,128)(2,1)} copy(bf16[256,128,4,15]{1,3,2,0:T(8,128)(2,1)S(1)} %fusion.3) | data formatting | bytes 7864320 | tf_op jit(solution)/shard_map/gab,jtb->gajt/dot_general | solution.py:31
  14.9 0.0 collective-permute-done
  14.9 0.0 collective-permute-done.1
  14.9 0.1 broadcast_in_dim.42
  15.1 0.0 copy-done.1
  15.1 1.3 %concatenate.3.ext_ref = bf16[4,256,256]{2,1,0:T(8,128)(2,1)} concatenate(bf16[4,256,128]{2,1,0:T(8,128)(2,1)S(1)} %bitcast.28, bf16[4,256,14]{2,1,0:T(8,128)(2,1)S(1)} %collective-permute-done, bf16[4,256,18]{2,1,0:T(8,128)(2,1)S(1)} %broadcast_in_dim.22, bf16[4,256,1]{2,1,0:T(8,128)(2,1)S(1)} %broadcast_in_dim.42, bf16[4,256,81]{2,1,0:T(8,128)(2,1)S(1)} %broadcast_in_dim.43, ...), dimensions={2} | concatenate | bytes 1048576 | tf_op jit(solution)/shard_map/concatenate | solution.py:142
  16.4 8.3 %shard_map.64 = bf16[256,640]{1,0:T(8,128)(2,1)} custom-call(s32[1,256]{1,0:T(1,128)} %bitcast.30, f32[1,128]{1,0:T(1,128)} %select_convert_fusion.edge_ref, bf16[4,256,256]{2,1,0:T(8,128)(2,1)} %concatenate.3.ext_ref, bf16[4,15,256,128]{3,2,1,0:T(8,128)(2,1)} %bitcast.25), custom_call_target="tpu_custom_call" | custom-call | tf_op jit(solution)/shard_map/pallas_call | solution.py:102
  24.8 1.8 %reshape.100 = bf16[128,2,640]{2,1,0:T(2,128)(2,1)} reshape(bf16[256,640]{1,0:T(8,128)(2,1)} %shard_map.64) | data formatting | bytes 655360 | tf_op jit(solution)/shard_map/reshape | solution.py:148
  26.6 0.0 copy-start.2
  26.6 18.5 %all-to-all-start = ((bf16[128,2,640]{2,1,0:T(2,128)(2,1)}), bf16[128,2,640]{2,1,0:T(2,128)(2,1)S(1)}, u32[]{:S(2)}, u32[]{:S(2)}) async-start(bf16[128,2,640]{2,1,0:T(2,128)(2,1)} %reshape.100), calls=%async_computation | async-start | bytes 655360 | tf_op jit(solution)/shard_map/all_to_all | solution.py:149
  45.1 0.0 copy-done
  45.1 0.6 fusion.1
  45.8 1.2 %copy.28 = bf16[256,128,15]{1,0,2:T(8,128)(2,1)} copy(bf16[256,128,15]{1,2,0:T(8,128)(2,1)S(1)} %fusion.1) | data formatting | bytes 1966080 | tf_op jit(solution)/shard_map/gab,jtb->gajt/dot_general | solution.py:31
  47.0 0.0 copy-done.2
  47.0 0.1 iota_add_fusion
  47.1 0.7 %add.51.target_ref = s32[1,256]{1,0:T(1,128)} reshape(s32[128,2]{1,0:T(8,128)S(1)} %iota_add_fusion) | data formatting | bytes 2048 | tf_op jit(solution)/shard_map/add | solution.py:151
  47.8 13.9 %all-to-all-done = bf16[128,2,640]{2,1,0:T(2,128)(2,1)S(1)} async-done(((bf16[128,2,640]{2,1,0:T(2,128)(2,1)}), bf16[128,2,640]{2,1,0:T(2,128)(2,1)S(1)}, u32[]{:S(2)}, u32[]{:S(2)}) %all-to-all-start) | async-done | bytes 327712 | tf_op jit(solution)/shard_map/all_to_all | solution.py:149
  61.7 0.8 %reshape.101.data_ref = bf16[256,640]{1,0:T(8,128)(2,1)} reshape(bf16[128,2,640]{2,1,0:T(2,128)(2,1)S(1)} %all-to-all-done) | data formatting | bytes 655360 | tf_op jit(solution)/shard_map/reshape | solution.py:150
  62.5 5.5 %shard_map.65 = bf16[4,256,128]{2,1,0:T(8,128)(2,1)} custom-call(s32[1,256]{1,0:T(1,128)} %add.51.target_ref, bf16[256,640]{1,0:T(8,128)(2,1)} %reshape.101.data_ref, bf16[1,15,256,128]{3,2,1,0:T(8,128)(2,1)} %bitcast.26), custom_call_target="tpu_custom_call" | custom-call | tf_op jit(solution)/shard_map/pallas_call | solution.py:121
  68.0 1.8 %copy.29 = bf16[4,128,2,128]{3,2,0,1:T(2,128)(2,1)} copy(bf16[4,128,2,128]{3,2,1,0:T(2,128)(2,1)} %bitcast.29) | data formatting | bytes 524288 | tf_op jit(solution)/shard_map/reshape | solution.py:153
  (3 shorter events, 0.1 us)
Async XLA Ops:
  0.0 45.1 %copy-start = (bf16[15,15]{1,0:T(8,128)(2,1)S(1)}, bf16[15,15]{1,0:T(8,128)(2,1)}, u32[]{:S(2)}) copy-start(bf16[15,15]{1,0:T(8,128)(2,1)} %param.8) | copy-start | bytes 1354
  1.2 13.7 %collective-permute-start = (bf16[4,256,14]{2,1,0:T(8,128)(2,1)S(1)}, bf16[4,256,14]{2,1,0:T(8,128)(2,1)S(1)}, u32[]{:S(2)}, u32[]{:S(2)}) collective-permute-start(bf16[4,256,14]{2,1,0:T(8,128)(2,1)S(1)} %get-tuple-element.6), channel_id=1, source_target_pairs={{1,0},{2,1},{3,2},{5,4},{6,5},{7,6},{9,8},{10,9},{11,10},{13,12},{... | collective-permute-start | bytes 86024 | tf_op jit(solution)/shard_map/ppermute | solution.py:20
  2.5 12.4 %collective-permute-start.1 = (bf16[4,256,14]{2,1,0:T(8,128)(2,1)S(1)}, bf16[4,256,14]{2,1,0:T(8,128)(2,1)S(1)}, u32[]{:S(2)}, u32[]{:S(2)}) collective-permute-start(bf16[4,256,14]{2,1,0:T(8,128)(2,1)S(1)} %get-tuple-element.5), channel_id=1, source_target_pairs={{0,1},{1,2},{2,3},{4,5},{5,6},{6,7},{8,9},{9,10},{10,11},{12,13},{... | collective-permute-start | bytes 86024 | tf_op jit(solution)/shard_map/ppermute | solution.py:19
  10.3 4.7 %copy-start.1 = (bf16[1,4,256,128]{3,2,1,0:T(8,128)(2,1)S(1)}, bf16[1,4,256,128]{3,2,1,0:T(8,128)(2,1)}, u32[]{:S(2)}) copy-start(bf16[1,4,256,128]{3,2,1,0:T(8,128)(2,1)} %param.6) | copy-start | bytes 786436
  26.6 20.4 %copy-start.2 = (s32[128]{0:T(128)S(1)}, s32[128]{0:T(128)}, u32[]{:S(2)}) copy-start(s32[128]{0:T(128)} %param.11) | copy-start | bytes 1540
  26.6 35.1 %all-to-all-start = ((bf16[128,2,640]{2,1,0:T(2,128)(2,1)}), bf16[128,2,640]{2,1,0:T(2,128)(2,1)S(1)}, u32[]{:S(2)}, u32[]{:S(2)}) async-start(bf16[128,2,640]{2,1,0:T(2,128)(2,1)} %reshape.100), calls=%async_computation | async-start | bytes 655360 | tf_op jit(solution)/shard_map/all_to_all | solution.py:149

commit v4 on v3

--- a/solution.py
+++ b/solution.py
@@ -28,7 +28,7 @@
     t = jnp.arange(samples, dtype=jnp.int32)
     b = (j[:, None] - t[None, :] + reach) % EXT
     onehot = (b[:, :, None] == jnp.arange(taps, dtype=jnp.int32)[None, None, :]).astype(jnp.bfloat16)
-    tables = jnp.einsum("gab,jtb->gajt", tap_set, onehot, preferred_element_type=jnp.float32)
+    tables = jnp.einsum("gab,jtb->jgat", tap_set, onehot, preferred_element_type=jnp.float32)
     return tables.astype(jnp.bfloat16)
 
 
@@ -51,7 +51,7 @@
     acc = jnp.zeros((rows, LANES), jnp.float32)
     acc_h = jnp.zeros((rows, LANES), jnp.float32)
     for a in range(taps):
-        table = table_ref[0, a]
+        table = table_ref[:, 0, a, :]
         scr_ref[8:rows + 8, :] = jnp.dot(ordered, table, preferred_element_type=jnp.float32)
         scr_ref[second:second + rows, :] = jnp.dot(swapped, table, preferred_element_type=jnp.float32)
         acc = acc + scr_ref[pl.ds(a + 8 - reach, rows), :]
@@ -89,7 +89,7 @@
         ordered = jnp.concatenate([main, mine], axis=1).astype(jnp.bfloat16)
         acc = jnp.zeros((rows, LANES), jnp.float32)
         for a in range(taps):
-            part = jnp.dot(ordered, table_ref[0, a], preferred_element_type=jnp.float32)
+            part = jnp.dot(ordered, table_ref[:, 0, a, :], preferred_element_type=jnp.float32)
             scr_ref[pad:rows + pad, :] = part
             acc = acc + scr_ref[pl.ds(pad + group * (a - reach), rows), :]
         out_ref[c] = acc.astype(out_ref.dtype)
@@ -97,7 +97,7 @@
 
 def fan_call(place, edge, ext, tables, live_col):
     comps, rows, _ = ext.shape
-    taps = tables.shape[1]
+    taps = tables.shape[2]
     kernel = functools.partial(fan_kernel, taps=taps, live_col=live_col, comps=comps)
     return pl.pallas_call(
         kernel,
@@ -106,7 +106,7 @@
             pl.BlockSpec((1, rows), lambda c: (0, 0)),
             pl.BlockSpec((1, LANES), lambda c: (0, 0)),
             pl.BlockSpec((1, rows, EXT), lambda c: (c, 0, 0)),
-            pl.BlockSpec((1, taps, EXT, LANES), lambda c: (c, 0, 0, 0)),
+            pl.BlockSpec((EXT, 1, taps, LANES), lambda c: (0, c, 0, 0)),
         ],
         out_specs=pl.BlockSpec((rows, (comps + 1) * LANES), lambda c: (0, 0)),
         out_shape=jax.ShapeDtypeStruct((rows, (comps + 1) * LANES), jnp.bfloat16),
@@ -116,7 +116,7 @@
 
 def dip_call(target, data, tables, group, comps):
     rows = data.shape[0]
-    taps = tables.shape[1]
+    taps = tables.shape[2]
     kernel = functools.partial(dip_kernel, taps=taps, group=group, comps=comps)
     return pl.pallas_call(
         kernel,

time: 70.3 us -> 76.9 us (1.094)
  Pallas kernels: 13.8 us -> 22.6 us
  local copies, waits for them, and re-layouts: 13.6 us -> 7.95 us
  matrix products: 2.58 us -> 5.53 us
    dot_general x2 -> x0, local copies, waits for them, and re-layouts: 5.75 us -> none  [circulant(): jnp.einsum('gab,jtb->gajt', tap_set, onehot, preferred_element_type=jnp.f...]
    pallas_call x1, Pallas kernels: 5.49 us -> 10.4 us  [dip_call(): pl.pallas_call(kernel, out_shape=jax.ShapeDtypeStruct((comps, rows, LANES...]
    pallas_call x1, Pallas kernels: 8.34 us -> 12.3 us  [fan_call(): pl.pallas_call(kernel, grid=(comps,), in_specs=[pl.BlockSpec((1, rows), l...]
    dot_general x2, matrix products: 2.58 us -> 5.53 us  [circulant(): jnp.einsum('gab,jtb->jgat', tap_set, onehot, preferred_element_type=jnp.f...]
  transfers between devices with their start and end apart: 3 -> 3, of which waited for: 1 -> 1; matrix products, arithmetic and copies ran while one was open for 15% -> 10% of each run, Pallas kernels for 0% -> 0%
where the time goes in v4:
time: 76.9 us; the launch traced here: 76 us
  starting transfers between devices  24.3 us (32%)
  Pallas kernels  22.6 us (29%)
  waiting for transfers between devices  14.2 us (18%)
  local copies, waits for them, and re-layouts  7.95 us (10%)
  matrix products  5.53 us (7%)
  other arithmetic  1.36 us (2%)
    all_to_all x1, starting transfers between devices, on_device(): lax.all_to_all(sent, 'shot', split_axis=0, concat_axis=0, tiled=True)  18.4 us
    all_to_all x1, waiting for transfers between devices, on_device(): lax.all_to_all(sent, 'shot', split_axis=0, concat_axis=0, tiled=True)  14.2 us
    pallas_call x1, Pallas kernels, fan_call(): pl.pallas_call(kernel, grid=(comps,), in_specs=[pl.BlockSpec((1, rows), l...  12.3 us
    pallas_call x1, Pallas kernels, dip_call(): pl.pallas_call(kernel, out_shape=jax.ShapeDtypeStruct((comps, rows, LANES...  10.4 us
    dot_general x2, matrix products, circulant(): jnp.einsum('gab,jtb->jgat', tap_set, onehot, preferred_element_type=jnp.f...  5.53 us
    ppermute x1, starting transfers between devices, time_halo(): lax.ppermute(lax.slice_in_dim(block, samples - width, None, axis=-1), axi...  4.59 us
    reshape x1, local copies, waits for them, and re-layouts, on_device(): return out.reshape(comps, devices, group, samples).transpose(1, 0, 2, 3)  1.83 us
    reshape x1, local copies, waits for them, and re-layouts, on_device(): sent = packed.reshape(devices, group, packed.shape[-1])  1.82 us
  transfers between devices with their start and end apart: 3, of which 1 were waited for; matrix products, arithmetic and copies ran while one was open for 10% of the time, Pallas kernels for 0%

profile of v4, /device:TPU:1, one launch (start us, length us, event | category | flops | bytes accessed | tf_op | source)
XLA Modules:
  0.0 76.0 jit_solution(1861034029904377929)
XLA Ops:
  0.0 0.0 copy-start
  0.0 1.2 %fusion.11 = (bf16[4,256,14]{2,1,0:T(8,128)(2,1)S(1)}, bf16[4,256,14]{2,1,0:T(8,128)(2,1)S(1)}) fusion(bf16[4,256,128]{2,1,0:T(8,128)(2,1)} %bitcast.23), kind=kLoop, calls=%fused_computation.21 | loop fusion | bytes 114688 | tf_op jit(solution)/shard_map/slice | solution.py:19
  1.2 1.3 %collective-permute-start = (bf16[4,256,14]{2,1,0:T(8,128)(2,1)S(1)}, bf16[4,256,14]{2,1,0:T(8,128)(2,1)S(1)}, u32[]{:S(2)}, u32[]{:S(2)}) collective-permute-start(bf16[4,256,14]{2,1,0:T(8,128)(2,1)S(1)} %get-tuple-element.6), channel_id=1, source_target_pairs={{1,0},{2,1},{3,2},{5,4},{6,5},{7,6},{9,8},{10,9},{11,10},{13,12},{... | collective-permute-start | bytes 86024 | tf_op jit(solution)/shard_map/ppermute | solution.py:20
  2.5 4.6 %collective-permute-start.1 = (bf16[4,256,14]{2,1,0:T(8,128)(2,1)S(1)}, bf16[4,256,14]{2,1,0:T(8,128)(2,1)S(1)}, u32[]{:S(2)}, u32[]{:S(2)}) collective-permute-start(bf16[4,256,14]{2,1,0:T(8,128)(2,1)S(1)} %get-tuple-element.5), channel_id=1, source_target_pairs={{0,1},{1,2},{2,3},{4,5},{5,6},{6,7},{8,9},{9,10},{10,11},{12,13},{... | collective-permute-start | bytes 86024 | tf_op jit(solution)/shard_map/ppermute | solution.py:19
  7.1 0.1 add_select_fusion
  7.1 0.7 convert_reduce_fusion
  7.8 0.0 copy-start.1
  7.8 3.9 %convert_bitcast_fusion.table_ref = bf16[256,4,15,128]{3,2,1,0:T(8,128)(2,1)} fusion(s32[256,128]{1,0:T(8,128)S(1)} %add_select_fusion, bf16[4,15,15]{2,0,1:T(4,128)(2,1)} %param.7), kind=kOutput, calls=%fused_computation | convolution fusion | flops 61440000 | bytes 4065032 | tf_op jit(solution)/shard_map/gab,jtb->jgat/dot_general | solution.py:31
  11.8 0.5 select_convert_fusion.edge_ref
  12.3 0.0 collective-permute-done
  12.3 0.0 collective-permute-done.1
  12.3 0.1 broadcast_in_dim.42
  12.5 0.0 copy-done.1
  12.5 1.4 %concatenate.3.ext_ref = bf16[4,256,256]{2,1,0:T(8,128)(2,1)} concatenate(bf16[4,256,128]{2,1,0:T(8,128)(2,1)S(1)} %bitcast.24, bf16[4,256,14]{2,1,0:T(8,128)(2,1)S(1)} %collective-permute-done, bf16[4,256,18]{2,1,0:T(8,128)(2,1)S(1)} %broadcast_in_dim.22, bf16[4,256,1]{2,1,0:T(8,128)(2,1)S(1)} %broadcast_in_dim.42, bf16[4,256,81]{2,1,0:T(8,128)(2,1)S(1)} %broadcast_in_dim.43, ...), dimensions={2} | concatenate | bytes 1048576 | tf_op jit(solution)/shard_map/concatenate | solution.py:142
  13.9 0.0 copy-start.2
  13.9 12.3 %shard_map.64 = bf16[256,640]{1,0:T(8,128)(2,1)} custom-call(s32[1,256]{1,0:T(1,128)} %bitcast.26, f32[1,128]{1,0:T(1,128)} %select_convert_fusion.edge_ref, bf16[4,256,256]{2,1,0:T(8,128)(2,1)} %concatenate.3.ext_ref, bf16[256,4,15,128]{3,2,1,0:T(8,128)(2,1)} %convert_bitcast_fusion.table_ref), custom_call_target="tpu_custom_call" | custom-call | tf_op jit(solution)/shard_map/pallas_call | solution.py:102
  26.2 1.8 %reshape.100 = bf16[128,2,640]{2,1,0:T(2,128)(2,1)} reshape(bf16[256,640]{1,0:T(8,128)(2,1)} %shard_map.64) | data formatting | bytes 655360 | tf_op jit(solution)/shard_map/reshape | solution.py:148
  28.0 18.4 %all-to-all-start = ((bf16[128,2,640]{2,1,0:T(2,128)(2,1)}), bf16[128,2,640]{2,1,0:T(2,128)(2,1)S(1)}, u32[]{:S(2)}, u32[]{:S(2)}) async-start(bf16[128,2,640]{2,1,0:T(2,128)(2,1)} %reshape.100), calls=%async_computation | async-start | bytes 655360 | tf_op jit(solution)/shard_map/all_to_all | solution.py:149
  46.4 0.0 copy-done.2
  46.5 0.1 iota_add_fusion
  46.5 0.7 add.51.target_ref
  47.2 0.0 copy-done
  47.2 1.6 %fusion.4.table_ref = bf16[256,1,15,128]{3,2,1,0:T(8,128)(2,1)} fusion(s32[256,128]{1,0:T(8,128)S(1)} %add_select_fusion, bf16[15,15]{1,0:T(8,128)(2,1)S(1)} %copy-done), kind=kOutput, calls=%fused_computation.5 | convolution fusion | flops 15728640 | bytes 1114562 | tf_op jit(solution)/shard_map/gab,jtb->jgat/dot_general | solution.py:31
  48.9 14.2 %all-to-all-done = bf16[128,2,640]{2,1,0:T(2,128)(2,1)S(1)} async-done(((bf16[128,2,640]{2,1,0:T(2,128)(2,1)}), bf16[128,2,640]{2,1,0:T(2,128)(2,1)S(1)}, u32[]{:S(2)}, u32[]{:S(2)}) %all-to-all-start) | async-done | bytes 327712 | tf_op jit(solution)/shard_map/all_to_all | solution.py:149
  63.0 0.9 %reshape.101.data_ref = bf16[256,640]{1,0:T(8,128)(2,1)} reshape(bf16[128,2,640]{2,1,0:T(2,128)(2,1)S(1)} %all-to-all-done) | data formatting | bytes 655360 | tf_op jit(solution)/shard_map/reshape | solution.py:150
  63.9 10.4 %shard_map.65 = bf16[4,256,128]{2,1,0:T(8,128)(2,1)} custom-call(s32[1,256]{1,0:T(1,128)} %add.51.target_ref, bf16[256,640]{1,0:T(8,128)(2,1)} %reshape.101.data_ref, bf16[256,1,15,128]{3,2,1,0:T(8,128)(2,1)} %fusion.4.table_ref), custom_call_target="tpu_custom_call" | custom-call | tf_op jit(solution)/shard_map/pallas_call | solution.py:121
  74.2 1.8 %copy.17 = bf16[4,128,2,128]{3,2,0,1:T(2,128)(2,1)} copy(bf16[4,128,2,128]{3,2,1,0:T(2,128)(2,1)} %bitcast.25) | data formatting | bytes 524288 | tf_op jit(solution)/shard_map/reshape | solution.py:153
  (3 shorter events, 0.1 us)
Async XLA Ops:
  0.0 47.2 %copy-start = (bf16[15,15]{1,0:T(8,128)(2,1)S(1)}, bf16[15,15]{1,0:T(8,128)(2,1)}, u32[]{:S(2)}) copy-start(bf16[15,15]{1,0:T(8,128)(2,1)} %param.8) | copy-start | bytes 1354
  1.2 11.1 %collective-permute-start = (bf16[4,256,14]{2,1,0:T(8,128)(2,1)S(1)}, bf16[4,256,14]{2,1,0:T(8,128)(2,1)S(1)}, u32[]{:S(2)}, u32[]{:S(2)}) collective-permute-start(bf16[4,256,14]{2,1,0:T(8,128)(2,1)S(1)} %get-tuple-element.6), channel_id=1, source_target_pairs={{1,0},{2,1},{3,2},{5,4},{6,5},{7,6},{9,8},{10,9},{11,10},{13,12},{... | collective-permute-start | bytes 86024 | tf_op jit(solution)/shard_map/ppermute | solution.py:20
  2.5 9.8 %collective-permute-start.1 = (bf16[4,256,14]{2,1,0:T(8,128)(2,1)S(1)}, bf16[4,256,14]{2,1,0:T(8,128)(2,1)S(1)}, u32[]{:S(2)}, u32[]{:S(2)}) collective-permute-start(bf16[4,256,14]{2,1,0:T(8,128)(2,1)S(1)} %get-tuple-element.5), channel_id=1, source_target_pairs={{0,1},{1,2},{2,3},{4,5},{5,6},{6,7},{8,9},{9,10},{10,11},{12,13},{... | collective-permute-start | bytes 86024 | tf_op jit(solution)/shard_map/ppermute | solution.py:19
  7.8 4.7 %copy-start.1 = (bf16[1,4,256,128]{3,2,1,0:T(8,128)(2,1)S(1)}, bf16[1,4,256,128]{3,2,1,0:T(8,128)(2,1)}, u32[]{:S(2)}) copy-start(bf16[1,4,256,128]{3,2,1,0:T(8,128)(2,1)} %param.6) | copy-start | bytes 786436
  13.9 32.5 %copy-start.2 = (s32[128]{0:T(128)S(1)}, s32[128]{0:T(128)}, u32[]{:S(2)}) copy-start(s32[128]{0:T(128)} %param.11) | copy-start | bytes 1540
  28.0 35.0 %all-to-all-start = ((bf16[128,2,640]{2,1,0:T(2,128)(2,1)}), bf16[128,2,640]{2,1,0:T(2,128)(2,1)S(1)}, u32[]{:S(2)}, u32[]{:S(2)}) async-start(bf16[128,2,640]{2,1,0:T(2,128)(2,1)} %reshape.100), calls=%async_computation | async-start | bytes 655360 | tf_op jit(solution)/shard_map/all_to_all | solution.py:149

commit v5 on v3

--- a/solution.py
+++ b/solution.py
@@ -32,16 +32,19 @@
     return tables.astype(jnp.bfloat16)
 
 
-def fan_kernel(place_ref, edge_ref, ext_ref, table_ref, out_ref, scr_ref, halo_ref, *, taps, live_col, comps):
+def fan_kernel(place_ref, edge_ref, live_ref, block_ref, prev_ref, next_ref, table_ref, out_ref, scr_ref, halo_ref, *, taps, comps):
     c = pl.program_id(0)
-    rows = ext_ref.shape[1]
+    rows = block_ref.shape[1]
     samples = LANES
     reach = (taps - 1) // 2
+    wide = 2 * reach
     place = place_ref[...]
     select = (lax.broadcasted_iota(jnp.int32, (rows, rows), 0) == place).astype(jnp.bfloat16)
-    ordered = jnp.dot(select, ext_ref[0], preferred_element_type=jnp.float32)
-    keep = ordered[:, live_col:live_col + 1]
-    ordered = ordered.astype(jnp.bfloat16)
+    keep = jnp.sum(select.astype(jnp.float32) * live_ref[...].astype(jnp.float32), axis=1, keepdims=True)
+    lane = lax.broadcasted_iota(jnp.int32, (rows, LANES), 1)
+    outer = jnp.where(lane < wide, next_ref[0], jnp.where(lane >= LANES - wide, prev_ref[0], jnp.zeros_like(prev_ref[0])))
+    ext = jnp.concatenate([block_ref[0], outer], axis=1)
+    ordered = jnp.dot(select, ext, preferred_element_type=jnp.float32).astype(jnp.bfloat16)
     swapped = jnp.concatenate([ordered[:, samples:], ordered[:, :samples]], axis=1)
     second = rows + 16
     zeros = jnp.zeros((8, LANES), jnp.float32)
@@ -57,7 +60,6 @@
         acc = acc + scr_ref[pl.ds(a + 8 - reach, rows), :]
         acc_h = acc_h + scr_ref[pl.ds(second + a - reach, rows), :]
     out_ref[:, pl.ds(pl.multiple_of(c * samples, samples), samples)] = (acc * keep).astype(out_ref.dtype)
-    lane = lax.broadcasted_iota(jnp.int32, (rows, LANES), 1)
     for k in range(comps):
         @pl.when(c == k)
         def _():
@@ -95,23 +97,27 @@
         out_ref[c] = acc.astype(out_ref.dtype)
 
 
-def fan_call(place, edge, ext, tables, live_col):
-    comps, rows, _ = ext.shape
+def fan_call(place, edge, live, block, prev, nxt, tables):
+    comps, rows, samples = block.shape
     taps = tables.shape[1]
-    kernel = functools.partial(fan_kernel, taps=taps, live_col=live_col, comps=comps)
+    kernel = functools.partial(fan_kernel, taps=taps, comps=comps)
+    part = pl.BlockSpec((1, rows, samples), lambda c: (c, 0, 0))
     return pl.pallas_call(
         kernel,
         grid=(comps,),
         in_specs=[
             pl.BlockSpec((1, rows), lambda c: (0, 0)),
             pl.BlockSpec((1, LANES), lambda c: (0, 0)),
-            pl.BlockSpec((1, rows, EXT), lambda c: (c, 0, 0)),
+            pl.BlockSpec((1, rows), lambda c: (0, 0)),
+            part,
+            part,
+            part,
             pl.BlockSpec((1, taps, EXT, LANES), lambda c: (c, 0, 0, 0)),
         ],
         out_specs=pl.BlockSpec((rows, (comps + 1) * LANES), lambda c: (0, 0)),
         out_shape=jax.ShapeDtypeStruct((rows, (comps + 1) * LANES), jnp.bfloat16),
         scratch_shapes=[pltpu.VMEM((2 * rows + 24, LANES), jnp.float32), pltpu.VMEM((rows, LANES), jnp.float32)],
-    )(place, edge, ext, tables)
+    )(place, edge, live, block, prev, nxt, tables)
 
 
 def dip_call(target, data, tables, group, comps):
@@ -134,16 +140,15 @@
     group = nodes // devices
 
     block = records[0]
-    low, high = time_halo(block, "tm", wide)
-    live_col = samples + 32
-    live = jnp.broadcast_to(live_mask[0].astype(jnp.bfloat16)[None, :, None], (comps, nodes, 1))
-    gap1 = jnp.zeros((comps, nodes, live_col - samples - wide), jnp.bfloat16)
-    gap2 = jnp.zeros((comps, nodes, EXT - wide - live_col - 1), jnp.bfloat16)
-    ext = jnp.concatenate([block, high, gap1, live, gap2, low], axis=-1)
+    count = lax.axis_size("tm")
+    forward = [(i, i + 1) for i in range(count - 1)]
+    backward = [(target, source) for source, target in forward]
+    prev = lax.ppermute(block, "tm", forward)
+    nxt = lax.ppermute(block, "tm", backward)
     place = lax.axis_index("tm")
     lane = jnp.arange(LANES, dtype=jnp.int32) % wide
-    edge = jnp.where(lane < reach, place > 0, place < lax.axis_size("tm") - 1).astype(jnp.float32)[None, :]
-    packed = fan_call(node_place[None, :], edge, ext, circulant(fan_taps, samples), live_col)
+    edge = jnp.where(lane < reach, place > 0, place < count - 1).astype(jnp.float32)[None, :]
+    packed = fan_call(node_place[None, :], edge, live_mask, block, prev, nxt, circulant(fan_taps, samples))
 
     sent = packed.reshape(devices, group, packed.shape[-1])
     arrived = lax.all_to_all(sent, "shot", split_axis=0, concat_axis=0, tiled=True)

time: 70.3 us -> 71.1 us (1.011)
  matrix products: 2.58 us -> 4.53 us
  starting transfers between devices: 24.4 us -> 23.4 us
    dot_general x2, local copies, waits for them, and re-layouts: 5.75 us -> 7.94 us  [circulant(): jnp.einsum('gab,jtb->gajt', tap_set, onehot, preferred_element_type=jnp.f...]
    dot_general x2, matrix products: 2.58 us -> 4.53 us  [circulant(): jnp.einsum('gab,jtb->gajt', tap_set, onehot, preferred_element_type=jnp.f...]
    concatenate x1 -> x0, local copies, waits for them, and re-layouts: 1.34 us -> none  [on_device(): ext = jnp.concatenate([block, high, gap1, live, gap2, low], axis=-1)]
    slice x1 -> x0, local copies, waits for them, and re-layouts: 1.18 us -> none  [time_halo(): lax.slice_in_dim(block, samples - width, None, axis=-1)]
    unnamed x6 -> x8, local copies, waits for them, and re-layouts: 0.01 us -> 0.78 us
  transfers between devices with their start and end apart: 3 -> 3, of which waited for: 1 -> 1; matrix products, arithmetic and copies ran while one was open for 15% -> 20% of each run, Pallas kernels for 0% -> 0%
where the time goes in v5:
time: 71.1 us; the launch traced here: 70.4 us
  starting transfers between devices  23.4 us (33%)
  local copies, waits for them, and re-layouts  13.9 us (20%)
  waiting for transfers between devices  13.9 us (20%)
  Pallas kernels  13.9 us (20%)
  matrix products  4.53 us (6%)
    all_to_all x1, starting transfers between devices, on_device(): lax.all_to_all(sent, 'shot', split_axis=0, concat_axis=0, tiled=True)  18 us
    all_to_all x1, waiting for transfers between devices, on_device(): lax.all_to_all(sent, 'shot', split_axis=0, concat_axis=0, tiled=True)  13.9 us
    pallas_call x1, Pallas kernels, fan_call(): pl.pallas_call(kernel, grid=(comps,), in_specs=[pl.BlockSpec((1, rows), l...  8.38 us
    dot_general x2, local copies, waits for them, and re-layouts, circulant(): jnp.einsum('gab,jtb->gajt', tap_set, onehot, preferred_element_type=jnp.f...  7.94 us
    pallas_call x1, Pallas kernels, dip_call(): pl.pallas_call(kernel, out_shape=jax.ShapeDtypeStruct((comps, rows, LANES...  5.48 us
    dot_general x2, matrix products, circulant(): jnp.einsum('gab,jtb->gajt', tap_set, onehot, preferred_element_type=jnp.f...  4.53 us
    ppermute x1, starting transfers between devices, on_device(): prev = lax.ppermute(block, 'tm', forward)  4.08 us
    reshape x1, local copies, waits for them, and re-layouts, on_device(): return out.reshape(comps, devices, group, samples).transpose(1, 0, 2, 3)  1.83 us
  transfers between devices with their start and end apart: 3, of which 1 were waited for; matrix products, arithmetic and copies ran while one was open for 20% of the time, Pallas kernels for 0%

profile of v5, /device:TPU:1, one launch (start us, length us, event | category | flops | bytes accessed | tf_op | source)
XLA Modules:
  0.0 70.4 jit_solution(12111909151918367064)
XLA Ops:
  0.0 0.0 copy-start
  0.0 4.1 %collective-permute-start = (bf16[4,256,128]{2,1,0:T(8,128)(2,1)}, bf16[4,256,128]{2,1,0:T(8,128)(2,1)S(1)}, u32[]{:S(2)}, u32[]{:S(2)}) collective-permute-start(bf16[4,256,128]{2,1,0:T(8,128)(2,1)} %bitcast.28), channel_id=1, source_target_pairs={{0,1},{1,2},{2,3},{4,5},{5,6},{6,7},{8,9},{9,10},{10,11},{12,13},{... | collective-permute-start | bytes 786440 | tf_op jit(solution)/shard_map/ppermute | solution.py:146
  4.1 1.3 %collective-permute-start.1 = (bf16[4,256,128]{2,1,0:T(8,128)(2,1)}, bf16[4,256,128]{2,1,0:T(8,128)(2,1)S(1)}, u32[]{:S(2)}, u32[]{:S(2)}) collective-permute-start(bf16[4,256,128]{2,1,0:T(8,128)(2,1)} %bitcast.29), channel_id=1, source_target_pairs={{1,0},{2,1},{3,2},{5,4},{6,5},{7,6},{9,8},{10,9},{11,10},{13,12},{... | collective-permute-start | bytes 786440 | tf_op jit(solution)/shard_map/ppermute | solution.py:147
  5.4 0.1 add_select_fusion
  5.5 3.9 %fusion.3 = bf16[256,128,4,15]{1,3,2,0:T(8,128)(2,1)} fusion(s32[256,128]{1,0:T(8,128)S(1)} %add_select_fusion, bf16[4,15,15]{2,0,1:T(4,128)(2,1)} %param.7), kind=kOutput, calls=%fused_computation.5 | convolution fusion | flops 59473920 | bytes 4065032 | tf_op jit(solution)/shard_map/gab,jtb->gajt/dot_general | solution.py:31
  9.4 6.7 %copy.27 = bf16[256,128,4,15]{1,0,3,2:T(8,128)(2,1)} copy(bf16[256,128,4,15]{1,3,2,0:T(8,128)(2,1)} %fusion.3) | data formatting | bytes 7864320 | tf_op jit(solution)/shard_map/gab,jtb->gajt/dot_general | solution.py:31
  16.1 0.6 select_convert_fusion.edge_ref
  16.6 0.0 collective-permute-done.prev_ref
  16.6 0.0 copy-start.1
  16.6 0.0 collective-permute-done.1.next_ref
  16.7 0.0 copy-start.2
  16.7 0.7 copy-done.1
  17.3 0.1 copy-done.2
  17.4 8.4 %shard_map.64 = bf16[256,640]{1,0:T(8,128)(2,1)} custom-call(s32[1,256]{1,0:T(1,128)} %bitcast.31, f32[1,128]{1,0:T(1,128)} %select_convert_fusion.edge_ref, s32[1,256]{1,0:T(1,128)} %live_ref.1, bf16[4,256,128]{2,1,0:T(8,128)(2,1)} %bitcast.30, bf16[4,256,128]{2,1,0:T(8,128)(2,1)} %copy-done.1, bf16[4,256,128]{2,1,0:T(8,128)(2,1)} %copy-done.2, ...), custom_call_target="tpu_custom_call" | custom-call | tf_op jit(solution)/shard_map/pallas_call | solution.py:105
  25.8 1.8 %reshape.92 = bf16[128,2,640]{2,1,0:T(2,128)(2,1)} reshape(bf16[256,640]{1,0:T(8,128)(2,1)} %shard_map.64) | data formatting | bytes 655360 | tf_op jit(solution)/shard_map/reshape | solution.py:153
  27.6 0.0 copy-start.3
  27.6 18.0 %all-to-all-start = ((bf16[128,2,640]{2,1,0:T(2,128)(2,1)}), bf16[128,2,640]{2,1,0:T(2,128)(2,1)S(1)}, u32[]{:S(2)}, u32[]{:S(2)}) async-start(bf16[128,2,640]{2,1,0:T(2,128)(2,1)} %reshape.92), calls=%async_computation | async-start | bytes 655360 | tf_op jit(solution)/shard_map/all_to_all | solution.py:154
  45.6 0.0 copy-done
  45.6 0.6 fusion.1
  46.3 1.2 %copy.28 = bf16[256,128,15]{1,0,2:T(8,128)(2,1)} copy(bf16[256,128,15]{1,2,0:T(8,128)(2,1)S(1)} %fusion.1) | data formatting | bytes 1966080 | tf_op jit(solution)/shard_map/gab,jtb->gajt/dot_general | solution.py:31
  47.5 0.0 copy-done.3
  47.5 0.1 iota_add_fusion
  47.6 0.7 %add.51.target_ref = s32[1,256]{1,0:T(1,128)} reshape(s32[128,2]{1,0:T(8,128)S(1)} %iota_add_fusion) | data formatting | bytes 2048 | tf_op jit(solution)/shard_map/add | solution.py:156
  48.3 13.9 %all-to-all-done = bf16[128,2,640]{2,1,0:T(2,128)(2,1)S(1)} async-done(((bf16[128,2,640]{2,1,0:T(2,128)(2,1)}), bf16[128,2,640]{2,1,0:T(2,128)(2,1)S(1)}, u32[]{:S(2)}, u32[]{:S(2)}) %all-to-all-start) | async-done | bytes 327712 | tf_op jit(solution)/shard_map/all_to_all | solution.py:154
  62.2 0.8 %reshape.93.data_ref = bf16[256,640]{1,0:T(8,128)(2,1)} reshape(bf16[128,2,640]{2,1,0:T(2,128)(2,1)S(1)} %all-to-all-done) | data formatting | bytes 655360 | tf_op jit(solution)/shard_map/reshape | solution.py:155
  63.1 5.5 %shard_map.65 = bf16[4,256,128]{2,1,0:T(8,128)(2,1)} custom-call(s32[1,256]{1,0:T(1,128)} %add.51.target_ref, bf16[256,640]{1,0:T(8,128)(2,1)} %reshape.93.data_ref, bf16[1,15,256,128]{3,2,1,0:T(8,128)(2,1)} %bitcast.26), custom_call_target="tpu_custom_call" | custom-call | tf_op jit(solution)/shard_map/pallas_call | solution.py:127
  68.5 1.8 %copy.29 = bf16[4,128,2,128]{3,2,0,1:T(2,128)(2,1)} copy(bf16[4,128,2,128]{3,2,1,0:T(2,128)(2,1)} %bitcast.27) | data formatting | bytes 524288 | tf_op jit(solution)/shard_map/reshape | solution.py:158
  (1 shorter events, 0.0 us)
Async XLA Ops:
  0.0 45.6 %copy-start = (bf16[15,15]{1,0:T(8,128)(2,1)S(1)}, bf16[15,15]{1,0:T(8,128)(2,1)}, u32[]{:S(2)}) copy-start(bf16[15,15]{1,0:T(8,128)(2,1)} %param.8) | copy-start | bytes 1354
  0.0 16.6 %collective-permute-start = (bf16[4,256,128]{2,1,0:T(8,128)(2,1)}, bf16[4,256,128]{2,1,0:T(8,128)(2,1)S(1)}, u32[]{:S(2)}, u32[]{:S(2)}) collective-permute-start(bf16[4,256,128]{2,1,0:T(8,128)(2,1)} %bitcast.28), channel_id=1, source_target_pairs={{0,1},{1,2},{2,3},{4,5},{5,6},{6,7},{8,9},{9,10},{10,11},{12,13},{... | collective-permute-start | bytes 786440 | tf_op jit(solution)/shard_map/ppermute | solution.py:146
  4.1 12.6 %collective-permute-start.1 = (bf16[4,256,128]{2,1,0:T(8,128)(2,1)}, bf16[4,256,128]{2,1,0:T(8,128)(2,1)S(1)}, u32[]{:S(2)}, u32[]{:S(2)}) collective-permute-start(bf16[4,256,128]{2,1,0:T(8,128)(2,1)} %bitcast.29), channel_id=1, source_target_pairs={{1,0},{2,1},{3,2},{5,4},{6,5},{7,6},{9,8},{10,9},{11,10},{13,12},{... | collective-permute-start | bytes 786440 | tf_op jit(solution)/shard_map/ppermute | solution.py:147
  16.6 0.7 copy-start.1
  16.7 0.8 %copy-start.2 = (bf16[4,256,128]{2,1,0:T(8,128)(2,1)}, bf16[4,256,128]{2,1,0:T(8,128)(2,1)S(1)}, u32[]{:S(2)}) copy-start(bf16[4,256,128]{2,1,0:T(8,128)(2,1)S(1)} %collective-permute-done.1.next_ref) | copy-start | bytes 786436
  27.6 19.9 %copy-start.3 = (s32[128]{0:T(128)S(1)}, s32[128]{0:T(128)}, u32[]{:S(2)}) copy-start(s32[128]{0:T(128)} %param.11) | copy-start | bytes 1540
  27.6 34.6 %all-to-all-start = ((bf16[128,2,640]{2,1,0:T(2,128)(2,1)}), bf16[128,2,640]{2,1,0:T(2,128)(2,1)S(1)}, u32[]{:S(2)}, u32[]{:S(2)}) async-start(bf16[128,2,640]{2,1,0:T(2,128)(2,1)} %reshape.92), calls=%async_computation | async-start | bytes 655360 | tf_op jit(solution)/shard_map/all_to_all | solution.py:154

commit v6 on v3

--- a/solution.py
+++ b/solution.py
@@ -73,26 +73,32 @@
         out_ref[:, comps * samples:(comps + 1) * samples] = (halo_ref[...] * keep * edge_ref[...]).astype(out_ref.dtype)
 
 
-def dip_kernel(target_ref, data_ref, table_ref, out_ref, scr_ref, *, taps, group, comps):
+def dip_kernel(target_ref, data_ref, table_ref, out_ref, *, taps, group, comps):
     rows = data_ref.shape[0]
     samples = LANES
     reach = (taps - 1) // 2
-    pad = group * 8
+    stride = comps * group
+    out_rows = out_ref.shape[0]
     target = target_ref[...]
-    select = (lax.broadcasted_iota(jnp.int32, (rows, rows), 0) == target).astype(jnp.bfloat16)
-    halo = jnp.dot(select, data_ref[:, comps * samples:(comps + 1) * samples], preferred_element_type=jnp.float32)
-    scr_ref[0:pad, :] = jnp.zeros((pad, LANES), jnp.float32)
-    scr_ref[rows + pad:rows + 2 * pad, :] = jnp.zeros((pad, LANES), jnp.float32)
+    row = lax.broadcasted_iota(jnp.int32, (out_rows, rows), 0)
+    halo = data_ref[:, comps * samples:(comps + 1) * samples].astype(jnp.float32)
+    selects, parts = [], []
     for c in range(comps):
-        main = jnp.dot(select, data_ref[:, c * samples:(c + 1) * samples], preferred_element_type=jnp.float32)
-        mine = pltpu.roll(halo, (samples - reach - 2 * reach * c) % samples, 1)
-        ordered = jnp.concatenate([main, mine], axis=1).astype(jnp.bfloat16)
-        acc = jnp.zeros((rows, LANES), jnp.float32)
-        for a in range(taps):
-            part = jnp.dot(ordered, table_ref[0, a], preferred_element_type=jnp.float32)
-            scr_ref[pad:rows + pad, :] = part
-            acc = acc + scr_ref[pl.ds(pad + group * (a - reach), rows), :]
-        out_ref[c] = acc.astype(out_ref.dtype)
+        mine = pltpu.roll(halo, (samples - reach - 2 * reach * c) % samples, 1).astype(jnp.bfloat16)
+        parts.append(jnp.concatenate([data_ref[:, c * samples:(c + 1) * samples], mine], axis=1))
+        selects.append((row == target + group * c).astype(jnp.bfloat16))
+    gathered = jnp.dot(jnp.concatenate(selects, axis=1), jnp.concatenate(parts, axis=0), preferred_element_type=jnp.float32)
+    gathered = gathered.astype(jnp.bfloat16)
+    acc = jnp.zeros((out_rows, LANES), jnp.float32)
+    for a in range(taps):
+        part = jnp.dot(gathered, table_ref[0, a], preferred_element_type=jnp.float32)
+        shift = stride * (a - reach)
+        if shift > 0:
+            part = jnp.concatenate([part[shift:], jnp.zeros((shift, LANES), jnp.float32)], axis=0)
+        elif shift < 0:
+            part = jnp.concatenate([jnp.zeros((-shift, LANES), jnp.float32), part[:shift]], axis=0)
+        acc = acc + part
+    out_ref[...] = acc.astype(out_ref.dtype)
 
 
 def fan_call(place, edge, ext, tables, live_col):
@@ -120,8 +126,7 @@
     kernel = functools.partial(dip_kernel, taps=taps, group=group, comps=comps)
     return pl.pallas_call(
         kernel,
-        out_shape=jax.ShapeDtypeStruct((comps, rows, LANES), jnp.bfloat16),
-        scratch_shapes=[pltpu.VMEM((rows + 16 * group, LANES), jnp.float32)],
+        out_shape=jax.ShapeDtypeStruct((rows * comps, LANES), jnp.bfloat16),
     )(target, data, tables)
 
 
@@ -148,9 +153,10 @@
     sent = packed.reshape(devices, group, packed.shape[-1])
     arrived = lax.all_to_all(sent, "shot", split_axis=0, concat_axis=0, tiled=True)
     data = arrived.reshape(devices * group, packed.shape[-1])
-    target = (jnp.repeat(shot_place, group) * group + jnp.tile(jnp.arange(group, dtype=jnp.int32), devices))[None, :]
+    spread = comps * group
+    target = (jnp.repeat(shot_place, group) * spread + jnp.tile(jnp.arange(group, dtype=jnp.int32), devices))[None, :]
     out = dip_call(target, data, circulant(dip_taps[None], samples), group, comps)
-    return out.reshape(comps, devices, group, samples).transpose(1, 0, 2, 3)
+    return out.reshape(devices, comps, group, samples)
 
 
 def solution(mesh):

time: 70.3 us -> 68.4 us (0.973)
  local copies, waits for them, and re-layouts: 13.6 us -> 11.8 us
    reshape x1 -> x0, local copies, waits for them, and re-layouts: 1.83 us -> none  [on_device(): return out.reshape(comps, devices, group, samples).transpose(1, 0, 2, 3)]
where the time goes in v6:
time: 68.4 us; the launch traced here: 68 us
  starting transfers between devices  24.4 us (36%)
  waiting for transfers between devices  13.9 us (20%)
  Pallas kernels  13.8 us (20%)
  local copies, waits for them, and re-layouts  11.8 us (17%)
  matrix products  2.58 us (4%)
  other arithmetic  1.37 us (2%)
    all_to_all x1, starting transfers between devices, on_device(): lax.all_to_all(sent, 'shot', split_axis=0, concat_axis=0, tiled=True)  18.5 us
    all_to_all x1, waiting for transfers between devices, on_device(): lax.all_to_all(sent, 'shot', split_axis=0, concat_axis=0, tiled=True)  13.9 us
    pallas_call x1, Pallas kernels, fan_call(): pl.pallas_call(kernel, grid=(comps,), in_specs=[pl.BlockSpec((1, rows), l...  8.34 us
    dot_general x2, local copies, waits for them, and re-layouts, circulant(): jnp.einsum('gab,jtb->gajt', tap_set, onehot, preferred_element_type=jnp.f...  5.75 us
    pallas_call x1, Pallas kernels, dip_call(): pl.pallas_call(kernel, out_shape=jax.ShapeDtypeStruct((rows * comps, LANE...  5.49 us
    ppermute x1, starting transfers between devices, time_halo(): lax.ppermute(lax.slice_in_dim(block, samples - width, None, axis=-1), axi...  4.59 us
    dot_general x2, matrix products, circulant(): jnp.einsum('gab,jtb->gajt', tap_set, onehot, preferred_element_type=jnp.f...  2.58 us
    reshape x1, local copies, waits for them, and re-layouts, on_device(): sent = packed.reshape(devices, group, packed.shape[-1])  1.81 us
  transfers between devices with their start and end apart: 3, of which 1 were waited for; matrix products, arithmetic and copies ran while one was open for 15% of the time, Pallas kernels for 0%

profile of v6, /device:TPU:1, one launch (start us, length us, event | category | flops | bytes accessed | tf_op | source)
XLA Modules:
  0.0 68.0 jit_solution(17713406584036573948)
XLA Ops:
  0.0 0.0 copy-start
  0.0 1.2 %fusion.12 = (bf16[4,256,14]{2,1,0:T(8,128)(2,1)S(1)}, bf16[4,256,14]{2,1,0:T(8,128)(2,1)S(1)}) fusion(bf16[4,256,128]{2,1,0:T(8,128)(2,1)} %bitcast.24), kind=kLoop, calls=%fused_computation.22 | loop fusion | bytes 114688 | tf_op jit(solution)/shard_map/slice | solution.py:19
  1.2 1.3 %collective-permute-start = (bf16[4,256,14]{2,1,0:T(8,128)(2,1)S(1)}, bf16[4,256,14]{2,1,0:T(8,128)(2,1)S(1)}, u32[]{:S(2)}, u32[]{:S(2)}) collective-permute-start(bf16[4,256,14]{2,1,0:T(8,128)(2,1)S(1)} %get-tuple-element.6), channel_id=1, source_target_pairs={{1,0},{2,1},{3,2},{5,4},{6,5},{7,6},{9,8},{10,9},{11,10},{13,12},{... | collective-permute-start | bytes 86024 | tf_op jit(solution)/shard_map/ppermute | solution.py:20
  2.5 4.6 %collective-permute-start.1 = (bf16[4,256,14]{2,1,0:T(8,128)(2,1)S(1)}, bf16[4,256,14]{2,1,0:T(8,128)(2,1)S(1)}, u32[]{:S(2)}, u32[]{:S(2)}) collective-permute-start(bf16[4,256,14]{2,1,0:T(8,128)(2,1)S(1)} %get-tuple-element.5), channel_id=1, source_target_pairs={{0,1},{1,2},{2,3},{4,5},{5,6},{6,7},{8,9},{9,10},{10,11},{12,13},{... | collective-permute-start | bytes 86024 | tf_op jit(solution)/shard_map/ppermute | solution.py:19
  7.1 0.1 add_select_fusion
  7.1 0.7 %convert_reduce_fusion = bf16[256]{0:T(256)(128)(2,1)S(1)} fusion(s32[1,256]{1,0:T(1,128)} %param.9), kind=kLoop, calls=%fused_computation.20 | loop fusion | flops 256 | bytes 1536 | tf_op jit(solution)/shard_map/convert_element_type | solution.py:144
  7.8 2.0 %fusion.3 = bf16[256,128,4,15]{1,3,2,0:T(8,128)(2,1)S(1)} fusion(s32[256,128]{1,0:T(8,128)S(1)} %add_select_fusion, bf16[4,15,15]{2,0,1:T(4,128)(2,1)} %param.7), kind=kOutput, calls=%fused_computation.5 | convolution fusion | flops 59473920 | bytes 4065032 | tf_op jit(solution)/shard_map/gab,jtb->gajt/dot_general | solution.py:31
  9.8 0.5 select_convert_fusion.edge_ref
  10.3 0.0 copy-start.1
  10.3 4.5 %copy.24 = bf16[256,128,4,15]{1,0,3,2:T(8,128)(2,1)} copy(bf16[256,128,4,15]{1,3,2,0:T(8,128)(2,1)S(1)} %fusion.3) | data formatting | bytes 7864320 | tf_op jit(solution)/shard_map/gab,jtb->gajt/dot_general | solution.py:31
  14.9 0.0 collective-permute-done
  14.9 0.0 collective-permute-done.1
  14.9 0.1 broadcast_in_dim.42
  15.1 0.0 copy-done.1
  15.1 1.3 %concatenate.3.ext_ref = bf16[4,256,256]{2,1,0:T(8,128)(2,1)} concatenate(bf16[4,256,128]{2,1,0:T(8,128)(2,1)S(1)} %bitcast.25, bf16[4,256,14]{2,1,0:T(8,128)(2,1)S(1)} %collective-permute-done, bf16[4,256,18]{2,1,0:T(8,128)(2,1)S(1)} %broadcast_in_dim.22, bf16[4,256,1]{2,1,0:T(8,128)(2,1)S(1)} %broadcast_in_dim.42, bf16[4,256,81]{2,1,0:T(8,128)(2,1)S(1)} %broadcast_in_dim.43, ...), dimensions={2} | concatenate | bytes 1048576 | tf_op jit(solution)/shard_map/concatenate | solution.py:147
  16.4 8.3 %shard_map.64 = bf16[256,640]{1,0:T(8,128)(2,1)} custom-call(s32[1,256]{1,0:T(1,128)} %bitcast.26, f32[1,128]{1,0:T(1,128)} %select_convert_fusion.edge_ref, bf16[4,256,256]{2,1,0:T(8,128)(2,1)} %concatenate.3.ext_ref, bf16[4,15,256,128]{3,2,1,0:T(8,128)(2,1)} %bitcast.22), custom_call_target="tpu_custom_call" | custom-call | tf_op jit(solution)/shard_map/pallas_call | solution.py:108
  24.8 1.8 %reshape.100 = bf16[128,2,640]{2,1,0:T(2,128)(2,1)} reshape(bf16[256,640]{1,0:T(8,128)(2,1)} %shard_map.64) | data formatting | bytes 655360 | tf_op jit(solution)/shard_map/reshape | solution.py:153
  26.6 0.0 copy-start.2
  26.6 18.5 %all-to-all-start = ((bf16[128,2,640]{2,1,0:T(2,128)(2,1)}), bf16[128,2,640]{2,1,0:T(2,128)(2,1)S(1)}, u32[]{:S(2)}, u32[]{:S(2)}) async-start(bf16[128,2,640]{2,1,0:T(2,128)(2,1)} %reshape.100), calls=%async_computation | async-start | bytes 655360 | tf_op jit(solution)/shard_map/all_to_all | solution.py:154
  45.1 0.0 copy-done
  45.1 0.6 fusion.1
  45.8 1.2 %copy.25 = bf16[256,128,15]{1,0,2:T(8,128)(2,1)} copy(bf16[256,128,15]{1,2,0:T(8,128)(2,1)S(1)} %fusion.1) | data formatting | bytes 1966080 | tf_op jit(solution)/shard_map/gab,jtb->gajt/dot_general | solution.py:31
  47.0 0.0 copy-done.2
  47.0 0.1 iota_add_fusion
  47.1 0.7 %add.51.target_ref = s32[1,256]{1,0:T(1,128)} reshape(s32[128,2]{1,0:T(8,128)S(1)} %iota_add_fusion) | data formatting | bytes 2048 | tf_op jit(solution)/shard_map/add | solution.py:157
  47.8 13.9 %all-to-all-done = bf16[128,2,640]{2,1,0:T(2,128)(2,1)S(1)} async-done(((bf16[128,2,640]{2,1,0:T(2,128)(2,1)}), bf16[128,2,640]{2,1,0:T(2,128)(2,1)S(1)}, u32[]{:S(2)}, u32[]{:S(2)}) %all-to-all-start) | async-done | bytes 327712 | tf_op jit(solution)/shard_map/all_to_all | solution.py:154
  61.7 0.8 %reshape.101.data_ref = bf16[256,640]{1,0:T(8,128)(2,1)} reshape(bf16[128,2,640]{2,1,0:T(2,128)(2,1)S(1)} %all-to-all-done) | data formatting | bytes 655360 | tf_op jit(solution)/shard_map/reshape | solution.py:155
  62.5 5.5 %shard_map.65 = bf16[1024,128]{1,0:T(8,128)(2,1)} custom-call(s32[1,256]{1,0:T(1,128)} %add.51.target_ref, bf16[256,640]{1,0:T(8,128)(2,1)} %reshape.101.data_ref, bf16[1,15,256,128]{3,2,1,0:T(8,128)(2,1)} %bitcast.23), custom_call_target="tpu_custom_call" | custom-call | tf_op jit(solution)/shard_map/pallas_call | solution.py:127
  (3 shorter events, 0.1 us)
Async XLA Ops:
  0.0 45.1 %copy-start = (bf16[15,15]{1,0:T(8,128)(2,1)S(1)}, bf16[15,15]{1,0:T(8,128)(2,1)}, u32[]{:S(2)}) copy-start(bf16[15,15]{1,0:T(8,128)(2,1)} %param.8) | copy-start | bytes 1354
  1.2 13.7 %collective-permute-start = (bf16[4,256,14]{2,1,0:T(8,128)(2,1)S(1)}, bf16[4,256,14]{2,1,0:T(8,128)(2,1)S(1)}, u32[]{:S(2)}, u32[]{:S(2)}) collective-permute-start(bf16[4,256,14]{2,1,0:T(8,128)(2,1)S(1)} %get-tuple-element.6), channel_id=1, source_target_pairs={{1,0},{2,1},{3,2},{5,4},{6,5},{7,6},{9,8},{10,9},{11,10},{13,12},{... | collective-permute-start | bytes 86024 | tf_op jit(solution)/shard_map/ppermute | solution.py:20
  2.5 12.4 %collective-permute-start.1 = (bf16[4,256,14]{2,1,0:T(8,128)(2,1)S(1)}, bf16[4,256,14]{2,1,0:T(8,128)(2,1)S(1)}, u32[]{:S(2)}, u32[]{:S(2)}) collective-permute-start(bf16[4,256,14]{2,1,0:T(8,128)(2,1)S(1)} %get-tuple-element.5), channel_id=1, source_target_pairs={{0,1},{1,2},{2,3},{4,5},{5,6},{6,7},{8,9},{9,10},{10,11},{12,13},{... | collective-permute-start | bytes 86024 | tf_op jit(solution)/shard_map/ppermute | solution.py:19
  10.3 4.7 %copy-start.1 = (bf16[1,4,256,128]{3,2,1,0:T(8,128)(2,1)S(1)}, bf16[1,4,256,128]{3,2,1,0:T(8,128)(2,1)}, u32[]{:S(2)}) copy-start(bf16[1,4,256,128]{3,2,1,0:T(8,128)(2,1)} %param.6) | copy-start | bytes 786436
  26.6 20.4 %copy-start.2 = (s32[128]{0:T(128)S(1)}, s32[128]{0:T(128)}, u32[]{:S(2)}) copy-start(s32[128]{0:T(128)} %param.11) | copy-start | bytes 1540
  26.6 35.1 %all-to-all-start = ((bf16[128,2,640]{2,1,0:T(2,128)(2,1)}), bf16[128,2,640]{2,1,0:T(2,128)(2,1)S(1)}, u32[]{:S(2)}, u32[]{:S(2)}) async-start(bf16[128,2,640]{2,1,0:T(2,128)(2,1)} %reshape.100), calls=%async_computation | async-start | bytes 655360 | tf_op jit(solution)/shard_map/all_to_all | solution.py:154

commit v7 on v6

--- a/solution.py
+++ b/solution.py
@@ -32,16 +32,19 @@
     return tables.astype(jnp.bfloat16)
 
 
-def fan_kernel(place_ref, edge_ref, ext_ref, table_ref, out_ref, scr_ref, halo_ref, *, taps, live_col, comps):
+def fan_kernel(place_ref, edge_ref, live_ref, block_ref, prev_ref, next_ref, table_ref, out_ref, scr_ref, halo_ref, *, taps, comps):
     c = pl.program_id(0)
-    rows = ext_ref.shape[1]
+    rows = block_ref.shape[1]
     samples = LANES
     reach = (taps - 1) // 2
+    wide = 2 * reach
     place = place_ref[...]
     select = (lax.broadcasted_iota(jnp.int32, (rows, rows), 0) == place).astype(jnp.bfloat16)
-    ordered = jnp.dot(select, ext_ref[0], preferred_element_type=jnp.float32)
-    keep = ordered[:, live_col:live_col + 1]
-    ordered = ordered.astype(jnp.bfloat16)
+    keep = jnp.sum(select.astype(jnp.float32) * live_ref[...].astype(jnp.float32), axis=1, keepdims=True)
+    lane = lax.broadcasted_iota(jnp.int32, (rows, LANES), 1)
+    outer = jnp.where(lane < wide, next_ref[0], jnp.where(lane >= LANES - wide, prev_ref[0], jnp.zeros_like(prev_ref[0])))
+    ext = jnp.concatenate([block_ref[0], outer], axis=1)
+    ordered = jnp.dot(select, ext, preferred_element_type=jnp.float32).astype(jnp.bfloat16)
     swapped = jnp.concatenate([ordered[:, samples:], ordered[:, :samples]], axis=1)
     second = rows + 16
     zeros = jnp.zeros((8, LANES), jnp.float32)
@@ -57,7 +60,6 @@
         acc = acc + scr_ref[pl.ds(a + 8 - reach, rows), :]
         acc_h = acc_h + scr_ref[pl.ds(second + a - reach, rows), :]
     out_ref[:, pl.ds(pl.multiple_of(c * samples, samples), samples)] = (acc * keep).astype(out_ref.dtype)
-    lane = lax.broadcasted_iota(jnp.int32, (rows, LANES), 1)
     for k in range(comps):
         @pl.when(c == k)
         def _():
@@ -101,23 +103,27 @@
     out_ref[...] = acc.astype(out_ref.dtype)
 
 
-def fan_call(place, edge, ext, tables, live_col):
-    comps, rows, _ = ext.shape
+def fan_call(place, edge, live, block, prev, nxt, tables):
+    comps, rows, samples = block.shape
     taps = tables.shape[1]
-    kernel = functools.partial(fan_kernel, taps=taps, live_col=live_col, comps=comps)
+    kernel = functools.partial(fan_kernel, taps=taps, comps=comps)
+    part = pl.BlockSpec((1, rows, samples), lambda c: (c, 0, 0))
     return pl.pallas_call(
         kernel,
         grid=(comps,),
         in_specs=[
             pl.BlockSpec((1, rows), lambda c: (0, 0)),
             pl.BlockSpec((1, LANES), lambda c: (0, 0)),
-            pl.BlockSpec((1, rows, EXT), lambda c: (c, 0, 0)),
+            pl.BlockSpec((1, rows), lambda c: (0, 0)),
+            part,
+            part,
+            part,
             pl.BlockSpec((1, taps, EXT, LANES), lambda c: (c, 0, 0, 0)),
         ],
         out_specs=pl.BlockSpec((rows, (comps + 1) * LANES), lambda c: (0, 0)),
         out_shape=jax.ShapeDtypeStruct((rows, (comps + 1) * LANES), jnp.bfloat16),
         scratch_shapes=[pltpu.VMEM((2 * rows + 24, LANES), jnp.float32), pltpu.VMEM((rows, LANES), jnp.float32)],
-    )(place, edge, ext, tables)
+    )(place, edge, live, block, prev, nxt, tables)
 
 
 def dip_call(target, data, tables, group, comps):
@@ -139,16 +145,15 @@
     group = nodes // devices
 
     block = records[0]
-    low, high = time_halo(block, "tm", wide)
-    live_col = samples + 32
-    live = jnp.broadcast_to(live_mask[0].astype(jnp.bfloat16)[None, :, None], (comps, nodes, 1))
-    gap1 = jnp.zeros((comps, nodes, live_col - samples - wide), jnp.bfloat16)
-    gap2 = jnp.zeros((comps, nodes, EXT - wide - live_col - 1), jnp.bfloat16)
-    ext = jnp.concatenate([block, high, gap1, live, gap2, low], axis=-1)
+    count = lax.axis_size("tm")
+    forward = [(i, i + 1) for i in range(count - 1)]
+    backward = [(target, source) for source, target in forward]
+    prev = lax.ppermute(block, "tm", forward)
+    nxt = lax.ppermute(block, "tm", backward)
     place = lax.axis_index("tm")
     lane = jnp.arange(LANES, dtype=jnp.int32) % wide
-    edge = jnp.where(lane < reach, place > 0, place < lax.axis_size("tm") - 1).astype(jnp.float32)[None, :]
-    packed = fan_call(node_place[None, :], edge, ext, circulant(fan_taps, samples), live_col)
+    edge = jnp.where(lane < reach, place > 0, place < count - 1).astype(jnp.float32)[None, :]
+    packed = fan_call(node_place[None, :], edge, live_mask, block, prev, nxt, circulant(fan_taps, samples))
 
     sent = packed.reshape(devices, group, packed.shape[-1])
     arrived = lax.all_to_all(sent, "shot", split_axis=0, concat_axis=0, tiled=True)

time: 68.4 us -> 69.3 us (1.013)
  matrix products: 2.58 us -> 4.52 us
  starting transfers between devices: 24.4 us -> 23.4 us
    dot_general x2, local copies, waits for them, and re-layouts: 5.75 us -> 7.94 us  [circulant(): jnp.einsum('gab,jtb->gajt', tap_set, onehot, preferred_element_type=jnp.f...]
    dot_general x2, matrix products: 2.58 us -> 4.52 us  [circulant(): jnp.einsum('gab,jtb->gajt', tap_set, onehot, preferred_element_type=jnp.f...]
    concatenate x1 -> x0, local copies, waits for them, and re-layouts: 1.34 us -> none  [on_device(): ext = jnp.concatenate([block, high, gap1, live, gap2, low], axis=-1)]
    slice x1 -> x0, local copies, waits for them, and re-layouts: 1.18 us -> none  [time_halo(): lax.slice_in_dim(block, samples - width, None, axis=-1)]
    unnamed x6 -> x8, local copies, waits for them, and re-layouts: 0.01 us -> 0.78 us
  transfers between devices with their start and end apart: 3 -> 3, of which waited for: 1 -> 1; matrix products, arithmetic and copies ran while one was open for 15% -> 20% of each run, Pallas kernels for 0% -> 0%
where the time goes in v7:
time: 69.3 us; the launch traced here: 68.5 us
  starting transfers between devices  23.4 us (34%)
  waiting for transfers between devices  13.9 us (20%)
  Pallas kernels  13.9 us (20%)
  local copies, waits for them, and re-layouts  12.1 us (17%)
  matrix products  4.52 us (7%)
    all_to_all x1, starting transfers between devices, on_device(): lax.all_to_all(sent, 'shot', split_axis=0, concat_axis=0, tiled=True)  18 us
    all_to_all x1, waiting for transfers between devices, on_device(): lax.all_to_all(sent, 'shot', split_axis=0, concat_axis=0, tiled=True)  13.9 us
    pallas_call x1, Pallas kernels, fan_call(): pl.pallas_call(kernel, grid=(comps,), in_specs=[pl.BlockSpec((1, rows), l...  8.38 us
    dot_general x2, local copies, waits for them, and re-layouts, circulant(): jnp.einsum('gab,jtb->gajt', tap_set, onehot, preferred_element_type=jnp.f...  7.94 us
    pallas_call x1, Pallas kernels, dip_call(): pl.pallas_call(kernel, out_shape=jax.ShapeDtypeStruct((rows * comps, LANE...  5.49 us
    dot_general x2, matrix products, circulant(): jnp.einsum('gab,jtb->gajt', tap_set, onehot, preferred_element_type=jnp.f...  4.52 us
    ppermute x1, starting transfers between devices, on_device(): prev = lax.ppermute(block, 'tm', forward)  4.08 us
    reshape x1, local copies, waits for them, and re-layouts, on_device(): sent = packed.reshape(devices, group, packed.shape[-1])  1.81 us
  transfers between devices with their start and end apart: 3, of which 1 were waited for; matrix products, arithmetic and copies ran while one was open for 20% of the time, Pallas kernels for 0%

profile of v7, /device:TPU:1, one launch (start us, length us, event | category | flops | bytes accessed | tf_op | source)
XLA Modules:
  0.0 68.5 jit_solution(16642407414379907142)
XLA Ops:
  0.0 0.0 copy-start
  0.0 4.1 %collective-permute-start = (bf16[4,256,128]{2,1,0:T(8,128)(2,1)}, bf16[4,256,128]{2,1,0:T(8,128)(2,1)S(1)}, u32[]{:S(2)}, u32[]{:S(2)}) collective-permute-start(bf16[4,256,128]{2,1,0:T(8,128)(2,1)} %bitcast.24), channel_id=1, source_target_pairs={{0,1},{1,2},{2,3},{4,5},{5,6},{6,7},{8,9},{9,10},{10,11},{12,13},{... | collective-permute-start | bytes 786440 | tf_op jit(solution)/shard_map/ppermute | solution.py:151
  4.1 1.3 %collective-permute-start.1 = (bf16[4,256,128]{2,1,0:T(8,128)(2,1)}, bf16[4,256,128]{2,1,0:T(8,128)(2,1)S(1)}, u32[]{:S(2)}, u32[]{:S(2)}) collective-permute-start(bf16[4,256,128]{2,1,0:T(8,128)(2,1)} %bitcast.25), channel_id=1, source_target_pairs={{1,0},{2,1},{3,2},{5,4},{6,5},{7,6},{9,8},{10,9},{11,10},{13,12},{... | collective-permute-start | bytes 786440 | tf_op jit(solution)/shard_map/ppermute | solution.py:152
  5.4 0.1 add_select_fusion
  5.5 3.9 %fusion.3 = bf16[256,128,4,15]{1,3,2,0:T(8,128)(2,1)} fusion(s32[256,128]{1,0:T(8,128)S(1)} %add_select_fusion, bf16[4,15,15]{2,0,1:T(4,128)(2,1)} %param.7), kind=kOutput, calls=%fused_computation.5 | convolution fusion | flops 59473920 | bytes 4065032 | tf_op jit(solution)/shard_map/gab,jtb->gajt/dot_general | solution.py:31
  9.4 6.7 %copy.24 = bf16[256,128,4,15]{1,0,3,2:T(8,128)(2,1)} copy(bf16[256,128,4,15]{1,3,2,0:T(8,128)(2,1)} %fusion.3) | data formatting | bytes 7864320 | tf_op jit(solution)/shard_map/gab,jtb->gajt/dot_general | solution.py:31
  16.1 0.6 select_convert_fusion.edge_ref
  16.6 0.0 collective-permute-done.prev_ref
  16.6 0.0 copy-start.1
  16.6 0.0 collective-permute-done.1.next_ref
  16.6 0.0 copy-start.2
  16.7 0.7 copy-done.1
  17.3 0.1 copy-done.2
  17.4 8.4 %shard_map.64 = bf16[256,640]{1,0:T(8,128)(2,1)} custom-call(s32[1,256]{1,0:T(1,128)} %bitcast.27, f32[1,128]{1,0:T(1,128)} %select_convert_fusion.edge_ref, s32[1,256]{1,0:T(1,128)} %live_ref.1, bf16[4,256,128]{2,1,0:T(8,128)(2,1)} %bitcast.26, bf16[4,256,128]{2,1,0:T(8,128)(2,1)} %copy-done.1, bf16[4,256,128]{2,1,0:T(8,128)(2,1)} %copy-done.2, ...), custom_call_target="tpu_custom_call" | custom-call | tf_op jit(solution)/shard_map/pallas_call | solution.py:111
  25.8 1.8 %reshape.92 = bf16[128,2,640]{2,1,0:T(2,128)(2,1)} reshape(bf16[256,640]{1,0:T(8,128)(2,1)} %shard_map.64) | data formatting | bytes 655360 | tf_op jit(solution)/shard_map/reshape | solution.py:158
  27.6 0.0 copy-start.3
  27.6 18.0 %all-to-all-start = ((bf16[128,2,640]{2,1,0:T(2,128)(2,1)}), bf16[128,2,640]{2,1,0:T(2,128)(2,1)S(1)}, u32[]{:S(2)}, u32[]{:S(2)}) async-start(bf16[128,2,640]{2,1,0:T(2,128)(2,1)} %reshape.92), calls=%async_computation | async-start | bytes 655360 | tf_op jit(solution)/shard_map/all_to_all | solution.py:159
  45.6 0.0 copy-done
  45.6 0.6 fusion.1
  46.3 1.2 %copy.25 = bf16[256,128,15]{1,0,2:T(8,128)(2,1)} copy(bf16[256,128,15]{1,2,0:T(8,128)(2,1)S(1)} %fusion.1) | data formatting | bytes 1966080 | tf_op jit(solution)/shard_map/gab,jtb->gajt/dot_general | solution.py:31
  47.5 0.0 copy-done.3
  47.5 0.1 iota_add_fusion
  47.6 0.7 %add.51.target_ref = s32[1,256]{1,0:T(1,128)} reshape(s32[128,2]{1,0:T(8,128)S(1)} %iota_add_fusion) | data formatting | bytes 2048 | tf_op jit(solution)/shard_map/add | solution.py:162
  48.3 13.9 %all-to-all-done = bf16[128,2,640]{2,1,0:T(2,128)(2,1)S(1)} async-done(((bf16[128,2,640]{2,1,0:T(2,128)(2,1)}), bf16[128,2,640]{2,1,0:T(2,128)(2,1)S(1)}, u32[]{:S(2)}, u32[]{:S(2)}) %all-to-all-start) | async-done | bytes 327712 | tf_op jit(solution)/shard_map/all_to_all | solution.py:159
  62.2 0.8 %reshape.93.data_ref = bf16[256,640]{1,0:T(8,128)(2,1)} reshape(bf16[128,2,640]{2,1,0:T(2,128)(2,1)S(1)} %all-to-all-done) | data formatting | bytes 655360 | tf_op jit(solution)/shard_map/reshape | solution.py:160
  63.1 5.5 %shard_map.65 = bf16[1024,128]{1,0:T(8,128)(2,1)} custom-call(s32[1,256]{1,0:T(1,128)} %add.51.target_ref, bf16[256,640]{1,0:T(8,128)(2,1)} %reshape.93.data_ref, bf16[1,15,256,128]{3,2,1,0:T(8,128)(2,1)} %bitcast.23), custom_call_target="tpu_custom_call" | custom-call | tf_op jit(solution)/shard_map/pallas_call | solution.py:133
  (1 shorter events, 0.0 us)
Async XLA Ops:
  0.0 45.6 %copy-start = (bf16[15,15]{1,0:T(8,128)(2,1)S(1)}, bf16[15,15]{1,0:T(8,128)(2,1)}, u32[]{:S(2)}) copy-start(bf16[15,15]{1,0:T(8,128)(2,1)} %param.8) | copy-start | bytes 1354
  0.0 16.6 %collective-permute-start = (bf16[4,256,128]{2,1,0:T(8,128)(2,1)}, bf16[4,256,128]{2,1,0:T(8,128)(2,1)S(1)}, u32[]{:S(2)}, u32[]{:S(2)}) collective-permute-start(bf16[4,256,128]{2,1,0:T(8,128)(2,1)} %bitcast.24), channel_id=1, source_target_pairs={{0,1},{1,2},{2,3},{4,5},{5,6},{6,7},{8,9},{9,10},{10,11},{12,13},{... | collective-permute-start | bytes 786440 | tf_op jit(solution)/shard_map/ppermute | solution.py:151
  4.1 12.6 %collective-permute-start.1 = (bf16[4,256,128]{2,1,0:T(8,128)(2,1)}, bf16[4,256,128]{2,1,0:T(8,128)(2,1)S(1)}, u32[]{:S(2)}, u32[]{:S(2)}) collective-permute-start(bf16[4,256,128]{2,1,0:T(8,128)(2,1)} %bitcast.25), channel_id=1, source_target_pairs={{1,0},{2,1},{3,2},{5,4},{6,5},{7,6},{9,8},{10,9},{11,10},{13,12},{... | collective-permute-start | bytes 786440 | tf_op jit(solution)/shard_map/ppermute | solution.py:152
  16.6 0.7 %copy-start.1 = (bf16[4,256,128]{2,1,0:T(8,128)(2,1)}, bf16[4,256,128]{2,1,0:T(8,128)(2,1)S(1)}, u32[]{:S(2)}) copy-start(bf16[4,256,128]{2,1,0:T(8,128)(2,1)S(1)} %collective-permute-done.prev_ref) | copy-start | bytes 786436
  16.6 0.8 %copy-start.2 = (bf16[4,256,128]{2,1,0:T(8,128)(2,1)}, bf16[4,256,128]{2,1,0:T(8,128)(2,1)S(1)}, u32[]{:S(2)}) copy-start(bf16[4,256,128]{2,1,0:T(8,128)(2,1)S(1)} %collective-permute-done.1.next_ref) | copy-start | bytes 786436
  27.6 19.9 %copy-start.3 = (s32[128]{0:T(128)S(1)}, s32[128]{0:T(128)}, u32[]{:S(2)}) copy-start(s32[128]{0:T(128)} %param.11) | copy-start | bytes 1540
  27.6 34.6 %all-to-all-start = ((bf16[128,2,640]{2,1,0:T(2,128)(2,1)}), bf16[128,2,640]{2,1,0:T(2,128)(2,1)S(1)}, u32[]{:S(2)}, u32[]{:S(2)}) async-start(bf16[128,2,640]{2,1,0:T(2,128)(2,1)} %reshape.92), calls=%async_computation | async-start | bytes 655360 | tf_op jit(solution)/shard_map/all_to_all | solution.py:159

commit v8 on v6

--- a/solution.py
+++ b/solution.py
@@ -41,21 +41,18 @@
     select = (lax.broadcasted_iota(jnp.int32, (rows, rows), 0) == place).astype(jnp.bfloat16)
     ordered = jnp.dot(select, ext_ref[0], preferred_element_type=jnp.float32)
     keep = ordered[:, live_col:live_col + 1]
-    ordered = ordered.astype(jnp.bfloat16)
-    swapped = jnp.concatenate([ordered[:, samples:], ordered[:, :samples]], axis=1)
-    second = rows + 16
-    zeros = jnp.zeros((8, LANES), jnp.float32)
+    zeros = jnp.zeros((8, EXT), jnp.float32)
     scr_ref[0:8, :] = zeros
     scr_ref[rows + 8:rows + 16, :] = zeros
-    scr_ref[second + rows:second + rows + 8, :] = zeros
+    scr_ref[8:rows + 8, :] = ordered
     acc = jnp.zeros((rows, LANES), jnp.float32)
     acc_h = jnp.zeros((rows, LANES), jnp.float32)
     for a in range(taps):
         table = table_ref[0, a]
-        scr_ref[8:rows + 8, :] = jnp.dot(ordered, table, preferred_element_type=jnp.float32)
-        scr_ref[second:second + rows, :] = jnp.dot(swapped, table, preferred_element_type=jnp.float32)
-        acc = acc + scr_ref[pl.ds(a + 8 - reach, rows), :]
-        acc_h = acc_h + scr_ref[pl.ds(second + a - reach, rows), :]
+        moved = scr_ref[pl.ds(a + 8 - reach, rows), :].astype(jnp.bfloat16)
+        swapped = jnp.concatenate([moved[:, samples:], moved[:, :samples]], axis=1)
+        acc = acc + jnp.dot(moved, table, preferred_element_type=jnp.float32)
+        acc_h = acc_h + jnp.dot(swapped, table, preferred_element_type=jnp.float32)
     out_ref[:, pl.ds(pl.multiple_of(c * samples, samples), samples)] = (acc * keep).astype(out_ref.dtype)
     lane = lax.broadcasted_iota(jnp.int32, (rows, LANES), 1)
     for k in range(comps):
@@ -116,7 +113,7 @@
         ],
         out_specs=pl.BlockSpec((rows, (comps + 1) * LANES), lambda c: (0, 0)),
         out_shape=jax.ShapeDtypeStruct((rows, (comps + 1) * LANES), jnp.bfloat16),
-        scratch_shapes=[pltpu.VMEM((2 * rows + 24, LANES), jnp.float32), pltpu.VMEM((rows, LANES), jnp.float32)],
+        scratch_shapes=[pltpu.VMEM((rows + 16, EXT), jnp.float32), pltpu.VMEM((rows, LANES), jnp.float32)],
     )(place, edge, ext, tables)
 
 

time: 68.4 us -> 68.1 us (level)
  no operation moved by 1% of the time
where the time goes in v8:
time: 68.1 us; the launch traced here: 67.8 us
  starting transfers between devices  24.4 us (36%)
  waiting for transfers between devices  13.9 us (20%)
  Pallas kernels  13.6 us (20%)
  local copies, waits for them, and re-layouts  11.8 us (17%)
  matrix products  2.58 us (4%)
  other arithmetic  1.37 us (2%)
    all_to_all x1, starting transfers between devices, on_device(): lax.all_to_all(sent, 'shot', split_axis=0, concat_axis=0, tiled=True)  18.5 us
    all_to_all x1, waiting for transfers between devices, on_device(): lax.all_to_all(sent, 'shot', split_axis=0, concat_axis=0, tiled=True)  13.9 us
    pallas_call x1, Pallas kernels, fan_call(): pl.pallas_call(kernel, grid=(comps,), in_specs=[pl.BlockSpec((1, rows), l...  8.09 us
    dot_general x2, local copies, waits for them, and re-layouts, circulant(): jnp.einsum('gab,jtb->gajt', tap_set, onehot, preferred_element_type=jnp.f...  5.75 us
    pallas_call x1, Pallas kernels, dip_call(): pl.pallas_call(kernel, out_shape=jax.ShapeDtypeStruct((rows * comps, LANE...  5.49 us
    ppermute x1, starting transfers between devices, time_halo(): lax.ppermute(lax.slice_in_dim(block, samples - width, None, axis=-1), axi...  4.59 us
    dot_general x2, matrix products, circulant(): jnp.einsum('gab,jtb->gajt', tap_set, onehot, preferred_element_type=jnp.f...  2.58 us
    reshape x1, local copies, waits for them, and re-layouts, on_device(): sent = packed.reshape(devices, group, packed.shape[-1])  1.81 us
  transfers between devices with their start and end apart: 3, of which 1 were waited for; matrix products, arithmetic and copies ran while one was open for 15% of the time, Pallas kernels for 0%

profile of v8, /device:TPU:1, one launch (start us, length us, event | category | flops | bytes accessed | tf_op | source)
XLA Modules:
  0.0 67.8 jit_solution(15962857429158155743)
XLA Ops:
  0.0 0.0 copy-start
  0.0 1.2 %fusion.12 = (bf16[4,256,14]{2,1,0:T(8,128)(2,1)S(1)}, bf16[4,256,14]{2,1,0:T(8,128)(2,1)S(1)}) fusion(bf16[4,256,128]{2,1,0:T(8,128)(2,1)} %bitcast.24), kind=kLoop, calls=%fused_computation.22 | loop fusion | bytes 114688 | tf_op jit(solution)/shard_map/slice | solution.py:19
  1.2 1.3 %collective-permute-start = (bf16[4,256,14]{2,1,0:T(8,128)(2,1)S(1)}, bf16[4,256,14]{2,1,0:T(8,128)(2,1)S(1)}, u32[]{:S(2)}, u32[]{:S(2)}) collective-permute-start(bf16[4,256,14]{2,1,0:T(8,128)(2,1)S(1)} %get-tuple-element.6), channel_id=1, source_target_pairs={{1,0},{2,1},{3,2},{5,4},{6,5},{7,6},{9,8},{10,9},{11,10},{13,12},{... | collective-permute-start | bytes 86024 | tf_op jit(solution)/shard_map/ppermute | solution.py:20
  2.5 4.6 %collective-permute-start.1 = (bf16[4,256,14]{2,1,0:T(8,128)(2,1)S(1)}, bf16[4,256,14]{2,1,0:T(8,128)(2,1)S(1)}, u32[]{:S(2)}, u32[]{:S(2)}) collective-permute-start(bf16[4,256,14]{2,1,0:T(8,128)(2,1)S(1)} %get-tuple-element.5), channel_id=1, source_target_pairs={{0,1},{1,2},{2,3},{4,5},{5,6},{6,7},{8,9},{9,10},{10,11},{12,13},{... | collective-permute-start | bytes 86024 | tf_op jit(solution)/shard_map/ppermute | solution.py:19
  7.1 0.1 add_select_fusion
  7.1 0.7 %convert_reduce_fusion = bf16[256]{0:T(256)(128)(2,1)S(1)} fusion(s32[1,256]{1,0:T(1,128)} %param.9), kind=kLoop, calls=%fused_computation.20 | loop fusion | flops 256 | bytes 1536 | tf_op jit(solution)/shard_map/convert_element_type | solution.py:141
  7.8 2.0 %fusion.3 = bf16[256,128,4,15]{1,3,2,0:T(8,128)(2,1)S(1)} fusion(s32[256,128]{1,0:T(8,128)S(1)} %add_select_fusion, bf16[4,15,15]{2,0,1:T(4,128)(2,1)} %param.7), kind=kOutput, calls=%fused_computation.5 | convolution fusion | flops 59473920 | bytes 4065032 | tf_op jit(solution)/shard_map/gab,jtb->gajt/dot_general | solution.py:31
  9.8 0.5 select_convert_fusion.edge_ref
  10.3 0.0 copy-start.1
  10.3 4.5 %copy.24 = bf16[256,128,4,15]{1,0,3,2:T(8,128)(2,1)} copy(bf16[256,128,4,15]{1,3,2,0:T(8,128)(2,1)S(1)} %fusion.3) | data formatting | bytes 7864320 | tf_op jit(solution)/shard_map/gab,jtb->gajt/dot_general | solution.py:31
  14.9 0.0 collective-permute-done
  14.9 0.0 collective-permute-done.1
  14.9 0.1 broadcast_in_dim.42
  15.1 0.0 copy-done.1
  15.1 1.3 %concatenate.3.ext_ref = bf16[4,256,256]{2,1,0:T(8,128)(2,1)} concatenate(bf16[4,256,128]{2,1,0:T(8,128)(2,1)S(1)} %bitcast.25, bf16[4,256,14]{2,1,0:T(8,128)(2,1)S(1)} %collective-permute-done, bf16[4,256,18]{2,1,0:T(8,128)(2,1)S(1)} %broadcast_in_dim.22, bf16[4,256,1]{2,1,0:T(8,128)(2,1)S(1)} %broadcast_in_dim.42, bf16[4,256,81]{2,1,0:T(8,128)(2,1)S(1)} %broadcast_in_dim.43, ...), dimensions={2} | concatenate | bytes 1048576 | tf_op jit(solution)/shard_map/concatenate | solution.py:144
  16.4 8.1 %shard_map.64 = bf16[256,640]{1,0:T(8,128)(2,1)} custom-call(s32[1,256]{1,0:T(1,128)} %bitcast.26, f32[1,128]{1,0:T(1,128)} %select_convert_fusion.edge_ref, bf16[4,256,256]{2,1,0:T(8,128)(2,1)} %concatenate.3.ext_ref, bf16[4,15,256,128]{3,2,1,0:T(8,128)(2,1)} %bitcast.22), custom_call_target="tpu_custom_call" | custom-call | tf_op jit(solution)/shard_map/pallas_call | solution.py:105
  24.5 1.8 %reshape.100 = bf16[128,2,640]{2,1,0:T(2,128)(2,1)} reshape(bf16[256,640]{1,0:T(8,128)(2,1)} %shard_map.64) | data formatting | bytes 655360 | tf_op jit(solution)/shard_map/reshape | solution.py:150
  26.3 0.0 copy-start.2
  26.3 18.5 %all-to-all-start = ((bf16[128,2,640]{2,1,0:T(2,128)(2,1)}), bf16[128,2,640]{2,1,0:T(2,128)(2,1)S(1)}, u32[]{:S(2)}, u32[]{:S(2)}) async-start(bf16[128,2,640]{2,1,0:T(2,128)(2,1)} %reshape.100), calls=%async_computation | async-start | bytes 655360 | tf_op jit(solution)/shard_map/all_to_all | solution.py:151
  44.9 0.0 copy-done
  44.9 0.6 fusion.1
  45.5 1.2 %copy.25 = bf16[256,128,15]{1,0,2:T(8,128)(2,1)} copy(bf16[256,128,15]{1,2,0:T(8,128)(2,1)S(1)} %fusion.1) | data formatting | bytes 1966080 | tf_op jit(solution)/shard_map/gab,jtb->gajt/dot_general | solution.py:31
  46.7 0.0 copy-done.2
  46.7 0.1 iota_add_fusion
  46.8 0.7 %add.51.target_ref = s32[1,256]{1,0:T(1,128)} reshape(s32[128,2]{1,0:T(8,128)S(1)} %iota_add_fusion) | data formatting | bytes 2048 | tf_op jit(solution)/shard_map/add | solution.py:154
  47.6 13.9 %all-to-all-done = bf16[128,2,640]{2,1,0:T(2,128)(2,1)S(1)} async-done(((bf16[128,2,640]{2,1,0:T(2,128)(2,1)}), bf16[128,2,640]{2,1,0:T(2,128)(2,1)S(1)}, u32[]{:S(2)}, u32[]{:S(2)}) %all-to-all-start) | async-done | bytes 327712 | tf_op jit(solution)/shard_map/all_to_all | solution.py:151
  61.4 0.8 %reshape.101.data_ref = bf16[256,640]{1,0:T(8,128)(2,1)} reshape(bf16[128,2,640]{2,1,0:T(2,128)(2,1)S(1)} %all-to-all-done) | data formatting | bytes 655360 | tf_op jit(solution)/shard_map/reshape | solution.py:152
  62.3 5.5 %shard_map.65 = bf16[1024,128]{1,0:T(8,128)(2,1)} custom-call(s32[1,256]{1,0:T(1,128)} %add.51.target_ref, bf16[256,640]{1,0:T(8,128)(2,1)} %reshape.101.data_ref, bf16[1,15,256,128]{3,2,1,0:T(8,128)(2,1)} %bitcast.23), custom_call_target="tpu_custom_call" | custom-call | tf_op jit(solution)/shard_map/pallas_call | solution.py:124
  (3 shorter events, 0.1 us)
Async XLA Ops:
  0.0 44.9 %copy-start = (bf16[15,15]{1,0:T(8,128)(2,1)S(1)}, bf16[15,15]{1,0:T(8,128)(2,1)}, u32[]{:S(2)}) copy-start(bf16[15,15]{1,0:T(8,128)(2,1)} %param.8) | copy-start | bytes 1354
  1.2 13.7 %collective-permute-start = (bf16[4,256,14]{2,1,0:T(8,128)(2,1)S(1)}, bf16[4,256,14]{2,1,0:T(8,128)(2,1)S(1)}, u32[]{:S(2)}, u32[]{:S(2)}) collective-permute-start(bf16[4,256,14]{2,1,0:T(8,128)(2,1)S(1)} %get-tuple-element.6), channel_id=1, source_target_pairs={{1,0},{2,1},{3,2},{5,4},{6,5},{7,6},{9,8},{10,9},{11,10},{13,12},{... | collective-permute-start | bytes 86024 | tf_op jit(solution)/shard_map/ppermute | solution.py:20
  2.5 12.4 %collective-permute-start.1 = (bf16[4,256,14]{2,1,0:T(8,128)(2,1)S(1)}, bf16[4,256,14]{2,1,0:T(8,128)(2,1)S(1)}, u32[]{:S(2)}, u32[]{:S(2)}) collective-permute-start(bf16[4,256,14]{2,1,0:T(8,128)(2,1)S(1)} %get-tuple-element.5), channel_id=1, source_target_pairs={{0,1},{1,2},{2,3},{4,5},{5,6},{6,7},{8,9},{9,10},{10,11},{12,13},{... | collective-permute-start | bytes 86024 | tf_op jit(solution)/shard_map/ppermute | solution.py:19
  10.3 4.7 %copy-start.1 = (bf16[1,4,256,128]{3,2,1,0:T(8,128)(2,1)S(1)}, bf16[1,4,256,128]{3,2,1,0:T(8,128)(2,1)}, u32[]{:S(2)}) copy-start(bf16[1,4,256,128]{3,2,1,0:T(8,128)(2,1)} %param.6) | copy-start | bytes 786436
  26.3 20.4 %copy-start.2 = (s32[128]{0:T(128)S(1)}, s32[128]{0:T(128)}, u32[]{:S(2)}) copy-start(s32[128]{0:T(128)} %param.11) | copy-start | bytes 1540
  26.3 35.1 %all-to-all-start = ((bf16[128,2,640]{2,1,0:T(2,128)(2,1)}), bf16[128,2,640]{2,1,0:T(2,128)(2,1)S(1)}, u32[]{:S(2)}, u32[]{:S(2)}) async-start(bf16[128,2,640]{2,1,0:T(2,128)(2,1)} %reshape.100), calls=%async_computation | async-start | bytes 655360 | tf_op jit(solution)/shard_map/all_to_all | solution.py:151

commit v9 on v8

--- a/solution.py
+++ b/solution.py
@@ -49,10 +49,11 @@
     acc_h = jnp.zeros((rows, LANES), jnp.float32)
     for a in range(taps):
         table = table_ref[0, a]
+        both = jnp.concatenate([table, jnp.concatenate([table[samples:], table[:samples]], axis=0)], axis=1)
         moved = scr_ref[pl.ds(a + 8 - reach, rows), :].astype(jnp.bfloat16)
-        swapped = jnp.concatenate([moved[:, samples:], moved[:, :samples]], axis=1)
-        acc = acc + jnp.dot(moved, table, preferred_element_type=jnp.float32)
-        acc_h = acc_h + jnp.dot(swapped, table, preferred_element_type=jnp.float32)
+        part = jnp.dot(moved, both, preferred_element_type=jnp.float32)
+        acc = acc + part[:, :samples]
+        acc_h = acc_h + part[:, samples:]
     out_ref[:, pl.ds(pl.multiple_of(c * samples, samples), samples)] = (acc * keep).astype(out_ref.dtype)
     lane = lax.broadcasted_iota(jnp.int32, (rows, LANES), 1)
     for k in range(comps):
@@ -87,14 +88,18 @@
     gathered = jnp.dot(jnp.concatenate(selects, axis=1), jnp.concatenate(parts, axis=0), preferred_element_type=jnp.float32)
     gathered = gathered.astype(jnp.bfloat16)
     acc = jnp.zeros((out_rows, LANES), jnp.float32)
-    for a in range(taps):
-        part = jnp.dot(gathered, table_ref[0, a], preferred_element_type=jnp.float32)
-        shift = stride * (a - reach)
-        if shift > 0:
-            part = jnp.concatenate([part[shift:], jnp.zeros((shift, LANES), jnp.float32)], axis=0)
-        elif shift < 0:
-            part = jnp.concatenate([jnp.zeros((-shift, LANES), jnp.float32), part[:shift]], axis=0)
-        acc = acc + part
+    for first in range(0, taps, 2):
+        pair = list(range(first, min(first + 2, taps)))
+        tables = jnp.concatenate([table_ref[0, a] for a in pair], axis=1)
+        both = jnp.dot(gathered, tables, preferred_element_type=jnp.float32)
+        for k, a in enumerate(pair):
+            part = both[:, k * samples:(k + 1) * samples]
+            shift = stride * (a - reach)
+            if shift > 0:
+                part = jnp.concatenate([part[shift:], jnp.zeros((shift, LANES), jnp.float32)], axis=0)
+            elif shift < 0:
+                part = jnp.concatenate([jnp.zeros((-shift, LANES), jnp.float32), part[:shift]], axis=0)
+            acc = acc + part
     out_ref[...] = acc.astype(out_ref.dtype)
 
 

time: 68.1 us -> 65.6 us (0.963)
  Pallas kernels: 13.6 us -> 11 us
    pallas_call x1, Pallas kernels: 8.09 us -> 6.22 us  [fan_call(): pl.pallas_call(kernel, grid=(comps,), in_specs=[pl.BlockSpec((1, rows), l...]
    pallas_call x1, Pallas kernels: 5.49 us -> 4.8 us  [dip_call(): pl.pallas_call(kernel, out_shape=jax.ShapeDtypeStruct((rows * comps, LANE...]
  transfers between devices with their start and end apart: 3 -> 3, of which waited for: 1 -> 1; matrix products, arithmetic and copies ran while one was open for 15% -> 16% of each run, Pallas kernels for 0% -> 0%
where the time goes in v9:
time: 65.6 us; the launch traced here: 65.2 us
  starting transfers between devices  24.4 us (37%)
  waiting for transfers between devices  13.9 us (21%)
  local copies, waits for them, and re-layouts  11.8 us (18%)
  Pallas kernels  11 us (17%)
  matrix products  2.58 us (4%)
  other arithmetic  1.37 us (2%)
    all_to_all x1, starting transfers between devices, on_device(): lax.all_to_all(sent, 'shot', split_axis=0, concat_axis=0, tiled=True)  18.5 us
    all_to_all x1, waiting for transfers between devices, on_device(): lax.all_to_all(sent, 'shot', split_axis=0, concat_axis=0, tiled=True)  13.9 us
    pallas_call x1, Pallas kernels, fan_call(): pl.pallas_call(kernel, grid=(comps,), in_specs=[pl.BlockSpec((1, rows), l...  6.22 us
    dot_general x2, local copies, waits for them, and re-layouts, circulant(): jnp.einsum('gab,jtb->gajt', tap_set, onehot, preferred_element_type=jnp.f...  5.75 us
    pallas_call x1, Pallas kernels, dip_call(): pl.pallas_call(kernel, out_shape=jax.ShapeDtypeStruct((rows * comps, LANE...  4.8 us
    ppermute x1, starting transfers between devices, time_halo(): lax.ppermute(lax.slice_in_dim(block, samples - width, None, axis=-1), axi...  4.59 us
    dot_general x2, matrix products, circulant(): jnp.einsum('gab,jtb->gajt', tap_set, onehot, preferred_element_type=jnp.f...  2.58 us
    reshape x1, local copies, waits for them, and re-layouts, on_device(): sent = packed.reshape(devices, group, packed.shape[-1])  1.81 us
  transfers between devices with their start and end apart: 3, of which 1 were waited for; matrix products, arithmetic and copies ran while one was open for 16% of the time, Pallas kernels for 0%

profile of v9, /device:TPU:1, one launch (start us, length us, event | category | flops | bytes accessed | tf_op | source)
XLA Modules:
  0.0 65.2 jit_solution(14993985318663175043)
XLA Ops:
  0.0 0.0 copy-start
  0.0 1.2 %fusion.12 = (bf16[4,256,14]{2,1,0:T(8,128)(2,1)S(1)}, bf16[4,256,14]{2,1,0:T(8,128)(2,1)S(1)}) fusion(bf16[4,256,128]{2,1,0:T(8,128)(2,1)} %bitcast.24), kind=kLoop, calls=%fused_computation.22 | loop fusion | bytes 114688 | tf_op jit(solution)/shard_map/slice | solution.py:19
  1.2 1.3 %collective-permute-start = (bf16[4,256,14]{2,1,0:T(8,128)(2,1)S(1)}, bf16[4,256,14]{2,1,0:T(8,128)(2,1)S(1)}, u32[]{:S(2)}, u32[]{:S(2)}) collective-permute-start(bf16[4,256,14]{2,1,0:T(8,128)(2,1)S(1)} %get-tuple-element.6), channel_id=1, source_target_pairs={{1,0},{2,1},{3,2},{5,4},{6,5},{7,6},{9,8},{10,9},{11,10},{13,12},{... | collective-permute-start | bytes 86024 | tf_op jit(solution)/shard_map/ppermute | solution.py:20
  2.5 4.6 %collective-permute-start.1 = (bf16[4,256,14]{2,1,0:T(8,128)(2,1)S(1)}, bf16[4,256,14]{2,1,0:T(8,128)(2,1)S(1)}, u32[]{:S(2)}, u32[]{:S(2)}) collective-permute-start(bf16[4,256,14]{2,1,0:T(8,128)(2,1)S(1)} %get-tuple-element.5), channel_id=1, source_target_pairs={{0,1},{1,2},{2,3},{4,5},{5,6},{6,7},{8,9},{9,10},{10,11},{12,13},{... | collective-permute-start | bytes 86024 | tf_op jit(solution)/shard_map/ppermute | solution.py:19
  7.1 0.1 add_select_fusion
  7.1 0.7 %convert_reduce_fusion = bf16[256]{0:T(256)(128)(2,1)S(1)} fusion(s32[1,256]{1,0:T(1,128)} %param.9), kind=kLoop, calls=%fused_computation.20 | loop fusion | flops 256 | bytes 1536 | tf_op jit(solution)/shard_map/convert_element_type | solution.py:146
  7.8 1.9 %fusion.3 = bf16[256,128,4,15]{1,3,2,0:T(8,128)(2,1)S(1)} fusion(s32[256,128]{1,0:T(8,128)S(1)} %add_select_fusion, bf16[4,15,15]{2,0,1:T(4,128)(2,1)} %param.7), kind=kOutput, calls=%fused_computation.5 | convolution fusion | flops 59473920 | bytes 4065032 | tf_op jit(solution)/shard_map/gab,jtb->gajt/dot_general | solution.py:31
  9.8 0.5 select_convert_fusion.edge_ref
  10.3 0.0 copy-start.1
  10.3 4.5 %copy.24 = bf16[256,128,4,15]{1,0,3,2:T(8,128)(2,1)} copy(bf16[256,128,4,15]{1,3,2,0:T(8,128)(2,1)S(1)} %fusion.3) | data formatting | bytes 7864320 | tf_op jit(solution)/shard_map/gab,jtb->gajt/dot_general | solution.py:31
  14.9 0.0 collective-permute-done
  14.9 0.0 collective-permute-done.1
  14.9 0.1 broadcast_in_dim.42
  15.1 0.0 copy-done.1
  15.1 1.3 %concatenate.3.ext_ref = bf16[4,256,256]{2,1,0:T(8,128)(2,1)} concatenate(bf16[4,256,128]{2,1,0:T(8,128)(2,1)S(1)} %bitcast.25, bf16[4,256,14]{2,1,0:T(8,128)(2,1)S(1)} %collective-permute-done, bf16[4,256,18]{2,1,0:T(8,128)(2,1)S(1)} %broadcast_in_dim.22, bf16[4,256,1]{2,1,0:T(8,128)(2,1)S(1)} %broadcast_in_dim.42, bf16[4,256,81]{2,1,0:T(8,128)(2,1)S(1)} %broadcast_in_dim.43, ...), dimensions={2} | concatenate | bytes 1048576 | tf_op jit(solution)/shard_map/concatenate | solution.py:149
  16.4 6.2 %shard_map.64 = bf16[256,640]{1,0:T(8,128)(2,1)} custom-call(s32[1,256]{1,0:T(1,128)} %bitcast.26, f32[1,128]{1,0:T(1,128)} %select_convert_fusion.edge_ref, bf16[4,256,256]{2,1,0:T(8,128)(2,1)} %concatenate.3.ext_ref, bf16[4,15,256,128]{3,2,1,0:T(8,128)(2,1)} %bitcast.22), custom_call_target="tpu_custom_call" | custom-call | tf_op jit(solution)/shard_map/pallas_call | solution.py:110
  22.6 1.8 %reshape.100 = bf16[128,2,640]{2,1,0:T(2,128)(2,1)} reshape(bf16[256,640]{1,0:T(8,128)(2,1)} %shard_map.64) | data formatting | bytes 655360 | tf_op jit(solution)/shard_map/reshape | solution.py:155
  24.5 0.0 copy-start.2
  24.5 18.5 %all-to-all-start = ((bf16[128,2,640]{2,1,0:T(2,128)(2,1)}), bf16[128,2,640]{2,1,0:T(2,128)(2,1)S(1)}, u32[]{:S(2)}, u32[]{:S(2)}) async-start(bf16[128,2,640]{2,1,0:T(2,128)(2,1)} %reshape.100), calls=%async_computation | async-start | bytes 655360 | tf_op jit(solution)/shard_map/all_to_all | solution.py:156
  43.0 0.0 copy-done
  43.0 0.6 fusion.1
  43.6 1.2 %copy.25 = bf16[256,128,15]{1,0,2:T(8,128)(2,1)} copy(bf16[256,128,15]{1,2,0:T(8,128)(2,1)S(1)} %fusion.1) | data formatting | bytes 1966080 | tf_op jit(solution)/shard_map/gab,jtb->gajt/dot_general | solution.py:31
  44.8 0.0 copy-done.2
  44.9 0.1 iota_add_fusion
  44.9 0.7 %add.51.target_ref = s32[1,256]{1,0:T(1,128)} reshape(s32[128,2]{1,0:T(8,128)S(1)} %iota_add_fusion) | data formatting | bytes 2048 | tf_op jit(solution)/shard_map/add | solution.py:159
  45.7 13.9 %all-to-all-done = bf16[128,2,640]{2,1,0:T(2,128)(2,1)S(1)} async-done(((bf16[128,2,640]{2,1,0:T(2,128)(2,1)}), bf16[128,2,640]{2,1,0:T(2,128)(2,1)S(1)}, u32[]{:S(2)}, u32[]{:S(2)}) %all-to-all-start) | async-done | bytes 327712 | tf_op jit(solution)/shard_map/all_to_all | solution.py:156
  59.6 0.8 %reshape.101.data_ref = bf16[256,640]{1,0:T(8,128)(2,1)} reshape(bf16[128,2,640]{2,1,0:T(2,128)(2,1)S(1)} %all-to-all-done) | data formatting | bytes 655360 | tf_op jit(solution)/shard_map/reshape | solution.py:157
  60.4 4.8 %shard_map.65 = bf16[1024,128]{1,0:T(8,128)(2,1)} custom-call(s32[1,256]{1,0:T(1,128)} %add.51.target_ref, bf16[256,640]{1,0:T(8,128)(2,1)} %reshape.101.data_ref, bf16[1,15,256,128]{3,2,1,0:T(8,128)(2,1)} %bitcast.23), custom_call_target="tpu_custom_call" | custom-call | tf_op jit(solution)/shard_map/pallas_call | solution.py:129
  (3 shorter events, 0.1 us)
Async XLA Ops:
  0.0 43.0 %copy-start = (bf16[15,15]{1,0:T(8,128)(2,1)S(1)}, bf16[15,15]{1,0:T(8,128)(2,1)}, u32[]{:S(2)}) copy-start(bf16[15,15]{1,0:T(8,128)(2,1)} %param.8) | copy-start | bytes 1354
  1.2 13.7 %collective-permute-start = (bf16[4,256,14]{2,1,0:T(8,128)(2,1)S(1)}, bf16[4,256,14]{2,1,0:T(8,128)(2,1)S(1)}, u32[]{:S(2)}, u32[]{:S(2)}) collective-permute-start(bf16[4,256,14]{2,1,0:T(8,128)(2,1)S(1)} %get-tuple-element.6), channel_id=1, source_target_pairs={{1,0},{2,1},{3,2},{5,4},{6,5},{7,6},{9,8},{10,9},{11,10},{13,12},{... | collective-permute-start | bytes 86024 | tf_op jit(solution)/shard_map/ppermute | solution.py:20
  2.5 12.4 %collective-permute-start.1 = (bf16[4,256,14]{2,1,0:T(8,128)(2,1)S(1)}, bf16[4,256,14]{2,1,0:T(8,128)(2,1)S(1)}, u32[]{:S(2)}, u32[]{:S(2)}) collective-permute-start(bf16[4,256,14]{2,1,0:T(8,128)(2,1)S(1)} %get-tuple-element.5), channel_id=1, source_target_pairs={{0,1},{1,2},{2,3},{4,5},{5,6},{6,7},{8,9},{9,10},{10,11},{12,13},{... | collective-permute-start | bytes 86024 | tf_op jit(solution)/shard_map/ppermute | solution.py:19
  10.3 4.7 %copy-start.1 = (bf16[1,4,256,128]{3,2,1,0:T(8,128)(2,1)S(1)}, bf16[1,4,256,128]{3,2,1,0:T(8,128)(2,1)}, u32[]{:S(2)}) copy-start(bf16[1,4,256,128]{3,2,1,0:T(8,128)(2,1)} %param.6) | copy-start | bytes 786436
  24.5 20.4 %copy-start.2 = (s32[128]{0:T(128)S(1)}, s32[128]{0:T(128)}, u32[]{:S(2)}) copy-start(s32[128]{0:T(128)} %param.11) | copy-start | bytes 1540
  24.5 35.1 %all-to-all-start = ((bf16[128,2,640]{2,1,0:T(2,128)(2,1)}), bf16[128,2,640]{2,1,0:T(2,128)(2,1)S(1)}, u32[]{:S(2)}, u32[]{:S(2)}) async-start(bf16[128,2,640]{2,1,0:T(2,128)(2,1)} %reshape.100), calls=%async_computation | async-start | bytes 655360 | tf_op jit(solution)/shard_map/all_to_all | solution.py:156

commit v10 on v9

--- a/solution.py
+++ b/solution.py
@@ -54,7 +54,7 @@
         part = jnp.dot(moved, both, preferred_element_type=jnp.float32)
         acc = acc + part[:, :samples]
         acc_h = acc_h + part[:, samples:]
-    out_ref[:, pl.ds(pl.multiple_of(c * samples, samples), samples)] = (acc * keep).astype(out_ref.dtype)
+    out_ref[:, :, pl.ds(pl.multiple_of(c * samples, samples), samples)] = (acc * keep).astype(out_ref.dtype).reshape(rows // 2, 2, samples)
     lane = lax.broadcasted_iota(jnp.int32, (rows, LANES), 1)
     for k in range(comps):
         @pl.when(c == k)
@@ -68,22 +68,22 @@
 
     @pl.when(c == comps - 1)
     def _():
-        out_ref[:, comps * samples:(comps + 1) * samples] = (halo_ref[...] * keep * edge_ref[...]).astype(out_ref.dtype)
+        out_ref[:, :, comps * samples:(comps + 1) * samples] = (halo_ref[...] * keep * edge_ref[...]).astype(out_ref.dtype).reshape(rows // 2, 2, samples)
 
 
 def dip_kernel(target_ref, data_ref, table_ref, out_ref, *, taps, group, comps):
-    rows = data_ref.shape[0]
+    rows = data_ref.shape[0] * data_ref.shape[1]
     samples = LANES
     reach = (taps - 1) // 2
     stride = comps * group
     out_rows = out_ref.shape[0]
     target = target_ref[...]
     row = lax.broadcasted_iota(jnp.int32, (out_rows, rows), 0)
-    halo = data_ref[:, comps * samples:(comps + 1) * samples].astype(jnp.float32)
+    halo = data_ref[:, :, comps * samples:(comps + 1) * samples].reshape(rows, samples).astype(jnp.float32)
     selects, parts = [], []
     for c in range(comps):
         mine = pltpu.roll(halo, (samples - reach - 2 * reach * c) % samples, 1).astype(jnp.bfloat16)
-        parts.append(jnp.concatenate([data_ref[:, c * samples:(c + 1) * samples], mine], axis=1))
+        parts.append(jnp.concatenate([data_ref[:, :, c * samples:(c + 1) * samples].reshape(rows, samples), mine], axis=1))
         selects.append((row == target + group * c).astype(jnp.bfloat16))
     gathered = jnp.dot(jnp.concatenate(selects, axis=1), jnp.concatenate(parts, axis=0), preferred_element_type=jnp.float32)
     gathered = gathered.astype(jnp.bfloat16)
@@ -116,14 +116,14 @@
             pl.BlockSpec((1, rows, EXT), lambda c: (c, 0, 0)),
             pl.BlockSpec((1, taps, EXT, LANES), lambda c: (c, 0, 0, 0)),
         ],
-        out_specs=pl.BlockSpec((rows, (comps + 1) * LANES), lambda c: (0, 0)),
-        out_shape=jax.ShapeDtypeStruct((rows, (comps + 1) * LANES), jnp.bfloat16),
+        out_specs=pl.BlockSpec((rows // 2, 2, (comps + 1) * LANES), lambda c: (0, 0, 0)),
+        out_shape=jax.ShapeDtypeStruct((rows // 2, 2, (comps + 1) * LANES), jnp.bfloat16),
         scratch_shapes=[pltpu.VMEM((rows + 16, EXT), jnp.float32), pltpu.VMEM((rows, LANES), jnp.float32)],
     )(place, edge, ext, tables)
 
 
 def dip_call(target, data, tables, group, comps):
-    rows = data.shape[0]
+    rows = data.shape[0] * data.shape[1]
     taps = tables.shape[1]
     kernel = functools.partial(dip_kernel, taps=taps, group=group, comps=comps)
     return pl.pallas_call(
@@ -152,9 +152,7 @@
     edge = jnp.where(lane < reach, place > 0, place < lax.axis_size("tm") - 1).astype(jnp.float32)[None, :]
     packed = fan_call(node_place[None, :], edge, ext, circulant(fan_taps, samples), live_col)
 
-    sent = packed.reshape(devices, group, packed.shape[-1])
-    arrived = lax.all_to_all(sent, "shot", split_axis=0, concat_axis=0, tiled=True)
-    data = arrived.reshape(devices * group, packed.shape[-1])
+    data = lax.all_to_all(packed, "shot", split_axis=0, concat_axis=0, tiled=True)
     spread = comps * group
     target = (jnp.repeat(shot_place, group) * spread + jnp.tile(jnp.arange(group, dtype=jnp.int32), devices))[None, :]
     out = dip_call(target, data, circulant(dip_taps[None], samples), group, comps)

time: 65.6 us -> 63.7 us (0.971)
  local copies, waits for them, and re-layouts: 11.8 us -> 9.92 us
    reshape x2 -> x0, local copies, waits for them, and re-layouts: 2.66 us -> none  [the longest x1 1.81 us: on_device(): sent = packed.reshape(devices, group, packed.shape[-1])]
    unnamed x6 -> x8, local copies, waits for them, and re-layouts: 0.01 us -> 0.74 us
where the time goes in v10:
time: 63.7 us; the launch traced here: 63.3 us
  starting transfers between devices  24.4 us (38%)
  waiting for transfers between devices  13.9 us (22%)
  Pallas kernels  11.1 us (17%)
  local copies, waits for them, and re-layouts  9.92 us (16%)
  matrix products  2.58 us (4%)
  other arithmetic  1.37 us (2%)
    all_to_all x1, starting transfers between devices, on_device(): lax.all_to_all(packed, 'shot', split_axis=0, concat_axis=0, tiled=True)  18.5 us
    all_to_all x1, waiting for transfers between devices, on_device(): lax.all_to_all(packed, 'shot', split_axis=0, concat_axis=0, tiled=True)  13.9 us
    pallas_call x1, Pallas kernels, fan_call(): pl.pallas_call(kernel, grid=(comps,), in_specs=[pl.BlockSpec((1, rows), l...  6.25 us
    dot_general x2, local copies, waits for them, and re-layouts, circulant(): jnp.einsum('gab,jtb->gajt', tap_set, onehot, preferred_element_type=jnp.f...  5.76 us
    pallas_call x1, Pallas kernels, dip_call(): pl.pallas_call(kernel, out_shape=jax.ShapeDtypeStruct((rows * comps, LANE...  4.81 us
    ppermute x1, starting transfers between devices, time_halo(): lax.ppermute(lax.slice_in_dim(block, samples - width, None, axis=-1), axi...  4.59 us
    dot_general x2, matrix products, circulant(): jnp.einsum('gab,jtb->gajt', tap_set, onehot, preferred_element_type=jnp.f...  2.58 us
    concatenate x1, local copies, waits for them, and re-layouts, on_device(): ext = jnp.concatenate([block, high, gap1, live, gap2, low], axis=-1)  1.36 us
  transfers between devices with their start and end apart: 3, of which 1 were waited for; matrix products, arithmetic and copies ran while one was open for 16% of the time, Pallas kernels for 0%

profile of v10, /device:TPU:1, one launch (start us, length us, event | category | flops | bytes accessed | tf_op | source)
XLA Modules:
  0.0 63.3 jit_solution(14101129514479075984)
XLA Ops:
  0.0 0.0 copy-start
  0.0 1.2 %fusion.12 = (bf16[4,256,14]{2,1,0:T(8,128)(2,1)S(1)}, bf16[4,256,14]{2,1,0:T(8,128)(2,1)S(1)}) fusion(bf16[4,256,128]{2,1,0:T(8,128)(2,1)} %bitcast.24), kind=kLoop, calls=%fused_computation.22 | loop fusion | bytes 114688 | tf_op jit(solution)/shard_map/slice | solution.py:19
  1.2 1.3 %collective-permute-start = (bf16[4,256,14]{2,1,0:T(8,128)(2,1)S(1)}, bf16[4,256,14]{2,1,0:T(8,128)(2,1)S(1)}, u32[]{:S(2)}, u32[]{:S(2)}) collective-permute-start(bf16[4,256,14]{2,1,0:T(8,128)(2,1)S(1)} %get-tuple-element.6), channel_id=1, source_target_pairs={{1,0},{2,1},{3,2},{5,4},{6,5},{7,6},{9,8},{10,9},{11,10},{13,12},{... | collective-permute-start | bytes 86024 | tf_op jit(solution)/shard_map/ppermute | solution.py:20
  2.5 4.6 %collective-permute-start.1 = (bf16[4,256,14]{2,1,0:T(8,128)(2,1)S(1)}, bf16[4,256,14]{2,1,0:T(8,128)(2,1)S(1)}, u32[]{:S(2)}, u32[]{:S(2)}) collective-permute-start(bf16[4,256,14]{2,1,0:T(8,128)(2,1)S(1)} %get-tuple-element.5), channel_id=1, source_target_pairs={{0,1},{1,2},{2,3},{4,5},{5,6},{6,7},{8,9},{9,10},{10,11},{12,13},{... | collective-permute-start | bytes 86024 | tf_op jit(solution)/shard_map/ppermute | solution.py:19
  7.1 0.1 add_select_fusion
  7.1 0.7 %convert_reduce_fusion = bf16[256]{0:T(256)(128)(2,1)S(1)} fusion(s32[1,256]{1,0:T(1,128)} %param.9), kind=kLoop, calls=%fused_computation.20 | loop fusion | flops 256 | bytes 1536 | tf_op jit(solution)/shard_map/convert_element_type | solution.py:146
  7.8 1.9 %fusion.3 = bf16[256,128,4,15]{1,3,2,0:T(8,128)(2,1)S(1)} fusion(s32[256,128]{1,0:T(8,128)S(1)} %add_select_fusion, bf16[4,15,15]{2,0,1:T(4,128)(2,1)} %param.7), kind=kOutput, calls=%fused_computation.5 | convolution fusion | flops 59473920 | bytes 4065032 | tf_op jit(solution)/shard_map/gab,jtb->gajt/dot_general | solution.py:31
  9.8 0.5 select_convert_fusion.edge_ref
  10.3 0.0 copy-start.1
  10.3 4.5 %copy.24 = bf16[256,128,4,15]{1,0,3,2:T(8,128)(2,1)} copy(bf16[256,128,4,15]{1,3,2,0:T(8,128)(2,1)S(1)} %fusion.3) | data formatting | bytes 7864320 | tf_op jit(solution)/shard_map/gab,jtb->gajt/dot_general | solution.py:31
  14.9 0.0 collective-permute-done
  14.9 0.0 collective-permute-done.1
  14.9 0.1 broadcast_in_dim.42
  15.1 0.0 copy-done.1
  15.1 1.4 %concatenate.3.ext_ref = bf16[4,256,256]{2,1,0:T(8,128)(2,1)} concatenate(bf16[4,256,128]{2,1,0:T(8,128)(2,1)S(1)} %bitcast.25, bf16[4,256,14]{2,1,0:T(8,128)(2,1)S(1)} %collective-permute-done, bf16[4,256,18]{2,1,0:T(8,128)(2,1)S(1)} %broadcast_in_dim.22, bf16[4,256,1]{2,1,0:T(8,128)(2,1)S(1)} %broadcast_in_dim.42, bf16[4,256,81]{2,1,0:T(8,128)(2,1)S(1)} %broadcast_in_dim.43, ...), dimensions={2} | concatenate | bytes 1048576 | tf_op jit(solution)/shard_map/concatenate | solution.py:149
  16.4 6.2 %shard_map.64 = bf16[128,2,640]{2,1,0:T(2,128)(2,1)} custom-call(s32[1,256]{1,0:T(1,128)} %bitcast.26, f32[1,128]{1,0:T(1,128)} %select_convert_fusion.edge_ref, bf16[4,256,256]{2,1,0:T(8,128)(2,1)} %concatenate.3.ext_ref, bf16[4,15,256,128]{3,2,1,0:T(8,128)(2,1)} %bitcast.22), custom_call_target="tpu_custom_call" | custom-call | tf_op jit(solution)/shard_map/pallas_call | solution.py:110
  22.7 0.0 copy-start.3
  22.7 18.5 %all-to-all-start = ((bf16[128,2,640]{2,1,0:T(2,128)(2,1)}), bf16[128,2,640]{2,1,0:T(2,128)(2,1)S(1)}, u32[]{:S(2)}, u32[]{:S(2)}) async-start(bf16[128,2,640]{2,1,0:T(2,128)(2,1)} %shard_map.64), calls=%async_computation | async-start | bytes 655360 | tf_op jit(solution)/shard_map/all_to_all | solution.py:155
  41.2 0.0 copy-done
  41.2 0.6 fusion.1
  41.9 1.2 %copy.25 = bf16[256,128,15]{1,0,2:T(8,128)(2,1)} copy(bf16[256,128,15]{1,2,0:T(8,128)(2,1)S(1)} %fusion.1) | data formatting | bytes 1966080 | tf_op jit(solution)/shard_map/gab,jtb->gajt/dot_general | solution.py:31
  43.1 0.0 copy-done.3
  43.1 0.1 iota_add_fusion
  43.2 0.7 %add.51.target_ref = s32[1,256]{1,0:T(1,128)} reshape(s32[128,2]{1,0:T(8,128)S(1)} %iota_add_fusion) | data formatting | bytes 2048 | tf_op jit(solution)/shard_map/add | solution.py:157
  43.9 13.9 %all-to-all-done.data_ref = bf16[128,2,640]{2,1,0:T(2,128)(2,1)S(1)} async-done(((bf16[128,2,640]{2,1,0:T(2,128)(2,1)}), bf16[128,2,640]{2,1,0:T(2,128)(2,1)S(1)}, u32[]{:S(2)}, u32[]{:S(2)}) %all-to-all-start) | async-done | bytes 327712 | tf_op jit(solution)/shard_map/all_to_all | solution.py:155
  57.8 0.0 copy-start.2
  57.8 0.7 %copy-done.2 = bf16[128,2,640]{2,1,0:T(2,128)(2,1)} copy-done((bf16[128,2,640]{2,1,0:T(2,128)(2,1)}, bf16[128,2,640]{2,1,0:T(2,128)(2,1)S(1)}, u32[]{:S(2)}) %copy-start.2) | copy-done | bytes 327704
  58.5 4.8 %shard_map.65 = bf16[1024,128]{1,0:T(8,128)(2,1)} custom-call(s32[1,256]{1,0:T(1,128)} %add.51.target_ref, bf16[128,2,640]{2,1,0:T(2,128)(2,1)} %copy-done.2, bf16[1,15,256,128]{3,2,1,0:T(8,128)(2,1)} %bitcast.23), custom_call_target="tpu_custom_call" | custom-call | tf_op jit(solution)/shard_map/pallas_call | solution.py:129
  (3 shorter events, 0.1 us)
Async XLA Ops:
  0.0 41.2 %copy-start = (bf16[15,15]{1,0:T(8,128)(2,1)S(1)}, bf16[15,15]{1,0:T(8,128)(2,1)}, u32[]{:S(2)}) copy-start(bf16[15,15]{1,0:T(8,128)(2,1)} %param.8) | copy-start | bytes 1354
  1.2 13.7 %collective-permute-start = (bf16[4,256,14]{2,1,0:T(8,128)(2,1)S(1)}, bf16[4,256,14]{2,1,0:T(8,128)(2,1)S(1)}, u32[]{:S(2)}, u32[]{:S(2)}) collective-permute-start(bf16[4,256,14]{2,1,0:T(8,128)(2,1)S(1)} %get-tuple-element.6), channel_id=1, source_target_pairs={{1,0},{2,1},{3,2},{5,4},{6,5},{7,6},{9,8},{10,9},{11,10},{13,12},{... | collective-permute-start | bytes 86024 | tf_op jit(solution)/shard_map/ppermute | solution.py:20
  2.5 12.4 %collective-permute-start.1 = (bf16[4,256,14]{2,1,0:T(8,128)(2,1)S(1)}, bf16[4,256,14]{2,1,0:T(8,128)(2,1)S(1)}, u32[]{:S(2)}, u32[]{:S(2)}) collective-permute-start(bf16[4,256,14]{2,1,0:T(8,128)(2,1)S(1)} %get-tuple-element.5), channel_id=1, source_target_pairs={{0,1},{1,2},{2,3},{4,5},{5,6},{6,7},{8,9},{9,10},{10,11},{12,13},{... | collective-permute-start | bytes 86024 | tf_op jit(solution)/shard_map/ppermute | solution.py:19
  10.3 4.7 %copy-start.1 = (bf16[1,4,256,128]{3,2,1,0:T(8,128)(2,1)S(1)}, bf16[1,4,256,128]{3,2,1,0:T(8,128)(2,1)}, u32[]{:S(2)}) copy-start(bf16[1,4,256,128]{3,2,1,0:T(8,128)(2,1)} %param.6) | copy-start | bytes 786436
  22.7 20.4 %copy-start.3 = (s32[128]{0:T(128)S(1)}, s32[128]{0:T(128)}, u32[]{:S(2)}) copy-start(s32[128]{0:T(128)} %param.11) | copy-start | bytes 1540
  22.7 35.1 %all-to-all-start = ((bf16[128,2,640]{2,1,0:T(2,128)(2,1)}), bf16[128,2,640]{2,1,0:T(2,128)(2,1)S(1)}, u32[]{:S(2)}, u32[]{:S(2)}) async-start(bf16[128,2,640]{2,1,0:T(2,128)(2,1)} %shard_map.64), calls=%async_computation | async-start | bytes 655360 | tf_op jit(solution)/shard_map/all_to_all | solution.py:155
  57.8 0.7 %copy-start.2 = (bf16[128,2,640]{2,1,0:T(2,128)(2,1)}, bf16[128,2,640]{2,1,0:T(2,128)(2,1)S(1)}, u32[]{:S(2)}) copy-start(bf16[128,2,640]{2,1,0:T(2,128)(2,1)S(1)} %all-to-all-done.data_ref) | copy-start | bytes 983044

commit v11 on v10

--- a/solution.py
+++ b/solution.py
@@ -32,15 +32,19 @@
     return tables.astype(jnp.bfloat16)
 
 
-def fan_kernel(place_ref, edge_ref, ext_ref, table_ref, out_ref, scr_ref, halo_ref, *, taps, live_col, comps):
+def fan_kernel(place_ref, edge_ref, live_ref, block_ref, prev_ref, next_ref, table_ref, out_ref, scr_ref, halo_ref, *, taps, comps):
     c = pl.program_id(0)
-    rows = ext_ref.shape[1]
+    rows = block_ref.shape[1]
     samples = LANES
     reach = (taps - 1) // 2
+    wide = 2 * reach
     place = place_ref[...]
     select = (lax.broadcasted_iota(jnp.int32, (rows, rows), 0) == place).astype(jnp.bfloat16)
-    ordered = jnp.dot(select, ext_ref[0], preferred_element_type=jnp.float32)
-    keep = ordered[:, live_col:live_col + 1]
+    keep = jnp.sum(select.astype(jnp.float32) * live_ref[...].astype(jnp.float32), axis=1, keepdims=True)
+    lane = lax.broadcasted_iota(jnp.int32, (rows, LANES), 1)
+    outer = jnp.where(lane < wide, next_ref[0], jnp.where(lane >= LANES - wide, prev_ref[0], jnp.zeros_like(prev_ref[0])))
+    ext = jnp.concatenate([block_ref[0], outer], axis=1)
+    ordered = jnp.dot(select, ext, preferred_element_type=jnp.float32)
     zeros = jnp.zeros((8, EXT), jnp.float32)
     scr_ref[0:8, :] = zeros
     scr_ref[rows + 8:rows + 16, :] = zeros
@@ -55,7 +59,6 @@
         acc = acc + part[:, :samples]
         acc_h = acc_h + part[:, samples:]
     out_ref[:, :, pl.ds(pl.multiple_of(c * samples, samples), samples)] = (acc * keep).astype(out_ref.dtype).reshape(rows // 2, 2, samples)
-    lane = lax.broadcasted_iota(jnp.int32, (rows, LANES), 1)
     for k in range(comps):
         @pl.when(c == k)
         def _():
@@ -103,23 +106,27 @@
     out_ref[...] = acc.astype(out_ref.dtype)
 
 
-def fan_call(place, edge, ext, tables, live_col):
-    comps, rows, _ = ext.shape
+def fan_call(place, edge, live, block, prev, nxt, tables):
+    comps, rows, samples = block.shape
     taps = tables.shape[1]
-    kernel = functools.partial(fan_kernel, taps=taps, live_col=live_col, comps=comps)
+    kernel = functools.partial(fan_kernel, taps=taps, comps=comps)
+    part = pl.BlockSpec((1, rows, samples), lambda c: (c, 0, 0))
     return pl.pallas_call(
         kernel,
         grid=(comps,),
         in_specs=[
             pl.BlockSpec((1, rows), lambda c: (0, 0)),
             pl.BlockSpec((1, LANES), lambda c: (0, 0)),
-            pl.BlockSpec((1, rows, EXT), lambda c: (c, 0, 0)),
+            pl.BlockSpec((1, rows), lambda c: (0, 0)),
+            part,
+            part,
+            part,
             pl.BlockSpec((1, taps, EXT, LANES), lambda c: (c, 0, 0, 0)),
         ],
         out_specs=pl.BlockSpec((rows // 2, 2, (comps + 1) * LANES), lambda c: (0, 0, 0)),
         out_shape=jax.ShapeDtypeStruct((rows // 2, 2, (comps + 1) * LANES), jnp.bfloat16),
         scratch_shapes=[pltpu.VMEM((rows + 16, EXT), jnp.float32), pltpu.VMEM((rows, LANES), jnp.float32)],
-    )(place, edge, ext, tables)
+    )(place, edge, live, block, prev, nxt, tables)
 
 
 def dip_call(target, data, tables, group, comps):
@@ -141,16 +148,15 @@
     group = nodes // devices
 
     block = records[0]
-    low, high = time_halo(block, "tm", wide)
-    live_col = samples + 32
-    live = jnp.broadcast_to(live_mask[0].astype(jnp.bfloat16)[None, :, None], (comps, nodes, 1))
-    gap1 = jnp.zeros((comps, nodes, live_col - samples - wide), jnp.bfloat16)
-    gap2 = jnp.zeros((comps, nodes, EXT - wide - live_col - 1), jnp.bfloat16)
-    ext = jnp.concatenate([block, high, gap1, live, gap2, low], axis=-1)
+    count = lax.axis_size("tm")
+    forward = [(i, i + 1) for i in range(count - 1)]
+    backward = [(target, source) for source, target in forward]
+    prev = lax.ppermute(block, "tm", forward)
+    nxt = lax.ppermute(block, "tm", backward)
     place = lax.axis_index("tm")
     lane = jnp.arange(LANES, dtype=jnp.int32) % wide
-    edge = jnp.where(lane < reach, place > 0, place < lax.axis_size("tm") - 1).astype(jnp.float32)[None, :]
-    packed = fan_call(node_place[None, :], edge, ext, circulant(fan_taps, samples), live_col)
+    edge = jnp.where(lane < reach, place > 0, place < count - 1).astype(jnp.float32)[None, :]
+    packed = fan_call(node_place[None, :], edge, live_mask, block, prev, nxt, circulant(fan_taps, samples))
 
     data = lax.all_to_all(packed, "shot", split_axis=0, concat_axis=0, tiled=True)
     spread = comps * group

time: 63.7 us -> 64.6 us (1.014)
  matrix products: 2.58 us -> 4.52 us
  starting transfers between devices: 24.4 us -> 23.4 us
  other arithmetic: 1.37 us -> 0.67 us
    dot_general x2, local copies, waits for them, and re-layouts: 5.76 us -> 7.93 us  [circulant(): jnp.einsum('gab,jtb->gajt', tap_set, onehot, preferred_element_type=jnp.f...]
    dot_general x2, matrix products: 2.58 us -> 4.52 us  [circulant(): jnp.einsum('gab,jtb->gajt', tap_set, onehot, preferred_element_type=jnp.f...]
    concatenate x1 -> x0, local copies, waits for them, and re-layouts: 1.36 us -> none  [on_device(): ext = jnp.concatenate([block, high, gap1, live, gap2, low], axis=-1)]
    slice x1 -> x0, local copies, waits for them, and re-layouts: 1.18 us -> none  [time_halo(): lax.slice_in_dim(block, samples - width, None, axis=-1)]
    unnamed x8 -> x10, local copies, waits for them, and re-layouts: 0.74 us -> 1.51 us
    convert_element_type x2 -> x1, other arithmetic: 1.23 us -> 0.53 us  [on_device(): jnp.where(lane < reach, place > 0, place < count - 1).astype(jnp.float32)]
  transfers between devices with their start and end apart: 3 -> 3, of which waited for: 1 -> 1; matrix products, arithmetic and copies ran while one was open for 16% -> 22% of each run, Pallas kernels for 0% -> 0%
where the time goes in v11:
time: 64.6 us; the launch traced here: 63.9 us
  starting transfers between devices  23.4 us (36%)
  waiting for transfers between devices  13.9 us (22%)
  Pallas kernels  11.1 us (17%)
  local copies, waits for them, and re-layouts  10.2 us (16%)
  matrix products  4.52 us (7%)
  other arithmetic  0.67 us (1%)
    all_to_all x1, starting transfers between devices, on_device(): lax.all_to_all(packed, 'shot', split_axis=0, concat_axis=0, tiled=True)  18 us
    all_to_all x1, waiting for transfers between devices, on_device(): lax.all_to_all(packed, 'shot', split_axis=0, concat_axis=0, tiled=True)  13.9 us
    dot_general x2, local copies, waits for them, and re-layouts, circulant(): jnp.einsum('gab,jtb->gajt', tap_set, onehot, preferred_element_type=jnp.f...  7.93 us
    pallas_call x1, Pallas kernels, fan_call(): pl.pallas_call(kernel, grid=(comps,), in_specs=[pl.BlockSpec((1, rows), l...  6.33 us
    pallas_call x1, Pallas kernels, dip_call(): pl.pallas_call(kernel, out_shape=jax.ShapeDtypeStruct((rows * comps, LANE...  4.81 us
    dot_general x2, matrix products, circulant(): jnp.einsum('gab,jtb->gajt', tap_set, onehot, preferred_element_type=jnp.f...  4.52 us
    ppermute x1, starting transfers between devices, on_device(): prev = lax.ppermute(block, 'tm', forward)  4.08 us
    unnamed x10, local copies, waits for them, and re-layouts  1.51 us
  transfers between devices with their start and end apart: 3, of which 1 were waited for; matrix products, arithmetic and copies ran while one was open for 22% of the time, Pallas kernels for 0%

profile of v11, /device:TPU:1, one launch (start us, length us, event | category | flops | bytes accessed | tf_op | source)
XLA Modules:
  0.0 63.9 jit_solution(9821656093127888975)
XLA Ops:
  0.0 0.0 copy-start
  0.0 4.1 %collective-permute-start = (bf16[4,256,128]{2,1,0:T(8,128)(2,1)}, bf16[4,256,128]{2,1,0:T(8,128)(2,1)S(1)}, u32[]{:S(2)}, u32[]{:S(2)}) collective-permute-start(bf16[4,256,128]{2,1,0:T(8,128)(2,1)} %bitcast.24), channel_id=1, source_target_pairs={{0,1},{1,2},{2,3},{4,5},{5,6},{6,7},{8,9},{9,10},{10,11},{12,13},{... | collective-permute-start | bytes 786440 | tf_op jit(solution)/shard_map/ppermute | solution.py:154
  4.1 1.3 %collective-permute-start.1 = (bf16[4,256,128]{2,1,0:T(8,128)(2,1)}, bf16[4,256,128]{2,1,0:T(8,128)(2,1)S(1)}, u32[]{:S(2)}, u32[]{:S(2)}) collective-permute-start(bf16[4,256,128]{2,1,0:T(8,128)(2,1)} %bitcast.25), channel_id=1, source_target_pairs={{1,0},{2,1},{3,2},{5,4},{6,5},{7,6},{9,8},{10,9},{11,10},{13,12},{... | collective-permute-start | bytes 786440 | tf_op jit(solution)/shard_map/ppermute | solution.py:155
  5.4 0.1 add_select_fusion
  5.5 3.9 %fusion.3 = bf16[256,128,4,15]{1,3,2,0:T(8,128)(2,1)} fusion(s32[256,128]{1,0:T(8,128)S(1)} %add_select_fusion, bf16[4,15,15]{2,0,1:T(4,128)(2,1)} %param.7), kind=kOutput, calls=%fused_computation.5 | convolution fusion | flops 59473920 | bytes 4065032 | tf_op jit(solution)/shard_map/gab,jtb->gajt/dot_general | solution.py:31
  9.3 6.7 %copy.24 = bf16[256,128,4,15]{1,0,3,2:T(8,128)(2,1)} copy(bf16[256,128,4,15]{1,3,2,0:T(8,128)(2,1)} %fusion.3) | data formatting | bytes 7864320 | tf_op jit(solution)/shard_map/gab,jtb->gajt/dot_general | solution.py:31
  16.1 0.5 select_convert_fusion.edge_ref
  16.6 0.0 collective-permute-done.prev_ref
  16.6 0.0 copy-start.2
  16.6 0.0 collective-permute-done.1.next_ref
  16.6 0.0 copy-start.3
  16.6 0.7 %copy-done.2 = bf16[4,256,128]{2,1,0:T(8,128)(2,1)} copy-done((bf16[4,256,128]{2,1,0:T(8,128)(2,1)}, bf16[4,256,128]{2,1,0:T(8,128)(2,1)S(1)}, u32[]{:S(2)}) %copy-start.2) | copy-done | bytes 262168
  17.3 0.1 copy-done.3
  17.4 6.3 %shard_map.64 = bf16[128,2,640]{2,1,0:T(2,128)(2,1)} custom-call(s32[1,256]{1,0:T(1,128)} %bitcast.27, f32[1,128]{1,0:T(1,128)} %select_convert_fusion.edge_ref, s32[1,256]{1,0:T(1,128)} %live_ref.1, bf16[4,256,128]{2,1,0:T(8,128)(2,1)} %bitcast.26, bf16[4,256,128]{2,1,0:T(8,128)(2,1)} %copy-done.2, bf16[4,256,128]{2,1,0:T(8,128)(2,1)} %copy-done.3, ...), custom_call_target="tpu_custom_call" | custom-call | tf_op jit(solution)/shard_map/pallas_call | solution.py:114
  23.7 0.0 copy-start.4
  23.7 18.0 %all-to-all-start = ((bf16[128,2,640]{2,1,0:T(2,128)(2,1)}), bf16[128,2,640]{2,1,0:T(2,128)(2,1)S(1)}, u32[]{:S(2)}, u32[]{:S(2)}) async-start(bf16[128,2,640]{2,1,0:T(2,128)(2,1)} %shard_map.64), calls=%async_computation | async-start | bytes 655360 | tf_op jit(solution)/shard_map/all_to_all | solution.py:161
  41.7 0.0 copy-done
  41.7 0.6 fusion.1
  42.4 1.2 %copy.25 = bf16[256,128,15]{1,0,2:T(8,128)(2,1)} copy(bf16[256,128,15]{1,2,0:T(8,128)(2,1)S(1)} %fusion.1) | data formatting | bytes 1966080 | tf_op jit(solution)/shard_map/gab,jtb->gajt/dot_general | solution.py:31
  43.6 0.0 copy-done.4
  43.6 0.1 iota_add_fusion
  43.7 0.7 %add.51.target_ref = s32[1,256]{1,0:T(1,128)} reshape(s32[128,2]{1,0:T(8,128)S(1)} %iota_add_fusion) | data formatting | bytes 2048 | tf_op jit(solution)/shard_map/add | solution.py:163
  44.4 13.9 %all-to-all-done.data_ref = bf16[128,2,640]{2,1,0:T(2,128)(2,1)S(1)} async-done(((bf16[128,2,640]{2,1,0:T(2,128)(2,1)}), bf16[128,2,640]{2,1,0:T(2,128)(2,1)S(1)}, u32[]{:S(2)}, u32[]{:S(2)}) %all-to-all-start) | async-done | bytes 327712 | tf_op jit(solution)/shard_map/all_to_all | solution.py:161
  58.3 0.0 copy-start.1
  58.3 0.7 %copy-done.1 = bf16[128,2,640]{2,1,0:T(2,128)(2,1)} copy-done((bf16[128,2,640]{2,1,0:T(2,128)(2,1)}, bf16[128,2,640]{2,1,0:T(2,128)(2,1)S(1)}, u32[]{:S(2)}) %copy-start.1) | copy-done | bytes 327704
  59.0 4.8 %shard_map.65 = bf16[1024,128]{1,0:T(8,128)(2,1)} custom-call(s32[1,256]{1,0:T(1,128)} %add.51.target_ref, bf16[128,2,640]{2,1,0:T(2,128)(2,1)} %copy-done.1, bf16[1,15,256,128]{3,2,1,0:T(8,128)(2,1)} %bitcast.23), custom_call_target="tpu_custom_call" | custom-call | tf_op jit(solution)/shard_map/pallas_call | solution.py:136
  (1 shorter events, 0.0 us)
Async XLA Ops:
  0.0 41.7 %copy-start = (bf16[15,15]{1,0:T(8,128)(2,1)S(1)}, bf16[15,15]{1,0:T(8,128)(2,1)}, u32[]{:S(2)}) copy-start(bf16[15,15]{1,0:T(8,128)(2,1)} %param.8) | copy-start | bytes 1354
  0.0 16.6 %collective-permute-start = (bf16[4,256,128]{2,1,0:T(8,128)(2,1)}, bf16[4,256,128]{2,1,0:T(8,128)(2,1)S(1)}, u32[]{:S(2)}, u32[]{:S(2)}) collective-permute-start(bf16[4,256,128]{2,1,0:T(8,128)(2,1)} %bitcast.24), channel_id=1, source_target_pairs={{0,1},{1,2},{2,3},{4,5},{5,6},{6,7},{8,9},{9,10},{10,11},{12,13},{... | collective-permute-start | bytes 786440 | tf_op jit(solution)/shard_map/ppermute | solution.py:154
  4.1 12.5 %collective-permute-start.1 = (bf16[4,256,128]{2,1,0:T(8,128)(2,1)}, bf16[4,256,128]{2,1,0:T(8,128)(2,1)S(1)}, u32[]{:S(2)}, u32[]{:S(2)}) collective-permute-start(bf16[4,256,128]{2,1,0:T(8,128)(2,1)} %bitcast.25), channel_id=1, source_target_pairs={{1,0},{2,1},{3,2},{5,4},{6,5},{7,6},{9,8},{10,9},{11,10},{13,12},{... | collective-permute-start | bytes 786440 | tf_op jit(solution)/shard_map/ppermute | solution.py:155
  16.6 0.7 %copy-start.2 = (bf16[4,256,128]{2,1,0:T(8,128)(2,1)}, bf16[4,256,128]{2,1,0:T(8,128)(2,1)S(1)}, u32[]{:S(2)}) copy-start(bf16[4,256,128]{2,1,0:T(8,128)(2,1)S(1)} %collective-permute-done.prev_ref) | copy-start | bytes 786436
  16.6 0.8 %copy-start.3 = (bf16[4,256,128]{2,1,0:T(8,128)(2,1)}, bf16[4,256,128]{2,1,0:T(8,128)(2,1)S(1)}, u32[]{:S(2)}) copy-start(bf16[4,256,128]{2,1,0:T(8,128)(2,1)S(1)} %collective-permute-done.1.next_ref) | copy-start | bytes 786436
  23.7 19.9 %copy-start.4 = (s32[128]{0:T(128)S(1)}, s32[128]{0:T(128)}, u32[]{:S(2)}) copy-start(s32[128]{0:T(128)} %param.11) | copy-start | bytes 1540
  23.7 34.6 %all-to-all-start = ((bf16[128,2,640]{2,1,0:T(2,128)(2,1)}), bf16[128,2,640]{2,1,0:T(2,128)(2,1)S(1)}, u32[]{:S(2)}, u32[]{:S(2)}) async-start(bf16[128,2,640]{2,1,0:T(2,128)(2,1)} %shard_map.64), calls=%async_computation | async-start | bytes 655360 | tf_op jit(solution)/shard_map/all_to_all | solution.py:161
  58.3 0.7 %copy-start.1 = (bf16[128,2,640]{2,1,0:T(2,128)(2,1)}, bf16[128,2,640]{2,1,0:T(2,128)(2,1)S(1)}, u32[]{:S(2)}) copy-start(bf16[128,2,640]{2,1,0:T(2,128)(2,1)S(1)} %all-to-all-done.data_ref) | copy-start | bytes 983044

commit v12 on v10

--- a/solution.py
+++ b/solution.py
@@ -71,36 +71,33 @@
         out_ref[:, :, comps * samples:(comps + 1) * samples] = (halo_ref[...] * keep * edge_ref[...]).astype(out_ref.dtype).reshape(rows // 2, 2, samples)
 
 
-def dip_kernel(target_ref, data_ref, table_ref, out_ref, *, taps, group, comps):
-    rows = data_ref.shape[0] * data_ref.shape[1]
-    samples = LANES
+def dip_kernel(target_ref, main_ref, halo_ref, table_ref, out_ref, turned_ref, scr_ref, *, taps, comps):
+    c = pl.program_id(0)
+    devices, group, samples = main_ref.shape
+    rows = devices * group
     reach = (taps - 1) // 2
-    stride = comps * group
-    out_rows = out_ref.shape[0]
+    pad = 16
     target = target_ref[...]
-    row = lax.broadcasted_iota(jnp.int32, (out_rows, rows), 0)
-    halo = data_ref[:, :, comps * samples:(comps + 1) * samples].reshape(rows, samples).astype(jnp.float32)
-    selects, parts = [], []
-    for c in range(comps):
-        mine = pltpu.roll(halo, (samples - reach - 2 * reach * c) % samples, 1).astype(jnp.bfloat16)
-        parts.append(jnp.concatenate([data_ref[:, :, c * samples:(c + 1) * samples].reshape(rows, samples), mine], axis=1))
-        selects.append((row == target + group * c).astype(jnp.bfloat16))
-    gathered = jnp.dot(jnp.concatenate(selects, axis=1), jnp.concatenate(parts, axis=0), preferred_element_type=jnp.float32)
-    gathered = gathered.astype(jnp.bfloat16)
-    acc = jnp.zeros((out_rows, LANES), jnp.float32)
+    select = (lax.broadcasted_iota(jnp.int32, (rows, rows), 0) == target).astype(jnp.bfloat16)
+    halo = halo_ref[...].reshape(rows, samples).astype(jnp.float32)
+    for k in range(comps):
+        @pl.when(c == k)
+        def _():
+            turned_ref[...] = pltpu.roll(halo, (samples - reach - 2 * reach * k) % samples, 1).astype(jnp.bfloat16)
+
+    ext = jnp.concatenate([main_ref[...].reshape(rows, samples), turned_ref[...]], axis=1)
+    gathered = jnp.dot(select, ext, preferred_element_type=jnp.float32).astype(jnp.bfloat16)
+    zeros = jnp.zeros((pad, EXT), jnp.float32)
+    scr_ref[0:pad, :] = zeros
+    scr_ref[rows + pad:rows + 2 * pad, :] = zeros
+    acc = jnp.zeros((rows, LANES), jnp.float32)
     for first in range(0, taps, 2):
         pair = list(range(first, min(first + 2, taps)))
         tables = jnp.concatenate([table_ref[0, a] for a in pair], axis=1)
-        both = jnp.dot(gathered, tables, preferred_element_type=jnp.float32)
+        scr_ref[pad:rows + pad, 0:len(pair) * samples] = jnp.dot(gathered, tables, preferred_element_type=jnp.float32)
         for k, a in enumerate(pair):
-            part = both[:, k * samples:(k + 1) * samples]
-            shift = stride * (a - reach)
-            if shift > 0:
-                part = jnp.concatenate([part[shift:], jnp.zeros((shift, LANES), jnp.float32)], axis=0)
-            elif shift < 0:
-                part = jnp.concatenate([jnp.zeros((-shift, LANES), jnp.float32), part[:shift]], axis=0)
-            acc = acc + part
-    out_ref[...] = acc.astype(out_ref.dtype)
+            acc = acc + scr_ref[pl.ds(pad + group * (a - reach), rows), k * samples:(k + 1) * samples]
+    out_ref[:, 0, :, :] = acc.astype(out_ref.dtype).reshape(devices, group, samples)
 
 
 def fan_call(place, edge, ext, tables, live_col):
@@ -122,14 +119,24 @@
     )(place, edge, ext, tables)
 
 
-def dip_call(target, data, tables, group, comps):
-    rows = data.shape[0] * data.shape[1]
+def dip_call(target, data, tables, comps):
+    devices, group, _ = data.shape
     taps = tables.shape[1]
-    kernel = functools.partial(dip_kernel, taps=taps, group=group, comps=comps)
+    rows = devices * group
+    kernel = functools.partial(dip_kernel, taps=taps, comps=comps)
     return pl.pallas_call(
         kernel,
-        out_shape=jax.ShapeDtypeStruct((rows * comps, LANES), jnp.bfloat16),
-    )(target, data, tables)
+        grid=(comps,),
+        in_specs=[
+            pl.BlockSpec((1, rows), lambda c: (0, 0)),
+            pl.BlockSpec((devices, group, LANES), lambda c: (0, 0, c)),
+            pl.BlockSpec((devices, group, LANES), lambda c: (0, 0, comps)),
+            pl.BlockSpec((1, taps, EXT, LANES), lambda c: (0, 0, 0, 0)),
+        ],
+        out_specs=pl.BlockSpec((devices, 1, group, LANES), lambda c: (0, c, 0, 0)),
+        out_shape=jax.ShapeDtypeStruct((devices, comps, group, LANES), jnp.bfloat16),
+        scratch_shapes=[pltpu.VMEM((rows, LANES), jnp.bfloat16), pltpu.VMEM((rows + 32, EXT), jnp.float32)],
+    )(target, data, data, tables)
 
 
 def on_device(records, fan_taps, dip_taps, live_mask, node_place, shot_place):
@@ -153,10 +160,8 @@
     packed = fan_call(node_place[None, :], edge, ext, circulant(fan_taps, samples), live_col)
 
     data = lax.all_to_all(packed, "shot", split_axis=0, concat_axis=0, tiled=True)
-    spread = comps * group
-    target = (jnp.repeat(shot_place, group) * spread + jnp.tile(jnp.arange(group, dtype=jnp.int32), devices))[None, :]
-    out = dip_call(target, data, circulant(dip_taps[None], samples), group, comps)
-    return out.reshape(devices, comps, group, samples)
+    target = (jnp.repeat(shot_place, group) * group + jnp.tile(jnp.arange(group, dtype=jnp.int32), devices))[None, :]
+    return dip_call(target, data, circulant(dip_taps[None], samples), comps)
 
 
 def solution(mesh):

time: 63.7 us -> 64.1 us (level)
  no operation moved by 1% of the time
where the time goes in v12:
time: 64.1 us; the launch traced here: 63.7 us
  starting transfers between devices  24.4 us (38%)
  waiting for transfers between devices  13.9 us (22%)
  Pallas kernels  11.3 us (18%)
  local copies, waits for them, and re-layouts  9.95 us (16%)
  matrix products  2.58 us (4%)
  other arithmetic  1.37 us (2%)
    all_to_all x1, starting transfers between devices, on_device(): lax.all_to_all(packed, 'shot', split_axis=0, concat_axis=0, tiled=True)  18.5 us
    all_to_all x1, waiting for transfers between devices, on_device(): lax.all_to_all(packed, 'shot', split_axis=0, concat_axis=0, tiled=True)  13.9 us
    pallas_call x1, Pallas kernels, fan_call(): pl.pallas_call(kernel, grid=(comps,), in_specs=[pl.BlockSpec((1, rows), l...  6.24 us
    dot_general x2, local copies, waits for them, and re-layouts, circulant(): jnp.einsum('gab,jtb->gajt', tap_set, onehot, preferred_element_type=jnp.f...  5.76 us
    pallas_call x1, Pallas kernels, dip_call(): pl.pallas_call(kernel, grid=(comps,), in_specs=[pl.BlockSpec((1, rows), l...  5.09 us
    ppermute x1, starting transfers between devices, time_halo(): lax.ppermute(lax.slice_in_dim(block, samples - width, None, axis=-1), axi...  4.59 us
    dot_general x2, matrix products, circulant(): jnp.einsum('gab,jtb->gajt', tap_set, onehot, preferred_element_type=jnp.f...  2.58 us
    concatenate x1, local copies, waits for them, and re-layouts, on_device(): ext = jnp.concatenate([block, high, gap1, live, gap2, low], axis=-1)  1.36 us
  transfers between devices with their start and end apart: 3, of which 1 were waited for; matrix products, arithmetic and copies ran while one was open for 16% of the time, Pallas kernels for 0%

profile of v12, /device:TPU:1, one launch (start us, length us, event | category | flops | bytes accessed | tf_op | source)
XLA Modules:
  0.0 63.7 jit_solution(6872255769614313439)
XLA Ops:
  0.0 0.0 copy-start
  0.0 1.2 %fusion.12 = (bf16[4,256,14]{2,1,0:T(8,128)(2,1)S(1)}, bf16[4,256,14]{2,1,0:T(8,128)(2,1)S(1)}) fusion(bf16[4,256,128]{2,1,0:T(8,128)(2,1)} %bitcast.23), kind=kLoop, calls=%fused_computation.22 | loop fusion | bytes 114688 | tf_op jit(solution)/shard_map/slice | solution.py:19
  1.2 1.3 %collective-permute-start = (bf16[4,256,14]{2,1,0:T(8,128)(2,1)S(1)}, bf16[4,256,14]{2,1,0:T(8,128)(2,1)S(1)}, u32[]{:S(2)}, u32[]{:S(2)}) collective-permute-start(bf16[4,256,14]{2,1,0:T(8,128)(2,1)S(1)} %get-tuple-element.6), channel_id=1, source_target_pairs={{1,0},{2,1},{3,2},{5,4},{6,5},{7,6},{9,8},{10,9},{11,10},{13,12},{... | collective-permute-start | bytes 86024 | tf_op jit(solution)/shard_map/ppermute | solution.py:20
  2.5 4.6 %collective-permute-start.1 = (bf16[4,256,14]{2,1,0:T(8,128)(2,1)S(1)}, bf16[4,256,14]{2,1,0:T(8,128)(2,1)S(1)}, u32[]{:S(2)}, u32[]{:S(2)}) collective-permute-start(bf16[4,256,14]{2,1,0:T(8,128)(2,1)S(1)} %get-tuple-element.5), channel_id=1, source_target_pairs={{0,1},{1,2},{2,3},{4,5},{5,6},{6,7},{8,9},{9,10},{10,11},{12,13},{... | collective-permute-start | bytes 86024 | tf_op jit(solution)/shard_map/ppermute | solution.py:19
  7.1 0.1 add_select_fusion
  7.2 0.7 %convert_reduce_fusion = bf16[256]{0:T(256)(128)(2,1)S(1)} fusion(s32[1,256]{1,0:T(1,128)} %param.9), kind=kLoop, calls=%fused_computation.20 | loop fusion | flops 256 | bytes 1536 | tf_op jit(solution)/shard_map/convert_element_type | solution.py:153
  7.9 2.0 %fusion.3 = bf16[256,128,4,15]{1,3,2,0:T(8,128)(2,1)S(1)} fusion(s32[256,128]{1,0:T(8,128)S(1)} %add_select_fusion, bf16[4,15,15]{2,0,1:T(4,128)(2,1)} %param.7), kind=kOutput, calls=%fused_computation.5 | convolution fusion | flops 59473920 | bytes 4065032 | tf_op jit(solution)/shard_map/gab,jtb->gajt/dot_general | solution.py:31
  9.8 0.5 select_convert_fusion.edge_ref
  10.4 0.0 copy-start.2
  10.4 4.5 %copy.24 = bf16[256,128,4,15]{1,0,3,2:T(8,128)(2,1)} copy(bf16[256,128,4,15]{1,3,2,0:T(8,128)(2,1)S(1)} %fusion.3) | data formatting | bytes 7864320 | tf_op jit(solution)/shard_map/gab,jtb->gajt/dot_general | solution.py:31
  14.9 0.0 collective-permute-done
  14.9 0.0 collective-permute-done.1
  14.9 0.1 broadcast_in_dim.42
  15.1 0.0 copy-done.2
  15.1 1.4 %concatenate.3.ext_ref = bf16[4,256,256]{2,1,0:T(8,128)(2,1)} concatenate(bf16[4,256,128]{2,1,0:T(8,128)(2,1)S(1)} %bitcast.24, bf16[4,256,14]{2,1,0:T(8,128)(2,1)S(1)} %collective-permute-done, bf16[4,256,18]{2,1,0:T(8,128)(2,1)S(1)} %broadcast_in_dim.22, bf16[4,256,1]{2,1,0:T(8,128)(2,1)S(1)} %broadcast_in_dim.42, bf16[4,256,81]{2,1,0:T(8,128)(2,1)S(1)} %broadcast_in_dim.43, ...), dimensions={2} | concatenate | bytes 1048576 | tf_op jit(solution)/shard_map/concatenate | solution.py:156
  16.5 6.2 %shard_map.64 = bf16[128,2,640]{2,1,0:T(2,128)(2,1)} custom-call(s32[1,256]{1,0:T(1,128)} %bitcast.25, f32[1,128]{1,0:T(1,128)} %select_convert_fusion.edge_ref, bf16[4,256,256]{2,1,0:T(8,128)(2,1)} %concatenate.3.ext_ref, bf16[4,15,256,128]{3,2,1,0:T(8,128)(2,1)} %bitcast.21), custom_call_target="tpu_custom_call" | custom-call | tf_op jit(solution)/shard_map/pallas_call | solution.py:107
  22.7 0.0 copy-start.3
  22.7 18.5 %all-to-all-start = ((bf16[128,2,640]{2,1,0:T(2,128)(2,1)}), bf16[128,2,640]{2,1,0:T(2,128)(2,1)S(1)}, u32[]{:S(2)}, u32[]{:S(2)}) async-start(bf16[128,2,640]{2,1,0:T(2,128)(2,1)} %shard_map.64), calls=%async_computation | async-start | bytes 655360 | tf_op jit(solution)/shard_map/all_to_all | solution.py:162
  41.3 0.0 copy-done
  41.3 0.6 fusion.1
  41.9 1.2 %copy.25 = bf16[256,128,15]{1,0,2:T(8,128)(2,1)} copy(bf16[256,128,15]{1,2,0:T(8,128)(2,1)S(1)} %fusion.1) | data formatting | bytes 1966080 | tf_op jit(solution)/shard_map/gab,jtb->gajt/dot_general | solution.py:31
  43.1 0.0 copy-done.3
  43.1 0.1 iota_add_fusion
  43.2 0.7 %add.51.target_ref = s32[1,256]{1,0:T(1,128)} reshape(s32[128,2]{1,0:T(8,128)S(1)} %iota_add_fusion) | data formatting | bytes 2048 | tf_op jit(solution)/shard_map/add | solution.py:163
  43.9 13.9 %all-to-all-done.main_ref.halo_ref = bf16[128,2,640]{2,1,0:T(2,128)(2,1)S(1)} async-done(((bf16[128,2,640]{2,1,0:T(2,128)(2,1)}), bf16[128,2,640]{2,1,0:T(2,128)(2,1)S(1)}, u32[]{:S(2)}, u32[]{:S(2)}) %all-to-all-start) | async-done | bytes 327712 | tf_op jit(solution)/shard_map/all_to_all | solution.py:162
  57.8 0.0 copy-start.1
  57.8 0.7 %copy-done.1 = bf16[128,2,640]{2,1,0:T(2,128)(2,1)} copy-done((bf16[128,2,640]{2,1,0:T(2,128)(2,1)}, bf16[128,2,640]{2,1,0:T(2,128)(2,1)S(1)}, u32[]{:S(2)}) %copy-start.1) | copy-done | bytes 327704
  58.6 5.1 %shard_map.65 = bf16[128,4,2,128]{3,2,1,0:T(2,128)(2,1)} custom-call(s32[1,256]{1,0:T(1,128)} %add.51.target_ref, bf16[128,2,640]{2,1,0:T(2,128)(2,1)} %copy-done.1, bf16[128,2,640]{2,1,0:T(2,128)(2,1)} %copy-done.1, bf16[1,15,256,128]{3,2,1,0:T(8,128)(2,1)} %bitcast.22), custom_call_target="tpu_custom_call" | custom-call | tf_op jit(solution)/shard_map/pallas_call | solution.py:127
  (3 shorter events, 0.1 us)
Async XLA Ops:
  0.0 41.3 %copy-start = (bf16[15,15]{1,0:T(8,128)(2,1)S(1)}, bf16[15,15]{1,0:T(8,128)(2,1)}, u32[]{:S(2)}) copy-start(bf16[15,15]{1,0:T(8,128)(2,1)} %param.8) | copy-start | bytes 1354
  1.2 13.7 %collective-permute-start = (bf16[4,256,14]{2,1,0:T(8,128)(2,1)S(1)}, bf16[4,256,14]{2,1,0:T(8,128)(2,1)S(1)}, u32[]{:S(2)}, u32[]{:S(2)}) collective-permute-start(bf16[4,256,14]{2,1,0:T(8,128)(2,1)S(1)} %get-tuple-element.6), channel_id=1, source_target_pairs={{1,0},{2,1},{3,2},{5,4},{6,5},{7,6},{9,8},{10,9},{11,10},{13,12},{... | collective-permute-start | bytes 86024 | tf_op jit(solution)/shard_map/ppermute | solution.py:20
  2.5 12.4 %collective-permute-start.1 = (bf16[4,256,14]{2,1,0:T(8,128)(2,1)S(1)}, bf16[4,256,14]{2,1,0:T(8,128)(2,1)S(1)}, u32[]{:S(2)}, u32[]{:S(2)}) collective-permute-start(bf16[4,256,14]{2,1,0:T(8,128)(2,1)S(1)} %get-tuple-element.5), channel_id=1, source_target_pairs={{0,1},{1,2},{2,3},{4,5},{5,6},{6,7},{8,9},{9,10},{10,11},{12,13},{... | collective-permute-start | bytes 86024 | tf_op jit(solution)/shard_map/ppermute | solution.py:19
  10.4 4.7 %copy-start.2 = (bf16[1,4,256,128]{3,2,1,0:T(8,128)(2,1)S(1)}, bf16[1,4,256,128]{3,2,1,0:T(8,128)(2,1)}, u32[]{:S(2)}) copy-start(bf16[1,4,256,128]{3,2,1,0:T(8,128)(2,1)} %param.6) | copy-start | bytes 786436
  22.7 20.4 %copy-start.3 = (s32[128]{0:T(128)S(1)}, s32[128]{0:T(128)}, u32[]{:S(2)}) copy-start(s32[128]{0:T(128)} %param.11) | copy-start | bytes 1540
  22.7 35.1 %all-to-all-start = ((bf16[128,2,640]{2,1,0:T(2,128)(2,1)}), bf16[128,2,640]{2,1,0:T(2,128)(2,1)S(1)}, u32[]{:S(2)}, u32[]{:S(2)}) async-start(bf16[128,2,640]{2,1,0:T(2,128)(2,1)} %shard_map.64), calls=%async_computation | async-start | bytes 655360 | tf_op jit(solution)/shard_map/all_to_all | solution.py:162
  57.8 0.7 %copy-start.1 = (bf16[128,2,640]{2,1,0:T(2,128)(2,1)}, bf16[128,2,640]{2,1,0:T(2,128)(2,1)S(1)}, u32[]{:S(2)}) copy-start(bf16[128,2,640]{2,1,0:T(2,128)(2,1)S(1)} %all-to-all-done.main_ref.halo_ref) | copy-start | bytes 983044

commit v13 on v10

--- a/solution.py
+++ b/solution.py
@@ -32,6 +32,16 @@
     return tables.astype(jnp.bfloat16)
 
 
+def fan_tables(tap_set, samples):
+    taps = tap_set.shape[-1]
+    reach = (taps - 1) // 2
+    j = jnp.arange(EXT, dtype=jnp.int32)
+    t = jnp.arange(samples, dtype=jnp.int32)
+    b = (j[:, None] - t[None, :] + reach) % EXT
+    onehot = (b[:, :, None] == jnp.arange(taps, dtype=jnp.int32)[None, None, :]).astype(jnp.bfloat16)
+    return jnp.einsum("gab,jtb->jgat", tap_set, onehot, preferred_element_type=jnp.float32)
+
+
 def fan_kernel(place_ref, edge_ref, ext_ref, table_ref, out_ref, scr_ref, halo_ref, *, taps, live_col, comps):
     c = pl.program_id(0)
     rows = ext_ref.shape[1]
@@ -48,7 +58,7 @@
     acc = jnp.zeros((rows, LANES), jnp.float32)
     acc_h = jnp.zeros((rows, LANES), jnp.float32)
     for a in range(taps):
-        table = table_ref[0, a]
+        table = table_ref[:, 0, a, :].astype(jnp.bfloat16)
         both = jnp.concatenate([table, jnp.concatenate([table[samples:], table[:samples]], axis=0)], axis=1)
         moved = scr_ref[pl.ds(a + 8 - reach, rows), :].astype(jnp.bfloat16)
         part = jnp.dot(moved, both, preferred_element_type=jnp.float32)
@@ -105,7 +115,7 @@
 
 def fan_call(place, edge, ext, tables, live_col):
     comps, rows, _ = ext.shape
-    taps = tables.shape[1]
+    taps = tables.shape[2]
     kernel = functools.partial(fan_kernel, taps=taps, live_col=live_col, comps=comps)
     return pl.pallas_call(
         kernel,
@@ -114,7 +124,7 @@
             pl.BlockSpec((1, rows), lambda c: (0, 0)),
             pl.BlockSpec((1, LANES), lambda c: (0, 0)),
             pl.BlockSpec((1, rows, EXT), lambda c: (c, 0, 0)),
-            pl.BlockSpec((1, taps, EXT, LANES), lambda c: (c, 0, 0, 0)),
+            pl.BlockSpec((EXT, 1, taps, LANES), lambda c: (0, c, 0, 0)),
         ],
         out_specs=pl.BlockSpec((rows // 2, 2, (comps + 1) * LANES), lambda c: (0, 0, 0)),
         out_shape=jax.ShapeDtypeStruct((rows // 2, 2, (comps + 1) * LANES), jnp.bfloat16),
@@ -150,7 +160,7 @@
     place = lax.axis_index("tm")
     lane = jnp.arange(LANES, dtype=jnp.int32) % wide
     edge = jnp.where(lane < reach, place > 0, place < lax.axis_size("tm") - 1).astype(jnp.float32)[None, :]
-    packed = fan_call(node_place[None, :], edge, ext, circulant(fan_taps, samples), live_col)
+    packed = fan_call(node_place[None, :], edge, ext, fan_tables(fan_taps, samples), live_col)
 
     data = lax.all_to_all(packed, "shot", split_axis=0, concat_axis=0, tiled=True)
     spread = comps * group

time: 63.7 us -> 69.2 us (1.086)
  Pallas kernels: 11.1 us -> 17.8 us
  local copies, waits for them, and re-layouts: 9.92 us -> 5.39 us
  matrix products: 2.58 us -> 5.85 us
    pallas_call x1, Pallas kernels: 6.25 us -> 13 us  [fan_call(): pl.pallas_call(kernel, grid=(comps,), in_specs=[pl.BlockSpec((1, rows), l...]
    dot_general x0 -> x1, matrix products: none -> 5.22 us  [fan_tables(): jnp.einsum('gab,jtb->jgat', tap_set, onehot, preferred_element_type=jnp.f...]
    dot_general x2 -> x1, local copies, waits for them, and re-layouts: 5.76 us -> 1.22 us  [circulant(): jnp.einsum('gab,jtb->gajt', tap_set, onehot, preferred_element_type=jnp.f...]
    dot_general x2 -> x1, matrix products: 2.58 us -> 0.63 us  [circulant(): jnp.einsum('gab,jtb->gajt', tap_set, onehot, preferred_element_type=jnp.f...]
  transfers between devices with their start and end apart: 3 -> 3, of which waited for: 1 -> 1; matrix products, arithmetic and copies ran while one was open for 16% -> 13% of each run, Pallas kernels for 0% -> 0%
where the time goes in v13:
time: 69.2 us; the launch traced here: 68.9 us
  starting transfers between devices  24.4 us (35%)
  Pallas kernels  17.8 us (26%)
  waiting for transfers between devices  13.9 us (20%)
  matrix products  5.85 us (8%)
  local copies, waits for them, and re-layouts  5.39 us (8%)
  other arithmetic  1.36 us (2%)
    all_to_all x1, starting transfers between devices, on_device(): lax.all_to_all(packed, 'shot', split_axis=0, concat_axis=0, tiled=True)  18.5 us
    all_to_all x1, waiting for transfers between devices, on_device(): lax.all_to_all(packed, 'shot', split_axis=0, concat_axis=0, tiled=True)  13.9 us
    pallas_call x1, Pallas kernels, fan_call(): pl.pallas_call(kernel, grid=(comps,), in_specs=[pl.BlockSpec((1, rows), l...  13 us
    dot_general x1, matrix products, fan_tables(): jnp.einsum('gab,jtb->jgat', tap_set, onehot, preferred_element_type=jnp.f...  5.22 us
    pallas_call x1, Pallas kernels, dip_call(): pl.pallas_call(kernel, out_shape=jax.ShapeDtypeStruct((rows * comps, LANE...  4.81 us
    ppermute x1, starting transfers between devices, time_halo(): lax.ppermute(lax.slice_in_dim(block, samples - width, None, axis=-1), axi...  4.59 us
  transfers between devices with their start and end apart: 3, of which 1 were waited for; matrix products, arithmetic and copies ran while one was open for 13% of the time, Pallas kernels for 0%

profile of v13, /device:TPU:1, one launch (start us, length us, event | category | flops | bytes accessed | tf_op | source)
XLA Modules:
  0.0 68.9 jit_solution(3300382534603756269)
XLA Ops:
  0.0 0.0 copy-start
  0.0 1.2 %fusion.10 = (bf16[4,256,14]{2,1,0:T(8,128)(2,1)S(1)}, bf16[4,256,14]{2,1,0:T(8,128)(2,1)S(1)}) fusion(bf16[4,256,128]{2,1,0:T(8,128)(2,1)} %bitcast.22), kind=kLoop, calls=%fused_computation.20 | loop fusion | bytes 114688 | tf_op jit(solution)/shard_map/slice | solution.py:19
  1.2 1.3 %collective-permute-start = (bf16[4,256,14]{2,1,0:T(8,128)(2,1)S(1)}, bf16[4,256,14]{2,1,0:T(8,128)(2,1)S(1)}, u32[]{:S(2)}, u32[]{:S(2)}) collective-permute-start(bf16[4,256,14]{2,1,0:T(8,128)(2,1)S(1)} %get-tuple-element.6), channel_id=1, source_target_pairs={{1,0},{2,1},{3,2},{5,4},{6,5},{7,6},{9,8},{10,9},{11,10},{13,12},{... | collective-permute-start | bytes 86024 | tf_op jit(solution)/shard_map/ppermute | solution.py:20
  2.5 4.6 %collective-permute-start.1 = (bf16[4,256,14]{2,1,0:T(8,128)(2,1)S(1)}, bf16[4,256,14]{2,1,0:T(8,128)(2,1)S(1)}, u32[]{:S(2)}, u32[]{:S(2)}) collective-permute-start(bf16[4,256,14]{2,1,0:T(8,128)(2,1)S(1)} %get-tuple-element.5), channel_id=1, source_target_pairs={{0,1},{1,2},{2,3},{4,5},{5,6},{6,7},{8,9},{9,10},{10,11},{12,13},{... | collective-permute-start | bytes 86024 | tf_op jit(solution)/shard_map/ppermute | solution.py:19
  7.1 0.1 add_select_fusion
  7.1 0.7 %convert_reduce_fusion = bf16[256]{0:T(256)(128)(2,1)S(1)} fusion(s32[1,256]{1,0:T(1,128)} %param.9), kind=kLoop, calls=%fused_computation.18 | loop fusion | flops 256 | bytes 1536 | tf_op jit(solution)/shard_map/convert_element_type | solution.py:156
  7.8 0.0 copy-start.1
  7.8 5.2 %convolution_bitcast_fusion.table_ref = f32[256,4,15,128]{3,2,1,0:T(8,128)} fusion(s32[256,128]{1,0:T(8,128)S(1)} %add_select_fusion, bf16[4,15,15]{2,0,1:T(4,128)(2,1)} %param.7), kind=kOutput, calls=%fused_computation | convolution fusion | flops 59473920 | bytes 7997192 | tf_op jit(solution)/shard_map/gab,jtb->jgat/dot_general | solution.py:42
  13.1 0.5 select_convert_fusion.edge_ref
  13.6 0.0 collective-permute-done
  13.6 0.0 collective-permute-done.1
  13.6 0.1 broadcast_in_dim.42
  13.8 0.0 copy-done.1
  13.8 1.4 %concatenate.3.ext_ref = bf16[4,256,256]{2,1,0:T(8,128)(2,1)} concatenate(bf16[4,256,128]{2,1,0:T(8,128)(2,1)S(1)} %bitcast.23, bf16[4,256,14]{2,1,0:T(8,128)(2,1)S(1)} %collective-permute-done, bf16[4,256,18]{2,1,0:T(8,128)(2,1)S(1)} %broadcast_in_dim.22, bf16[4,256,1]{2,1,0:T(8,128)(2,1)S(1)} %broadcast_in_dim.42, bf16[4,256,81]{2,1,0:T(8,128)(2,1)S(1)} %broadcast_in_dim.43, ...), dimensions={2} | concatenate | bytes 1048576 | tf_op jit(solution)/shard_map/concatenate | solution.py:159
  15.2 13.0 %shard_map.64 = bf16[128,2,640]{2,1,0:T(2,128)(2,1)} custom-call(s32[1,256]{1,0:T(1,128)} %bitcast.24, f32[1,128]{1,0:T(1,128)} %select_convert_fusion.edge_ref, bf16[4,256,256]{2,1,0:T(8,128)(2,1)} %concatenate.3.ext_ref, f32[256,4,15,128]{3,2,1,0:T(8,128)} %convolution_bitcast_fusion.table_ref), custom_call_target="tpu_custom_call" | custom-call | tf_op jit(solution)/shard_map/pallas_call | solution.py:120
  28.2 0.0 copy-start.3
  28.2 18.5 %all-to-all-start = ((bf16[128,2,640]{2,1,0:T(2,128)(2,1)}), bf16[128,2,640]{2,1,0:T(2,128)(2,1)S(1)}, u32[]{:S(2)}, u32[]{:S(2)}) async-start(bf16[128,2,640]{2,1,0:T(2,128)(2,1)} %shard_map.64), calls=%async_computation | async-start | bytes 655360 | tf_op jit(solution)/shard_map/all_to_all | solution.py:165
  46.7 0.0 copy-done
  46.7 0.6 fusion
  47.4 1.2 %copy.19 = bf16[256,128,15]{1,0,2:T(8,128)(2,1)} copy(bf16[256,128,15]{1,2,0:T(8,128)(2,1)S(1)} %fusion) | data formatting | bytes 1966080 | tf_op jit(solution)/shard_map/gab,jtb->gajt/dot_general | solution.py:31
  48.6 0.0 copy-done.3
  48.6 0.1 iota_add_fusion
  48.7 0.7 %add.51.target_ref = s32[1,256]{1,0:T(1,128)} reshape(s32[128,2]{1,0:T(8,128)S(1)} %iota_add_fusion) | data formatting | bytes 2048 | tf_op jit(solution)/shard_map/add | solution.py:167
  49.4 13.9 %all-to-all-done.data_ref = bf16[128,2,640]{2,1,0:T(2,128)(2,1)S(1)} async-done(((bf16[128,2,640]{2,1,0:T(2,128)(2,1)}), bf16[128,2,640]{2,1,0:T(2,128)(2,1)S(1)}, u32[]{:S(2)}, u32[]{:S(2)}) %all-to-all-start) | async-done | bytes 327712 | tf_op jit(solution)/shard_map/all_to_all | solution.py:165
  63.3 0.0 copy-start.2
  63.3 0.7 %copy-done.2 = bf16[128,2,640]{2,1,0:T(2,128)(2,1)} copy-done((bf16[128,2,640]{2,1,0:T(2,128)(2,1)}, bf16[128,2,640]{2,1,0:T(2,128)(2,1)S(1)}, u32[]{:S(2)}) %copy-start.2) | copy-done | bytes 327704
  64.0 4.8 %shard_map.65 = bf16[1024,128]{1,0:T(8,128)(2,1)} custom-call(s32[1,256]{1,0:T(1,128)} %add.51.target_ref, bf16[128,2,640]{2,1,0:T(2,128)(2,1)} %copy-done.2, bf16[1,15,256,128]{3,2,1,0:T(8,128)(2,1)} %bitcast.21), custom_call_target="tpu_custom_call" | custom-call | tf_op jit(solution)/shard_map/pallas_call | solution.py:139
  (3 shorter events, 0.1 us)
Async XLA Ops:
  0.0 46.7 %copy-start = (bf16[15,15]{1,0:T(8,128)(2,1)S(1)}, bf16[15,15]{1,0:T(8,128)(2,1)}, u32[]{:S(2)}) copy-start(bf16[15,15]{1,0:T(8,128)(2,1)} %param.8) | copy-start | bytes 1354
  1.2 12.4 %collective-permute-start = (bf16[4,256,14]{2,1,0:T(8,128)(2,1)S(1)}, bf16[4,256,14]{2,1,0:T(8,128)(2,1)S(1)}, u32[]{:S(2)}, u32[]{:S(2)}) collective-permute-start(bf16[4,256,14]{2,1,0:T(8,128)(2,1)S(1)} %get-tuple-element.6), channel_id=1, source_target_pairs={{1,0},{2,1},{3,2},{5,4},{6,5},{7,6},{9,8},{10,9},{11,10},{13,12},{... | collective-permute-start | bytes 86024 | tf_op jit(solution)/shard_map/ppermute | solution.py:20
  2.5 11.1 %collective-permute-start.1 = (bf16[4,256,14]{2,1,0:T(8,128)(2,1)S(1)}, bf16[4,256,14]{2,1,0:T(8,128)(2,1)S(1)}, u32[]{:S(2)}, u32[]{:S(2)}) collective-permute-start(bf16[4,256,14]{2,1,0:T(8,128)(2,1)S(1)} %get-tuple-element.5), channel_id=1, source_target_pairs={{0,1},{1,2},{2,3},{4,5},{5,6},{6,7},{8,9},{9,10},{10,11},{12,13},{... | collective-permute-start | bytes 86024 | tf_op jit(solution)/shard_map/ppermute | solution.py:19
  7.8 6.0 %copy-start.1 = (bf16[1,4,256,128]{3,2,1,0:T(8,128)(2,1)S(1)}, bf16[1,4,256,128]{3,2,1,0:T(8,128)(2,1)}, u32[]{:S(2)}) copy-start(bf16[1,4,256,128]{3,2,1,0:T(8,128)(2,1)} %param.6) | copy-start | bytes 786436
  28.2 20.4 %copy-start.3 = (s32[128]{0:T(128)S(1)}, s32[128]{0:T(128)}, u32[]{:S(2)}) copy-start(s32[128]{0:T(128)} %param.11) | copy-start | bytes 1540
  28.2 35.1 %all-to-all-start = ((bf16[128,2,640]{2,1,0:T(2,128)(2,1)}), bf16[128,2,640]{2,1,0:T(2,128)(2,1)S(1)}, u32[]{:S(2)}, u32[]{:S(2)}) async-start(bf16[128,2,640]{2,1,0:T(2,128)(2,1)} %shard_map.64), calls=%async_computation | async-start | bytes 655360 | tf_op jit(solution)/shard_map/all_to_all | solution.py:165
  63.3 0.7 %copy-start.2 = (bf16[128,2,640]{2,1,0:T(2,128)(2,1)}, bf16[128,2,640]{2,1,0:T(2,128)(2,1)S(1)}, u32[]{:S(2)}) copy-start(bf16[128,2,640]{2,1,0:T(2,128)(2,1)S(1)} %all-to-all-done.data_ref) | copy-start | bytes 983044

commit v14 on v10

--- a/solution.py
+++ b/solution.py
@@ -71,21 +71,18 @@
         out_ref[:, :, comps * samples:(comps + 1) * samples] = (halo_ref[...] * keep * edge_ref[...]).astype(out_ref.dtype).reshape(rows // 2, 2, samples)
 
 
-def dip_kernel(target_ref, data_ref, table_ref, out_ref, *, taps, group, comps):
+def dip_kernel(select_ref, data_ref, table_ref, out_ref, *, taps, group, comps):
     rows = data_ref.shape[0] * data_ref.shape[1]
     samples = LANES
     reach = (taps - 1) // 2
     stride = comps * group
     out_rows = out_ref.shape[0]
-    target = target_ref[...]
-    row = lax.broadcasted_iota(jnp.int32, (out_rows, rows), 0)
     halo = data_ref[:, :, comps * samples:(comps + 1) * samples].reshape(rows, samples).astype(jnp.float32)
-    selects, parts = [], []
+    parts = []
     for c in range(comps):
         mine = pltpu.roll(halo, (samples - reach - 2 * reach * c) % samples, 1).astype(jnp.bfloat16)
         parts.append(jnp.concatenate([data_ref[:, :, c * samples:(c + 1) * samples].reshape(rows, samples), mine], axis=1))
-        selects.append((row == target + group * c).astype(jnp.bfloat16))
-    gathered = jnp.dot(jnp.concatenate(selects, axis=1), jnp.concatenate(parts, axis=0), preferred_element_type=jnp.float32)
+    gathered = jnp.dot(select_ref[...], jnp.concatenate(parts, axis=0), preferred_element_type=jnp.float32)
     gathered = gathered.astype(jnp.bfloat16)
     acc = jnp.zeros((out_rows, LANES), jnp.float32)
     for first in range(0, taps, 2):
@@ -122,14 +119,14 @@
     )(place, edge, ext, tables)
 
 
-def dip_call(target, data, tables, group, comps):
+def dip_call(select, data, tables, group, comps):
     rows = data.shape[0] * data.shape[1]
     taps = tables.shape[1]
     kernel = functools.partial(dip_kernel, taps=taps, group=group, comps=comps)
     return pl.pallas_call(
         kernel,
         out_shape=jax.ShapeDtypeStruct((rows * comps, LANES), jnp.bfloat16),
-    )(target, data, tables)
+    )(select, data, tables)
 
 
 def on_device(records, fan_taps, dip_taps, live_mask, node_place, shot_place):
@@ -155,7 +152,9 @@
     data = lax.all_to_all(packed, "shot", split_axis=0, concat_axis=0, tiled=True)
     spread = comps * group
     target = (jnp.repeat(shot_place, group) * spread + jnp.tile(jnp.arange(group, dtype=jnp.int32), devices))[None, :]
-    out = dip_call(target, data, circulant(dip_taps[None], samples), group, comps)
+    row = jnp.arange(devices * spread, dtype=jnp.int32)[:, None]
+    select = jnp.concatenate([(row == target + group * c).astype(jnp.bfloat16) for c in range(comps)], axis=1)
+    out = dip_call(select, data, circulant(dip_taps[None], samples), group, comps)
     return out.reshape(devices, comps, group, samples)
 
 

time: 63.7 us -> 66.9 us (1.050)
  other arithmetic: 1.37 us -> 4.52 us
    concatenate x0 -> x1, other arithmetic: none -> 1.86 us  [on_device(): jnp.concatenate([(row == target + group * c).astype(jnp.bfloat16) for c i...]
  transfers between devices with their start and end apart: 3 -> 3, of which waited for: 1 -> 1; matrix products, arithmetic and copies ran while one was open for 16% -> 19% of each run, Pallas kernels for 0% -> 0%
where the time goes in v14:
time: 66.9 us; the launch traced here: 66.6 us
  starting transfers between devices  24.3 us (36%)
  waiting for transfers between devices  14.1 us (21%)
  Pallas kernels  11.7 us (17%)
  local copies, waits for them, and re-layouts  9.29 us (14%)
  other arithmetic  4.52 us (7%)
  matrix products  2.58 us (4%)
    all_to_all x1, starting transfers between devices, on_device(): lax.all_to_all(packed, 'shot', split_axis=0, concat_axis=0, tiled=True)  18.4 us
    all_to_all x1, waiting for transfers between devices, on_device(): lax.all_to_all(packed, 'shot', split_axis=0, concat_axis=0, tiled=True)  14.1 us
    pallas_call x1, Pallas kernels, fan_call(): pl.pallas_call(kernel, grid=(comps,), in_specs=[pl.BlockSpec((1, rows), l...  6.25 us
    dot_general x2, local copies, waits for them, and re-layouts, circulant(): jnp.einsum('gab,jtb->gajt', tap_set, onehot, preferred_element_type=jnp.f...  5.74 us
    pallas_call x1, Pallas kernels, dip_call(): pl.pallas_call(kernel, out_shape=jax.ShapeDtypeStruct((rows * comps, LANE...  5.44 us
    ppermute x1, starting transfers between devices, time_halo(): lax.ppermute(lax.slice_in_dim(block, samples - width, None, axis=-1), axi...  4.59 us
    dot_general x2, matrix products, circulant(): jnp.einsum('gab,jtb->gajt', tap_set, onehot, preferred_element_type=jnp.f...  2.58 us
    concatenate x1, other arithmetic, on_device(): jnp.concatenate([(row == target + group * c).astype(jnp.bfloat16) for c i...  1.86 us
  transfers between devices with their start and end apart: 3, of which 1 were waited for; matrix products, arithmetic and copies ran while one was open for 19% of the time, Pallas kernels for 0%

profile of v14, /device:TPU:1, one launch (start us, length us, event | category | flops | bytes accessed | tf_op | source)
XLA Modules:
  0.0 66.6 jit_solution(5958684134809750179)
XLA Ops:
  0.0 0.0 copy-start
  0.0 1.2 %fusion.12 = (bf16[4,256,14]{2,1,0:T(8,128)(2,1)S(1)}, bf16[4,256,14]{2,1,0:T(8,128)(2,1)S(1)}) fusion(bf16[4,256,128]{2,1,0:T(8,128)(2,1)} %bitcast.24), kind=kLoop, calls=%fused_computation.30 | loop fusion | bytes 114688 | tf_op jit(solution)/shard_map/slice | solution.py:19
  1.2 1.3 %collective-permute-start = (bf16[4,256,14]{2,1,0:T(8,128)(2,1)S(1)}, bf16[4,256,14]{2,1,0:T(8,128)(2,1)S(1)}, u32[]{:S(2)}, u32[]{:S(2)}) collective-permute-start(bf16[4,256,14]{2,1,0:T(8,128)(2,1)S(1)} %get-tuple-element.6), channel_id=1, source_target_pairs={{1,0},{2,1},{3,2},{5,4},{6,5},{7,6},{9,8},{10,9},{11,10},{13,12},{... | collective-permute-start | bytes 86024 | tf_op jit(solution)/shard_map/ppermute | solution.py:20
  2.5 4.6 %collective-permute-start.1 = (bf16[4,256,14]{2,1,0:T(8,128)(2,1)S(1)}, bf16[4,256,14]{2,1,0:T(8,128)(2,1)S(1)}, u32[]{:S(2)}, u32[]{:S(2)}) collective-permute-start(bf16[4,256,14]{2,1,0:T(8,128)(2,1)S(1)} %get-tuple-element.5), channel_id=1, source_target_pairs={{0,1},{1,2},{2,3},{4,5},{5,6},{6,7},{8,9},{9,10},{10,11},{12,13},{... | collective-permute-start | bytes 86024 | tf_op jit(solution)/shard_map/ppermute | solution.py:19
  7.1 0.1 add_select_fusion
  7.1 0.7 broadcast_multiply_fusion
  7.8 0.1 iota_add_fusion
  7.9 0.1 add.90
  8.0 0.7 %convert_reduce_fusion = bf16[256]{0:T(256)(128)(2,1)S(1)} fusion(s32[1,256]{1,0:T(1,128)} %param.9), kind=kLoop, calls=%fused_computation.25 | loop fusion | flops 256 | bytes 1536 | tf_op jit(solution)/shard_map/convert_element_type | solution.py:143
  8.7 2.0 %fusion.3 = bf16[256,128,4,15]{1,3,2,0:T(8,128)(2,1)S(1)} fusion(s32[256,128]{1,0:T(8,128)S(1)} %add_select_fusion, bf16[4,15,15]{2,0,1:T(4,128)(2,1)} %param.7), kind=kOutput, calls=%fused_computation.6 | convolution fusion | flops 59473920 | bytes 4065032 | tf_op jit(solution)/shard_map/gab,jtb->gajt/dot_general | solution.py:31
  10.7 0.0 copy-done
  10.7 0.6 fusion.1
  11.4 0.5 select_convert_fusion.edge_ref
  11.9 4.5 %copy.24 = bf16[256,128,4,15]{1,0,3,2:T(8,128)(2,1)} copy(bf16[256,128,4,15]{1,3,2,0:T(8,128)(2,1)S(1)} %fusion.3) | data formatting | bytes 7864320 | tf_op jit(solution)/shard_map/gab,jtb->gajt/dot_general | solution.py:31
  16.4 0.0 copy-start.1
  16.4 1.2 %copy.25 = bf16[256,128,15]{1,0,2:T(8,128)(2,1)} copy(bf16[256,128,15]{1,2,0:T(8,128)(2,1)S(1)} %fusion.1) | data formatting | bytes 1966080 | tf_op jit(solution)/shard_map/gab,jtb->gajt/dot_general | solution.py:31
  17.6 0.0 collective-permute-done
  17.6 0.0 collective-permute-done.1
  17.6 0.1 broadcast_in_dim.23
  17.8 0.0 copy-done.1
  17.8 1.3 %concatenate.10.ext_ref = bf16[4,256,256]{2,1,0:T(8,128)(2,1)} concatenate(bf16[4,256,128]{2,1,0:T(8,128)(2,1)S(1)} %bitcast.25, bf16[4,256,14]{2,1,0:T(8,128)(2,1)S(1)} %collective-permute-done, bf16[4,256,18]{2,1,0:T(8,128)(2,1)S(1)} %broadcast_in_dim.22, bf16[4,256,1]{2,1,0:T(8,128)(2,1)S(1)} %broadcast_in_dim.23, bf16[4,256,81]{2,1,0:T(8,128)(2,1)S(1)} %broadcast_in_dim.44, ...), dimensions={2} | concatenate | bytes 1048576 | tf_op jit(solution)/shard_map/concatenate | solution.py:146
  19.2 6.2 %shard_map.64 = bf16[128,2,640]{2,1,0:T(2,128)(2,1)} custom-call(s32[1,256]{1,0:T(1,128)} %bitcast.26, f32[1,128]{1,0:T(1,128)} %select_convert_fusion.edge_ref, bf16[4,256,256]{2,1,0:T(8,128)(2,1)} %concatenate.10.ext_ref, bf16[4,15,256,128]{3,2,1,0:T(8,128)(2,1)} %bitcast.22), custom_call_target="tpu_custom_call" | custom-call | tf_op jit(solution)/shard_map/pallas_call | solution.py:107
  25.4 18.4 %all-to-all-start = ((bf16[128,2,640]{2,1,0:T(2,128)(2,1)}), bf16[128,2,640]{2,1,0:T(2,128)(2,1)S(1)}, u32[]{:S(2)}, u32[]{:S(2)}) async-start(bf16[128,2,640]{2,1,0:T(2,128)(2,1)} %shard_map.64), calls=%async_computation | async-start | bytes 655360 | tf_op jit(solution)/shard_map/all_to_all | solution.py:152
  43.8 0.3 iota_compare_fusion.4
  44.2 0.3 iota_compare_fusion.2
  44.5 1.9 %add_convert_fusion.select_ref = bf16[1024,1024]{1,0:T(8,128)(2,1)} fusion(pred[1024,256]{1,0:T(8,128)(4,1)S(1)} %get-tuple-element.10, pred[1024,256]{1,0:T(8,128)(4,1)S(1)} %get-tuple-element.11, pred[1024,256]{1,0:T(8,128)(4,1)S(1)} %get-tuple-element.12, pred[1024,256]{1,0:T(8,128)(4,1)S(1)} %get-tuple-element.13), kind=kLoop, calls=%fused_computation.1 | loop fusion | flops 4194304 | bytes 3145728 | tf_op jit(solution)/shard_map/concatenate | solution.py:156
  46.3 14.1 %all-to-all-done.data_ref = bf16[128,2,640]{2,1,0:T(2,128)(2,1)S(1)} async-done(((bf16[128,2,640]{2,1,0:T(2,128)(2,1)}), bf16[128,2,640]{2,1,0:T(2,128)(2,1)S(1)}, u32[]{:S(2)}, u32[]{:S(2)}) %all-to-all-start) | async-done | bytes 327712 | tf_op jit(solution)/shard_map/all_to_all | solution.py:152
  60.4 0.0 copy-start.2
  60.4 0.7 %copy-done.2 = bf16[128,2,640]{2,1,0:T(2,128)(2,1)} copy-done((bf16[128,2,640]{2,1,0:T(2,128)(2,1)}, bf16[128,2,640]{2,1,0:T(2,128)(2,1)S(1)}, u32[]{:S(2)}) %copy-start.2) | copy-done | bytes 327704
  61.1 5.4 %shard_map.65 = bf16[1024,128]{1,0:T(8,128)(2,1)} custom-call(bf16[1024,1024]{1,0:T(8,128)(2,1)} %add_convert_fusion.select_ref, bf16[128,2,640]{2,1,0:T(2,128)(2,1)} %copy-done.2, bf16[1,15,256,128]{3,2,1,0:T(8,128)(2,1)} %bitcast.23), custom_call_target="tpu_custom_call" | custom-call | tf_op jit(solution)/shard_map/pallas_call | solution.py:126
  (3 shorter events, 0.1 us)
Async XLA Ops:
  0.0 10.7 %copy-start = (bf16[15,15]{1,0:T(8,128)(2,1)S(1)}, bf16[15,15]{1,0:T(8,128)(2,1)}, u32[]{:S(2)}) copy-start(bf16[15,15]{1,0:T(8,128)(2,1)} %param.8) | copy-start | bytes 1354
  1.2 16.4 %collective-permute-start = (bf16[4,256,14]{2,1,0:T(8,128)(2,1)S(1)}, bf16[4,256,14]{2,1,0:T(8,128)(2,1)S(1)}, u32[]{:S(2)}, u32[]{:S(2)}) collective-permute-start(bf16[4,256,14]{2,1,0:T(8,128)(2,1)S(1)} %get-tuple-element.6), channel_id=1, source_target_pairs={{1,0},{2,1},{3,2},{5,4},{6,5},{7,6},{9,8},{10,9},{11,10},{13,12},{... | collective-permute-start | bytes 86024 | tf_op jit(solution)/shard_map/ppermute | solution.py:20
  2.5 15.1 %collective-permute-start.1 = (bf16[4,256,14]{2,1,0:T(8,128)(2,1)S(1)}, bf16[4,256,14]{2,1,0:T(8,128)(2,1)S(1)}, u32[]{:S(2)}, u32[]{:S(2)}) collective-permute-start(bf16[4,256,14]{2,1,0:T(8,128)(2,1)S(1)} %get-tuple-element.5), channel_id=1, source_target_pairs={{0,1},{1,2},{2,3},{4,5},{5,6},{6,7},{8,9},{9,10},{10,11},{12,13},{... | collective-permute-start | bytes 86024 | tf_op jit(solution)/shard_map/ppermute | solution.py:19
  16.4 1.4 %copy-start.1 = (bf16[1,4,256,128]{3,2,1,0:T(8,128)(2,1)S(1)}, bf16[1,4,256,128]{3,2,1,0:T(8,128)(2,1)}, u32[]{:S(2)}) copy-start(bf16[1,4,256,128]{3,2,1,0:T(8,128)(2,1)} %param.6) | copy-start | bytes 786436
  25.4 35.0 %all-to-all-start = ((bf16[128,2,640]{2,1,0:T(2,128)(2,1)}), bf16[128,2,640]{2,1,0:T(2,128)(2,1)S(1)}, u32[]{:S(2)}, u32[]{:S(2)}) async-start(bf16[128,2,640]{2,1,0:T(2,128)(2,1)} %shard_map.64), calls=%async_computation | async-start | bytes 655360 | tf_op jit(solution)/shard_map/all_to_all | solution.py:152
  60.4 0.7 %copy-start.2 = (bf16[128,2,640]{2,1,0:T(2,128)(2,1)}, bf16[128,2,640]{2,1,0:T(2,128)(2,1)S(1)}, u32[]{:S(2)}) copy-start(bf16[128,2,640]{2,1,0:T(2,128)(2,1)S(1)} %all-to-all-done.data_ref) | copy-start | bytes 983044

commit v15 on v10

--- a/solution.py
+++ b/solution.py
@@ -85,7 +85,7 @@
         mine = pltpu.roll(halo, (samples - reach - 2 * reach * c) % samples, 1).astype(jnp.bfloat16)
         parts.append(jnp.concatenate([data_ref[:, :, c * samples:(c + 1) * samples].reshape(rows, samples), mine], axis=1))
         selects.append((row == target + group * c).astype(jnp.bfloat16))
-    gathered = jnp.dot(jnp.concatenate(selects, axis=1), jnp.concatenate(parts, axis=0), preferred_element_type=jnp.float32)
+    gathered = sum(jnp.dot(sel, part, preferred_element_type=jnp.float32) for sel, part in zip(selects, parts))
     gathered = gathered.astype(jnp.bfloat16)
     acc = jnp.zeros((out_rows, LANES), jnp.float32)
     for first in range(0, taps, 2):

time: 63.7 us -> 63.7 us (level)
  no operation moved by 1% of the time
where the time goes in v15:
time: 63.7 us; the launch traced here: 63.3 us
  starting transfers between devices  24.4 us (38%)
  waiting for transfers between devices  13.9 us (22%)
  Pallas kernels  11.1 us (17%)
  local copies, waits for them, and re-layouts  9.92 us (16%)
  matrix products  2.58 us (4%)
  other arithmetic  1.37 us (2%)
    all_to_all x1, starting transfers between devices, on_device(): lax.all_to_all(packed, 'shot', split_axis=0, concat_axis=0, tiled=True)  18.5 us
    all_to_all x1, waiting for transfers between devices, on_device(): lax.all_to_all(packed, 'shot', split_axis=0, concat_axis=0, tiled=True)  13.9 us
    pallas_call x1, Pallas kernels, fan_call(): pl.pallas_call(kernel, grid=(comps,), in_specs=[pl.BlockSpec((1, rows), l...  6.25 us
    dot_general x2, local copies, waits for them, and re-layouts, circulant(): jnp.einsum('gab,jtb->gajt', tap_set, onehot, preferred_element_type=jnp.f...  5.76 us
    pallas_call x1, Pallas kernels, dip_call(): pl.pallas_call(kernel, out_shape=jax.ShapeDtypeStruct((rows * comps, LANE...  4.82 us
    ppermute x1, starting transfers between devices, time_halo(): lax.ppermute(lax.slice_in_dim(block, samples - width, None, axis=-1), axi...  4.59 us
    dot_general x2, matrix products, circulant(): jnp.einsum('gab,jtb->gajt', tap_set, onehot, preferred_element_type=jnp.f...  2.58 us
    concatenate x1, local copies, waits for them, and re-layouts, on_device(): ext = jnp.concatenate([block, high, gap1, live, gap2, low], axis=-1)  1.36 us
  transfers between devices with their start and end apart: 3, of which 1 were waited for; matrix products, arithmetic and copies ran while one was open for 16% of the time, Pallas kernels for 0%

profile of v15, /device:TPU:1, one launch (start us, length us, event | category | flops | bytes accessed | tf_op | source)
XLA Modules:
  0.0 63.3 jit_solution(5145672518230047723)
XLA Ops:
  0.0 0.0 copy-start
  0.0 1.2 %fusion.12 = (bf16[4,256,14]{2,1,0:T(8,128)(2,1)S(1)}, bf16[4,256,14]{2,1,0:T(8,128)(2,1)S(1)}) fusion(bf16[4,256,128]{2,1,0:T(8,128)(2,1)} %bitcast.24), kind=kLoop, calls=%fused_computation.22 | loop fusion | bytes 114688 | tf_op jit(solution)/shard_map/slice | solution.py:19
  1.2 1.3 %collective-permute-start = (bf16[4,256,14]{2,1,0:T(8,128)(2,1)S(1)}, bf16[4,256,14]{2,1,0:T(8,128)(2,1)S(1)}, u32[]{:S(2)}, u32[]{:S(2)}) collective-permute-start(bf16[4,256,14]{2,1,0:T(8,128)(2,1)S(1)} %get-tuple-element.6), channel_id=1, source_target_pairs={{1,0},{2,1},{3,2},{5,4},{6,5},{7,6},{9,8},{10,9},{11,10},{13,12},{... | collective-permute-start | bytes 86024 | tf_op jit(solution)/shard_map/ppermute | solution.py:20
  2.5 4.6 %collective-permute-start.1 = (bf16[4,256,14]{2,1,0:T(8,128)(2,1)S(1)}, bf16[4,256,14]{2,1,0:T(8,128)(2,1)S(1)}, u32[]{:S(2)}, u32[]{:S(2)}) collective-permute-start(bf16[4,256,14]{2,1,0:T(8,128)(2,1)S(1)} %get-tuple-element.5), channel_id=1, source_target_pairs={{0,1},{1,2},{2,3},{4,5},{5,6},{6,7},{8,9},{9,10},{10,11},{12,13},{... | collective-permute-start | bytes 86024 | tf_op jit(solution)/shard_map/ppermute | solution.py:19
  7.1 0.1 add_select_fusion
  7.1 0.7 %convert_reduce_fusion = bf16[256]{0:T(256)(128)(2,1)S(1)} fusion(s32[1,256]{1,0:T(1,128)} %param.9), kind=kLoop, calls=%fused_computation.20 | loop fusion | flops 256 | bytes 1536 | tf_op jit(solution)/shard_map/convert_element_type | solution.py:146
  7.8 1.9 %fusion.3 = bf16[256,128,4,15]{1,3,2,0:T(8,128)(2,1)S(1)} fusion(s32[256,128]{1,0:T(8,128)S(1)} %add_select_fusion, bf16[4,15,15]{2,0,1:T(4,128)(2,1)} %param.7), kind=kOutput, calls=%fused_computation.5 | convolution fusion | flops 59473920 | bytes 4065032 | tf_op jit(solution)/shard_map/gab,jtb->gajt/dot_general | solution.py:31
  9.8 0.5 select_convert_fusion.edge_ref
  10.3 0.0 copy-start.1
  10.3 4.5 %copy.24 = bf16[256,128,4,15]{1,0,3,2:T(8,128)(2,1)} copy(bf16[256,128,4,15]{1,3,2,0:T(8,128)(2,1)S(1)} %fusion.3) | data formatting | bytes 7864320 | tf_op jit(solution)/shard_map/gab,jtb->gajt/dot_general | solution.py:31
  14.9 0.0 collective-permute-done
  14.9 0.0 collective-permute-done.1
  14.9 0.1 broadcast_in_dim.42
  15.1 0.0 copy-done.1
  15.1 1.4 %concatenate.3.ext_ref = bf16[4,256,256]{2,1,0:T(8,128)(2,1)} concatenate(bf16[4,256,128]{2,1,0:T(8,128)(2,1)S(1)} %bitcast.25, bf16[4,256,14]{2,1,0:T(8,128)(2,1)S(1)} %collective-permute-done, bf16[4,256,18]{2,1,0:T(8,128)(2,1)S(1)} %broadcast_in_dim.22, bf16[4,256,1]{2,1,0:T(8,128)(2,1)S(1)} %broadcast_in_dim.42, bf16[4,256,81]{2,1,0:T(8,128)(2,1)S(1)} %broadcast_in_dim.43, ...), dimensions={2} | concatenate | bytes 1048576 | tf_op jit(solution)/shard_map/concatenate | solution.py:149
  16.4 6.2 %shard_map.64 = bf16[128,2,640]{2,1,0:T(2,128)(2,1)} custom-call(s32[1,256]{1,0:T(1,128)} %bitcast.26, f32[1,128]{1,0:T(1,128)} %select_convert_fusion.edge_ref, bf16[4,256,256]{2,1,0:T(8,128)(2,1)} %concatenate.3.ext_ref, bf16[4,15,256,128]{3,2,1,0:T(8,128)(2,1)} %bitcast.22), custom_call_target="tpu_custom_call" | custom-call | tf_op jit(solution)/shard_map/pallas_call | solution.py:110
  22.7 0.0 copy-start.3
  22.7 18.5 %all-to-all-start = ((bf16[128,2,640]{2,1,0:T(2,128)(2,1)}), bf16[128,2,640]{2,1,0:T(2,128)(2,1)S(1)}, u32[]{:S(2)}, u32[]{:S(2)}) async-start(bf16[128,2,640]{2,1,0:T(2,128)(2,1)} %shard_map.64), calls=%async_computation | async-start | bytes 655360 | tf_op jit(solution)/shard_map/all_to_all | solution.py:155
  41.2 0.0 copy-done
  41.2 0.6 fusion.1
  41.9 1.2 %copy.25 = bf16[256,128,15]{1,0,2:T(8,128)(2,1)} copy(bf16[256,128,15]{1,2,0:T(8,128)(2,1)S(1)} %fusion.1) | data formatting | bytes 1966080 | tf_op jit(solution)/shard_map/gab,jtb->gajt/dot_general | solution.py:31
  43.1 0.0 copy-done.3
  43.1 0.1 iota_add_fusion
  43.2 0.7 %add.51.target_ref = s32[1,256]{1,0:T(1,128)} reshape(s32[128,2]{1,0:T(8,128)S(1)} %iota_add_fusion) | data formatting | bytes 2048 | tf_op jit(solution)/shard_map/add | solution.py:157
  43.9 13.9 %all-to-all-done.data_ref = bf16[128,2,640]{2,1,0:T(2,128)(2,1)S(1)} async-done(((bf16[128,2,640]{2,1,0:T(2,128)(2,1)}), bf16[128,2,640]{2,1,0:T(2,128)(2,1)S(1)}, u32[]{:S(2)}, u32[]{:S(2)}) %all-to-all-start) | async-done | bytes 327712 | tf_op jit(solution)/shard_map/all_to_all | solution.py:155
  57.8 0.0 copy-start.2
  57.8 0.7 %copy-done.2 = bf16[128,2,640]{2,1,0:T(2,128)(2,1)} copy-done((bf16[128,2,640]{2,1,0:T(2,128)(2,1)}, bf16[128,2,640]{2,1,0:T(2,128)(2,1)S(1)}, u32[]{:S(2)}) %copy-start.2) | copy-done | bytes 327704
  58.5 4.8 %shard_map.65 = bf16[1024,128]{1,0:T(8,128)(2,1)} custom-call(s32[1,256]{1,0:T(1,128)} %add.51.target_ref, bf16[128,2,640]{2,1,0:T(2,128)(2,1)} %copy-done.2, bf16[1,15,256,128]{3,2,1,0:T(8,128)(2,1)} %bitcast.23), custom_call_target="tpu_custom_call" | custom-call | tf_op jit(solution)/shard_map/pallas_call | solution.py:129
  (3 shorter events, 0.1 us)
Async XLA Ops:
  0.0 41.2 %copy-start = (bf16[15,15]{1,0:T(8,128)(2,1)S(1)}, bf16[15,15]{1,0:T(8,128)(2,1)}, u32[]{:S(2)}) copy-start(bf16[15,15]{1,0:T(8,128)(2,1)} %param.8) | copy-start | bytes 1354
  1.2 13.7 %collective-permute-start = (bf16[4,256,14]{2,1,0:T(8,128)(2,1)S(1)}, bf16[4,256,14]{2,1,0:T(8,128)(2,1)S(1)}, u32[]{:S(2)}, u32[]{:S(2)}) collective-permute-start(bf16[4,256,14]{2,1,0:T(8,128)(2,1)S(1)} %get-tuple-element.6), channel_id=1, source_target_pairs={{1,0},{2,1},{3,2},{5,4},{6,5},{7,6},{9,8},{10,9},{11,10},{13,12},{... | collective-permute-start | bytes 86024 | tf_op jit(solution)/shard_map/ppermute | solution.py:20
  2.5 12.4 %collective-permute-start.1 = (bf16[4,256,14]{2,1,0:T(8,128)(2,1)S(1)}, bf16[4,256,14]{2,1,0:T(8,128)(2,1)S(1)}, u32[]{:S(2)}, u32[]{:S(2)}) collective-permute-start(bf16[4,256,14]{2,1,0:T(8,128)(2,1)S(1)} %get-tuple-element.5), channel_id=1, source_target_pairs={{0,1},{1,2},{2,3},{4,5},{5,6},{6,7},{8,9},{9,10},{10,11},{12,13},{... | collective-permute-start | bytes 86024 | tf_op jit(solution)/shard_map/ppermute | solution.py:19
  10.3 4.7 %copy-start.1 = (bf16[1,4,256,128]{3,2,1,0:T(8,128)(2,1)S(1)}, bf16[1,4,256,128]{3,2,1,0:T(8,128)(2,1)}, u32[]{:S(2)}) copy-start(bf16[1,4,256,128]{3,2,1,0:T(8,128)(2,1)} %param.6) | copy-start | bytes 786436
  22.7 20.4 %copy-start.3 = (s32[128]{0:T(128)S(1)}, s32[128]{0:T(128)}, u32[]{:S(2)}) copy-start(s32[128]{0:T(128)} %param.11) | copy-start | bytes 1540
  22.7 35.1 %all-to-all-start = ((bf16[128,2,640]{2,1,0:T(2,128)(2,1)}), bf16[128,2,640]{2,1,0:T(2,128)(2,1)S(1)}, u32[]{:S(2)}, u32[]{:S(2)}) async-start(bf16[128,2,640]{2,1,0:T(2,128)(2,1)} %shard_map.64), calls=%async_computation | async-start | bytes 655360 | tf_op jit(solution)/shard_map/all_to_all | solution.py:155
  57.8 0.7 %copy-start.2 = (bf16[128,2,640]{2,1,0:T(2,128)(2,1)}, bf16[128,2,640]{2,1,0:T(2,128)(2,1)S(1)}, u32[]{:S(2)}) copy-start(bf16[128,2,640]{2,1,0:T(2,128)(2,1)S(1)} %all-to-all-done.data_ref) | copy-start | bytes 983044

commit v16 on v10

--- a/solution.py
+++ b/solution.py
@@ -71,7 +71,9 @@
         out_ref[:, :, comps * samples:(comps + 1) * samples] = (halo_ref[...] * keep * edge_ref[...]).astype(out_ref.dtype).reshape(rows // 2, 2, samples)
 
 
-def dip_kernel(target_ref, data_ref, table_ref, out_ref, *, taps, group, comps):
+def dip_kernel(target_ref, source_ref, table_ref, out_ref, data_ref, sem, *, taps, group, comps):
+    fetch = pltpu.make_async_copy(source_ref, data_ref, sem)
+    fetch.start()
     rows = data_ref.shape[0] * data_ref.shape[1]
     samples = LANES
     reach = (taps - 1) // 2
@@ -79,12 +81,13 @@
     out_rows = out_ref.shape[0]
     target = target_ref[...]
     row = lax.broadcasted_iota(jnp.int32, (out_rows, rows), 0)
+    selects = [(row == target + group * c).astype(jnp.bfloat16) for c in range(comps)]
+    fetch.wait()
     halo = data_ref[:, :, comps * samples:(comps + 1) * samples].reshape(rows, samples).astype(jnp.float32)
-    selects, parts = [], []
+    parts = []
     for c in range(comps):
         mine = pltpu.roll(halo, (samples - reach - 2 * reach * c) % samples, 1).astype(jnp.bfloat16)
         parts.append(jnp.concatenate([data_ref[:, :, c * samples:(c + 1) * samples].reshape(rows, samples), mine], axis=1))
-        selects.append((row == target + group * c).astype(jnp.bfloat16))
     gathered = jnp.dot(jnp.concatenate(selects, axis=1), jnp.concatenate(parts, axis=0), preferred_element_type=jnp.float32)
     gathered = gathered.astype(jnp.bfloat16)
     acc = jnp.zeros((out_rows, LANES), jnp.float32)
@@ -126,9 +129,13 @@
     rows = data.shape[0] * data.shape[1]
     taps = tables.shape[1]
     kernel = functools.partial(dip_kernel, taps=taps, group=group, comps=comps)
+    vmem = pl.BlockSpec(memory_space=pltpu.VMEM)
     return pl.pallas_call(
         kernel,
+        in_specs=[vmem, pl.BlockSpec(memory_space=pl.ANY), vmem],
+        out_specs=vmem,
         out_shape=jax.ShapeDtypeStruct((rows * comps, LANES), jnp.bfloat16),
+        scratch_shapes=[pltpu.VMEM(data.shape, data.dtype), pltpu.SemaphoreType.DMA(())],
     )(target, data, tables)
 
 

time: 63.7 us -> 64.6 us (1.014)
  Pallas kernels: 11.1 us -> 11.9 us
    pallas_call x1, Pallas kernels: 4.81 us -> 5.69 us  [dip_call(): pl.pallas_call(kernel, in_specs=[vmem, pl.BlockSpec(memory_space=pl.ANY),...]
where the time goes in v16:
time: 64.6 us; the launch traced here: 64.2 us
  starting transfers between devices  24.4 us (38%)
  waiting for transfers between devices  13.9 us (22%)
  Pallas kernels  11.9 us (18%)
  local copies, waits for them, and re-layouts  9.92 us (15%)
  matrix products  2.58 us (4%)
  other arithmetic  1.37 us (2%)
    all_to_all x1, starting transfers between devices, on_device(): lax.all_to_all(packed, 'shot', split_axis=0, concat_axis=0, tiled=True)  18.5 us
    all_to_all x1, waiting for transfers between devices, on_device(): lax.all_to_all(packed, 'shot', split_axis=0, concat_axis=0, tiled=True)  13.9 us
    pallas_call x1, Pallas kernels, fan_call(): pl.pallas_call(kernel, grid=(comps,), in_specs=[pl.BlockSpec((1, rows), l...  6.25 us
    dot_general x2, local copies, waits for them, and re-layouts, circulant(): jnp.einsum('gab,jtb->gajt', tap_set, onehot, preferred_element_type=jnp.f...  5.76 us
    pallas_call x1, Pallas kernels, dip_call(): pl.pallas_call(kernel, in_specs=[vmem, pl.BlockSpec(memory_space=pl.ANY),...  5.69 us
    ppermute x1, starting transfers between devices, time_halo(): lax.ppermute(lax.slice_in_dim(block, samples - width, None, axis=-1), axi...  4.59 us
    dot_general x2, matrix products, circulant(): jnp.einsum('gab,jtb->gajt', tap_set, onehot, preferred_element_type=jnp.f...  2.58 us
    concatenate x1, local copies, waits for them, and re-layouts, on_device(): ext = jnp.concatenate([block, high, gap1, live, gap2, low], axis=-1)  1.36 us
  transfers between devices with their start and end apart: 3, of which 1 were waited for; matrix products, arithmetic and copies ran while one was open for 16% of the time, Pallas kernels for 0%

profile of v16, /device:TPU:1, one launch (start us, length us, event | category | flops | bytes accessed | tf_op | source)
XLA Modules:
  0.0 64.2 jit_solution(245459448877879789)
XLA Ops:
  0.0 0.0 copy-start
  0.0 1.2 %fusion.12 = (bf16[4,256,14]{2,1,0:T(8,128)(2,1)S(1)}, bf16[4,256,14]{2,1,0:T(8,128)(2,1)S(1)}) fusion(bf16[4,256,128]{2,1,0:T(8,128)(2,1)} %bitcast.24), kind=kLoop, calls=%fused_computation.22 | loop fusion | bytes 114688 | tf_op jit(solution)/shard_map/slice | solution.py:19
  1.2 1.3 %collective-permute-start = (bf16[4,256,14]{2,1,0:T(8,128)(2,1)S(1)}, bf16[4,256,14]{2,1,0:T(8,128)(2,1)S(1)}, u32[]{:S(2)}, u32[]{:S(2)}) collective-permute-start(bf16[4,256,14]{2,1,0:T(8,128)(2,1)S(1)} %get-tuple-element.6), channel_id=1, source_target_pairs={{1,0},{2,1},{3,2},{5,4},{6,5},{7,6},{9,8},{10,9},{11,10},{13,12},{... | collective-permute-start | bytes 86024 | tf_op jit(solution)/shard_map/ppermute | solution.py:20
  2.5 4.6 %collective-permute-start.1 = (bf16[4,256,14]{2,1,0:T(8,128)(2,1)S(1)}, bf16[4,256,14]{2,1,0:T(8,128)(2,1)S(1)}, u32[]{:S(2)}, u32[]{:S(2)}) collective-permute-start(bf16[4,256,14]{2,1,0:T(8,128)(2,1)S(1)} %get-tuple-element.5), channel_id=1, source_target_pairs={{0,1},{1,2},{2,3},{4,5},{5,6},{6,7},{8,9},{9,10},{10,11},{12,13},{... | collective-permute-start | bytes 86024 | tf_op jit(solution)/shard_map/ppermute | solution.py:19
  7.1 0.1 add_select_fusion
  7.1 0.7 %convert_reduce_fusion = bf16[256]{0:T(256)(128)(2,1)S(1)} fusion(s32[1,256]{1,0:T(1,128)} %param.9), kind=kLoop, calls=%fused_computation.20 | loop fusion | flops 256 | bytes 1536 | tf_op jit(solution)/shard_map/convert_element_type | solution.py:153
  7.8 1.9 %fusion.3 = bf16[256,128,4,15]{1,3,2,0:T(8,128)(2,1)S(1)} fusion(s32[256,128]{1,0:T(8,128)S(1)} %add_select_fusion, bf16[4,15,15]{2,0,1:T(4,128)(2,1)} %param.7), kind=kOutput, calls=%fused_computation.5 | convolution fusion | flops 59473920 | bytes 4065032 | tf_op jit(solution)/shard_map/gab,jtb->gajt/dot_general | solution.py:31
  9.8 0.5 select_convert_fusion.edge_ref
  10.3 0.0 copy-start.1
  10.3 4.5 %copy.24 = bf16[256,128,4,15]{1,0,3,2:T(8,128)(2,1)} copy(bf16[256,128,4,15]{1,3,2,0:T(8,128)(2,1)S(1)} %fusion.3) | data formatting | bytes 7864320 | tf_op jit(solution)/shard_map/gab,jtb->gajt/dot_general | solution.py:31
  14.9 0.0 collective-permute-done
  14.9 0.0 collective-permute-done.1
  14.9 0.1 broadcast_in_dim.42
  15.1 0.0 copy-done.1
  15.1 1.4 %concatenate.3.ext_ref = bf16[4,256,256]{2,1,0:T(8,128)(2,1)} concatenate(bf16[4,256,128]{2,1,0:T(8,128)(2,1)S(1)} %bitcast.25, bf16[4,256,14]{2,1,0:T(8,128)(2,1)S(1)} %collective-permute-done, bf16[4,256,18]{2,1,0:T(8,128)(2,1)S(1)} %broadcast_in_dim.22, bf16[4,256,1]{2,1,0:T(8,128)(2,1)S(1)} %broadcast_in_dim.42, bf16[4,256,81]{2,1,0:T(8,128)(2,1)S(1)} %broadcast_in_dim.43, ...), dimensions={2} | concatenate | bytes 1048576 | tf_op jit(solution)/shard_map/concatenate | solution.py:156
  16.4 6.2 %shard_map.64 = bf16[128,2,640]{2,1,0:T(2,128)(2,1)} custom-call(s32[1,256]{1,0:T(1,128)} %bitcast.26, f32[1,128]{1,0:T(1,128)} %select_convert_fusion.edge_ref, bf16[4,256,256]{2,1,0:T(8,128)(2,1)} %concatenate.3.ext_ref, bf16[4,15,256,128]{3,2,1,0:T(8,128)(2,1)} %bitcast.22), custom_call_target="tpu_custom_call" | custom-call | tf_op jit(solution)/shard_map/pallas_call | solution.py:113
  22.7 0.0 copy-start.3
  22.7 18.5 %all-to-all-start = ((bf16[128,2,640]{2,1,0:T(2,128)(2,1)}), bf16[128,2,640]{2,1,0:T(2,128)(2,1)S(1)}, u32[]{:S(2)}, u32[]{:S(2)}) async-start(bf16[128,2,640]{2,1,0:T(2,128)(2,1)} %shard_map.64), calls=%async_computation | async-start | bytes 655360 | tf_op jit(solution)/shard_map/all_to_all | solution.py:162
  41.2 0.0 copy-done
  41.2 0.6 fusion.1
  41.9 1.2 %copy.25 = bf16[256,128,15]{1,0,2:T(8,128)(2,1)} copy(bf16[256,128,15]{1,2,0:T(8,128)(2,1)S(1)} %fusion.1) | data formatting | bytes 1966080 | tf_op jit(solution)/shard_map/gab,jtb->gajt/dot_general | solution.py:31
  43.1 0.0 copy-done.3
  43.1 0.1 iota_add_fusion
  43.2 0.7 %add.51.target_ref = s32[1,256]{1,0:T(1,128)} reshape(s32[128,2]{1,0:T(8,128)S(1)} %iota_add_fusion) | data formatting | bytes 2048 | tf_op jit(solution)/shard_map/add | solution.py:164
  43.9 13.9 %all-to-all-done.source_ref = bf16[128,2,640]{2,1,0:T(2,128)(2,1)S(1)} async-done(((bf16[128,2,640]{2,1,0:T(2,128)(2,1)}), bf16[128,2,640]{2,1,0:T(2,128)(2,1)S(1)}, u32[]{:S(2)}, u32[]{:S(2)}) %all-to-all-start) | async-done | bytes 327712 | tf_op jit(solution)/shard_map/all_to_all | solution.py:162
  57.8 0.0 copy-start.2
  57.8 0.7 %copy-done.2 = bf16[128,2,640]{2,1,0:T(2,128)(2,1)} copy-done((bf16[128,2,640]{2,1,0:T(2,128)(2,1)}, bf16[128,2,640]{2,1,0:T(2,128)(2,1)S(1)}, u32[]{:S(2)}) %copy-start.2) | copy-done | bytes 327704
  58.5 5.7 %shard_map.65 = bf16[1024,128]{1,0:T(8,128)(2,1)} custom-call(s32[1,256]{1,0:T(1,128)} %add.51.target_ref, bf16[128,2,640]{2,1,0:T(2,128)(2,1)} %copy-done.2, bf16[1,15,256,128]{3,2,1,0:T(8,128)(2,1)} %bitcast.23), custom_call_target="tpu_custom_call" | custom-call | tf_op jit(solution)/shard_map/pallas_call | solution.py:133
  (3 shorter events, 0.1 us)
Async XLA Ops:
  0.0 41.2 %copy-start = (bf16[15,15]{1,0:T(8,128)(2,1)S(1)}, bf16[15,15]{1,0:T(8,128)(2,1)}, u32[]{:S(2)}) copy-start(bf16[15,15]{1,0:T(8,128)(2,1)} %param.8) | copy-start | bytes 1354
  1.2 13.7 %collective-permute-start = (bf16[4,256,14]{2,1,0:T(8,128)(2,1)S(1)}, bf16[4,256,14]{2,1,0:T(8,128)(2,1)S(1)}, u32[]{:S(2)}, u32[]{:S(2)}) collective-permute-start(bf16[4,256,14]{2,1,0:T(8,128)(2,1)S(1)} %get-tuple-element.6), channel_id=1, source_target_pairs={{1,0},{2,1},{3,2},{5,4},{6,5},{7,6},{9,8},{10,9},{11,10},{13,12},{... | collective-permute-start | bytes 86024 | tf_op jit(solution)/shard_map/ppermute | solution.py:20
  2.5 12.4 %collective-permute-start.1 = (bf16[4,256,14]{2,1,0:T(8,128)(2,1)S(1)}, bf16[4,256,14]{2,1,0:T(8,128)(2,1)S(1)}, u32[]{:S(2)}, u32[]{:S(2)}) collective-permute-start(bf16[4,256,14]{2,1,0:T(8,128)(2,1)S(1)} %get-tuple-element.5), channel_id=1, source_target_pairs={{0,1},{1,2},{2,3},{4,5},{5,6},{6,7},{8,9},{9,10},{10,11},{12,13},{... | collective-permute-start | bytes 86024 | tf_op jit(solution)/shard_map/ppermute | solution.py:19
  10.3 4.7 %copy-start.1 = (bf16[1,4,256,128]{3,2,1,0:T(8,128)(2,1)S(1)}, bf16[1,4,256,128]{3,2,1,0:T(8,128)(2,1)}, u32[]{:S(2)}) copy-start(bf16[1,4,256,128]{3,2,1,0:T(8,128)(2,1)} %param.6) | copy-start | bytes 786436
  22.7 20.4 %copy-start.3 = (s32[128]{0:T(128)S(1)}, s32[128]{0:T(128)}, u32[]{:S(2)}) copy-start(s32[128]{0:T(128)} %param.11) | copy-start | bytes 1540
  22.7 35.1 %all-to-all-start = ((bf16[128,2,640]{2,1,0:T(2,128)(2,1)}), bf16[128,2,640]{2,1,0:T(2,128)(2,1)S(1)}, u32[]{:S(2)}, u32[]{:S(2)}) async-start(bf16[128,2,640]{2,1,0:T(2,128)(2,1)} %shard_map.64), calls=%async_computation | async-start | bytes 655360 | tf_op jit(solution)/shard_map/all_to_all | solution.py:162
  57.8 0.7 %copy-start.2 = (bf16[128,2,640]{2,1,0:T(2,128)(2,1)}, bf16[128,2,640]{2,1,0:T(2,128)(2,1)S(1)}, u32[]{:S(2)}) copy-start(bf16[128,2,640]{2,1,0:T(2,128)(2,1)S(1)} %all-to-all-done.source_ref) | copy-start | bytes 983044

commit v17 on v10

--- a/solution.py
+++ b/solution.py
@@ -71,7 +71,7 @@
         out_ref[:, :, comps * samples:(comps + 1) * samples] = (halo_ref[...] * keep * edge_ref[...]).astype(out_ref.dtype).reshape(rows // 2, 2, samples)
 
 
-def dip_kernel(target_ref, data_ref, table_ref, out_ref, *, taps, group, comps):
+def dip_kernel(target_ref, data_ref, table_ref, out_ref, acc_ref, *, taps, group, comps):
     rows = data_ref.shape[0] * data_ref.shape[1]
     samples = LANES
     reach = (taps - 1) // 2
@@ -87,20 +87,16 @@
         selects.append((row == target + group * c).astype(jnp.bfloat16))
     gathered = jnp.dot(jnp.concatenate(selects, axis=1), jnp.concatenate(parts, axis=0), preferred_element_type=jnp.float32)
     gathered = gathered.astype(jnp.bfloat16)
-    acc = jnp.zeros((out_rows, LANES), jnp.float32)
+    acc_ref[...] = jnp.zeros((out_rows, LANES), jnp.float32)
     for first in range(0, taps, 2):
         pair = list(range(first, min(first + 2, taps)))
         tables = jnp.concatenate([table_ref[0, a] for a in pair], axis=1)
         both = jnp.dot(gathered, tables, preferred_element_type=jnp.float32)
         for k, a in enumerate(pair):
-            part = both[:, k * samples:(k + 1) * samples]
             shift = stride * (a - reach)
-            if shift > 0:
-                part = jnp.concatenate([part[shift:], jnp.zeros((shift, LANES), jnp.float32)], axis=0)
-            elif shift < 0:
-                part = jnp.concatenate([jnp.zeros((-shift, LANES), jnp.float32), part[:shift]], axis=0)
-            acc = acc + part
-    out_ref[...] = acc.astype(out_ref.dtype)
+            lo, hi = max(0, -shift), out_rows - max(0, shift)
+            acc_ref[lo:hi, :] += both[lo + shift:hi + shift, k * samples:(k + 1) * samples]
+    out_ref[...] = acc_ref[...].astype(out_ref.dtype)
 
 
 def fan_call(place, edge, ext, tables, live_col):
@@ -129,6 +125,7 @@
     return pl.pallas_call(
         kernel,
         out_shape=jax.ShapeDtypeStruct((rows * comps, LANES), jnp.bfloat16),
+        scratch_shapes=[pltpu.VMEM((rows * comps, LANES), jnp.float32)],
     )(target, data, tables)
 
 

time: 63.7 us -> 63.7 us (level)
  no operation moved by 1% of the time
where the time goes in v17:
time: 63.7 us; the launch traced here: 63.3 us
  starting transfers between devices  24.4 us (38%)
  waiting for transfers between devices  13.9 us (22%)
  Pallas kernels  11.1 us (17%)
  local copies, waits for them, and re-layouts  9.92 us (16%)
  matrix products  2.58 us (4%)
  other arithmetic  1.37 us (2%)
    all_to_all x1, starting transfers between devices, on_device(): lax.all_to_all(packed, 'shot', split_axis=0, concat_axis=0, tiled=True)  18.5 us
    all_to_all x1, waiting for transfers between devices, on_device(): lax.all_to_all(packed, 'shot', split_axis=0, concat_axis=0, tiled=True)  13.9 us
    pallas_call x1, Pallas kernels, fan_call(): pl.pallas_call(kernel, grid=(comps,), in_specs=[pl.BlockSpec((1, rows), l...  6.25 us
    dot_general x2, local copies, waits for them, and re-layouts, circulant(): jnp.einsum('gab,jtb->gajt', tap_set, onehot, preferred_element_type=jnp.f...  5.76 us
    pallas_call x1, Pallas kernels, dip_call(): pl.pallas_call(kernel, out_shape=jax.ShapeDtypeStruct((rows * comps, LANE...  4.81 us
    ppermute x1, starting transfers between devices, time_halo(): lax.ppermute(lax.slice_in_dim(block, samples - width, None, axis=-1), axi...  4.59 us
    dot_general x2, matrix products, circulant(): jnp.einsum('gab,jtb->gajt', tap_set, onehot, preferred_element_type=jnp.f...  2.58 us
    concatenate x1, local copies, waits for them, and re-layouts, on_device(): ext = jnp.concatenate([block, high, gap1, live, gap2, low], axis=-1)  1.36 us
  transfers between devices with their start and end apart: 3, of which 1 were waited for; matrix products, arithmetic and copies ran while one was open for 16% of the time, Pallas kernels for 0%

profile of v17, /device:TPU:1, one launch (start us, length us, event | category | flops | bytes accessed | tf_op | source)
XLA Modules:
  0.0 63.3 jit_solution(14101129514479075984)
XLA Ops:
  0.0 0.0 copy-start
  0.0 1.2 %fusion.12 = (bf16[4,256,14]{2,1,0:T(8,128)(2,1)S(1)}, bf16[4,256,14]{2,1,0:T(8,128)(2,1)S(1)}) fusion(bf16[4,256,128]{2,1,0:T(8,128)(2,1)} %bitcast.24), kind=kLoop, calls=%fused_computation.22 | loop fusion | bytes 114688 | tf_op jit(solution)/shard_map/slice | solution.py:19
  1.2 1.3 %collective-permute-start = (bf16[4,256,14]{2,1,0:T(8,128)(2,1)S(1)}, bf16[4,256,14]{2,1,0:T(8,128)(2,1)S(1)}, u32[]{:S(2)}, u32[]{:S(2)}) collective-permute-start(bf16[4,256,14]{2,1,0:T(8,128)(2,1)S(1)} %get-tuple-element.6), channel_id=1, source_target_pairs={{1,0},{2,1},{3,2},{5,4},{6,5},{7,6},{9,8},{10,9},{11,10},{13,12},{... | collective-permute-start | bytes 86024 | tf_op jit(solution)/shard_map/ppermute | solution.py:20
  2.5 4.6 %collective-permute-start.1 = (bf16[4,256,14]{2,1,0:T(8,128)(2,1)S(1)}, bf16[4,256,14]{2,1,0:T(8,128)(2,1)S(1)}, u32[]{:S(2)}, u32[]{:S(2)}) collective-permute-start(bf16[4,256,14]{2,1,0:T(8,128)(2,1)S(1)} %get-tuple-element.5), channel_id=1, source_target_pairs={{0,1},{1,2},{2,3},{4,5},{5,6},{6,7},{8,9},{9,10},{10,11},{12,13},{... | collective-permute-start | bytes 86024 | tf_op jit(solution)/shard_map/ppermute | solution.py:19
  7.1 0.1 add_select_fusion
  7.1 0.7 %convert_reduce_fusion = bf16[256]{0:T(256)(128)(2,1)S(1)} fusion(s32[1,256]{1,0:T(1,128)} %param.9), kind=kLoop, calls=%fused_computation.20 | loop fusion | flops 256 | bytes 1536 | tf_op jit(solution)/shard_map/convert_element_type | solution.py:143
  7.8 1.9 %fusion.3 = bf16[256,128,4,15]{1,3,2,0:T(8,128)(2,1)S(1)} fusion(s32[256,128]{1,0:T(8,128)S(1)} %add_select_fusion, bf16[4,15,15]{2,0,1:T(4,128)(2,1)} %param.7), kind=kOutput, calls=%fused_computation.5 | convolution fusion | flops 59473920 | bytes 4065032 | tf_op jit(solution)/shard_map/gab,jtb->gajt/dot_general | solution.py:31
  9.8 0.5 select_convert_fusion.edge_ref
  10.3 0.0 copy-start.1
  10.3 4.5 %copy.24 = bf16[256,128,4,15]{1,0,3,2:T(8,128)(2,1)} copy(bf16[256,128,4,15]{1,3,2,0:T(8,128)(2,1)S(1)} %fusion.3) | data formatting | bytes 7864320 | tf_op jit(solution)/shard_map/gab,jtb->gajt/dot_general | solution.py:31
  14.9 0.0 collective-permute-done
  14.9 0.0 collective-permute-done.1
  14.9 0.1 broadcast_in_dim.42
  15.1 0.0 copy-done.1
  15.1 1.4 %concatenate.3.ext_ref = bf16[4,256,256]{2,1,0:T(8,128)(2,1)} concatenate(bf16[4,256,128]{2,1,0:T(8,128)(2,1)S(1)} %bitcast.25, bf16[4,256,14]{2,1,0:T(8,128)(2,1)S(1)} %collective-permute-done, bf16[4,256,18]{2,1,0:T(8,128)(2,1)S(1)} %broadcast_in_dim.22, bf16[4,256,1]{2,1,0:T(8,128)(2,1)S(1)} %broadcast_in_dim.42, bf16[4,256,81]{2,1,0:T(8,128)(2,1)S(1)} %broadcast_in_dim.43, ...), dimensions={2} | concatenate | bytes 1048576 | tf_op jit(solution)/shard_map/concatenate | solution.py:146
  16.4 6.2 %shard_map.64 = bf16[128,2,640]{2,1,0:T(2,128)(2,1)} custom-call(s32[1,256]{1,0:T(1,128)} %bitcast.26, f32[1,128]{1,0:T(1,128)} %select_convert_fusion.edge_ref, bf16[4,256,256]{2,1,0:T(8,128)(2,1)} %concatenate.3.ext_ref, bf16[4,15,256,128]{3,2,1,0:T(8,128)(2,1)} %bitcast.22), custom_call_target="tpu_custom_call" | custom-call | tf_op jit(solution)/shard_map/pallas_call | solution.py:106
  22.7 0.0 copy-start.3
  22.7 18.5 %all-to-all-start = ((bf16[128,2,640]{2,1,0:T(2,128)(2,1)}), bf16[128,2,640]{2,1,0:T(2,128)(2,1)S(1)}, u32[]{:S(2)}, u32[]{:S(2)}) async-start(bf16[128,2,640]{2,1,0:T(2,128)(2,1)} %shard_map.64), calls=%async_computation | async-start | bytes 655360 | tf_op jit(solution)/shard_map/all_to_all | solution.py:152
  41.2 0.0 copy-done
  41.2 0.6 fusion.1
  41.9 1.2 %copy.25 = bf16[256,128,15]{1,0,2:T(8,128)(2,1)} copy(bf16[256,128,15]{1,2,0:T(8,128)(2,1)S(1)} %fusion.1) | data formatting | bytes 1966080 | tf_op jit(solution)/shard_map/gab,jtb->gajt/dot_general | solution.py:31
  43.1 0.0 copy-done.3
  43.1 0.1 iota_add_fusion
  43.2 0.7 %add.51.target_ref = s32[1,256]{1,0:T(1,128)} reshape(s32[128,2]{1,0:T(8,128)S(1)} %iota_add_fusion) | data formatting | bytes 2048 | tf_op jit(solution)/shard_map/add | solution.py:154
  43.9 13.9 %all-to-all-done.data_ref = bf16[128,2,640]{2,1,0:T(2,128)(2,1)S(1)} async-done(((bf16[128,2,640]{2,1,0:T(2,128)(2,1)}), bf16[128,2,640]{2,1,0:T(2,128)(2,1)S(1)}, u32[]{:S(2)}, u32[]{:S(2)}) %all-to-all-start) | async-done | bytes 327712 | tf_op jit(solution)/shard_map/all_to_all | solution.py:152
  57.8 0.0 copy-start.2
  57.8 0.7 %copy-done.2 = bf16[128,2,640]{2,1,0:T(2,128)(2,1)} copy-done((bf16[128,2,640]{2,1,0:T(2,128)(2,1)}, bf16[128,2,640]{2,1,0:T(2,128)(2,1)S(1)}, u32[]{:S(2)}) %copy-start.2) | copy-done | bytes 327704
  58.5 4.8 %shard_map.65 = bf16[1024,128]{1,0:T(8,128)(2,1)} custom-call(s32[1,256]{1,0:T(1,128)} %add.51.target_ref, bf16[128,2,640]{2,1,0:T(2,128)(2,1)} %copy-done.2, bf16[1,15,256,128]{3,2,1,0:T(8,128)(2,1)} %bitcast.23), custom_call_target="tpu_custom_call" | custom-call | tf_op jit(solution)/shard_map/pallas_call | solution.py:125
  (3 shorter events, 0.1 us)
Async XLA Ops:
  0.0 41.2 %copy-start = (bf16[15,15]{1,0:T(8,128)(2,1)S(1)}, bf16[15,15]{1,0:T(8,128)(2,1)}, u32[]{:S(2)}) copy-start(bf16[15,15]{1,0:T(8,128)(2,1)} %param.8) | copy-start | bytes 1354
  1.2 13.7 %collective-permute-start = (bf16[4,256,14]{2,1,0:T(8,128)(2,1)S(1)}, bf16[4,256,14]{2,1,0:T(8,128)(2,1)S(1)}, u32[]{:S(2)}, u32[]{:S(2)}) collective-permute-start(bf16[4,256,14]{2,1,0:T(8,128)(2,1)S(1)} %get-tuple-element.6), channel_id=1, source_target_pairs={{1,0},{2,1},{3,2},{5,4},{6,5},{7,6},{9,8},{10,9},{11,10},{13,12},{... | collective-permute-start | bytes 86024 | tf_op jit(solution)/shard_map/ppermute | solution.py:20
  2.5 12.4 %collective-permute-start.1 = (bf16[4,256,14]{2,1,0:T(8,128)(2,1)S(1)}, bf16[4,256,14]{2,1,0:T(8,128)(2,1)S(1)}, u32[]{:S(2)}, u32[]{:S(2)}) collective-permute-start(bf16[4,256,14]{2,1,0:T(8,128)(2,1)S(1)} %get-tuple-element.5), channel_id=1, source_target_pairs={{0,1},{1,2},{2,3},{4,5},{5,6},{6,7},{8,9},{9,10},{10,11},{12,13},{... | collective-permute-start | bytes 86024 | tf_op jit(solution)/shard_map/ppermute | solution.py:19
  10.3 4.7 %copy-start.1 = (bf16[1,4,256,128]{3,2,1,0:T(8,128)(2,1)S(1)}, bf16[1,4,256,128]{3,2,1,0:T(8,128)(2,1)}, u32[]{:S(2)}) copy-start(bf16[1,4,256,128]{3,2,1,0:T(8,128)(2,1)} %param.6) | copy-start | bytes 786436
  22.7 20.4 %copy-start.3 = (s32[128]{0:T(128)S(1)}, s32[128]{0:T(128)}, u32[]{:S(2)}) copy-start(s32[128]{0:T(128)} %param.11) | copy-start | bytes 1540
  22.7 35.1 %all-to-all-start = ((bf16[128,2,640]{2,1,0:T(2,128)(2,1)}), bf16[128,2,640]{2,1,0:T(2,128)(2,1)S(1)}, u32[]{:S(2)}, u32[]{:S(2)}) async-start(bf16[128,2,640]{2,1,0:T(2,128)(2,1)} %shard_map.64), calls=%async_computation | async-start | bytes 655360 | tf_op jit(solution)/shard_map/all_to_all | solution.py:152
  57.8 0.7 %copy-start.2 = (bf16[128,2,640]{2,1,0:T(2,128)(2,1)}, bf16[128,2,640]{2,1,0:T(2,128)(2,1)S(1)}, u32[]{:S(2)}) copy-start(bf16[128,2,640]{2,1,0:T(2,128)(2,1)S(1)} %all-to-all-done.data_ref) | copy-start | bytes 983044

commit v18 on v10

--- a/solution.py
+++ b/solution.py
@@ -33,40 +33,44 @@
 
 
 def fan_kernel(place_ref, edge_ref, ext_ref, table_ref, out_ref, scr_ref, halo_ref, *, taps, live_col, comps):
-    c = pl.program_id(0)
+    step = pl.program_id(0)
+    per = ext_ref.shape[0]
     rows = ext_ref.shape[1]
     samples = LANES
     reach = (taps - 1) // 2
     place = place_ref[...]
     select = (lax.broadcasted_iota(jnp.int32, (rows, rows), 0) == place).astype(jnp.bfloat16)
-    ordered = jnp.dot(select, ext_ref[0], preferred_element_type=jnp.float32)
-    keep = ordered[:, live_col:live_col + 1]
+    lane = lax.broadcasted_iota(jnp.int32, (rows, LANES), 1)
     zeros = jnp.zeros((8, EXT), jnp.float32)
     scr_ref[0:8, :] = zeros
     scr_ref[rows + 8:rows + 16, :] = zeros
-    scr_ref[8:rows + 8, :] = ordered
-    acc = jnp.zeros((rows, LANES), jnp.float32)
-    acc_h = jnp.zeros((rows, LANES), jnp.float32)
-    for a in range(taps):
-        table = table_ref[0, a]
-        both = jnp.concatenate([table, jnp.concatenate([table[samples:], table[:samples]], axis=0)], axis=1)
-        moved = scr_ref[pl.ds(a + 8 - reach, rows), :].astype(jnp.bfloat16)
-        part = jnp.dot(moved, both, preferred_element_type=jnp.float32)
-        acc = acc + part[:, :samples]
-        acc_h = acc_h + part[:, samples:]
-    out_ref[:, :, pl.ds(pl.multiple_of(c * samples, samples), samples)] = (acc * keep).astype(out_ref.dtype).reshape(rows // 2, 2, samples)
-    lane = lax.broadcasted_iota(jnp.int32, (rows, LANES), 1)
-    for k in range(comps):
-        @pl.when(c == k)
-        def _():
-            moved = pltpu.roll(acc_h, reach + 2 * reach * k, 1)
-            mine = jnp.where((lane >= 2 * reach * k) & (lane < 2 * reach * (k + 1)), moved, 0.0)
-            if k == 0:
-                halo_ref[...] = mine
-            else:
-                halo_ref[...] += mine
+    keep = None
+    for i in range(per):
+        ordered = jnp.dot(select, ext_ref[i], preferred_element_type=jnp.float32)
+        keep = ordered[:, live_col:live_col + 1]
+        scr_ref[8:rows + 8, :] = ordered
+        acc = jnp.zeros((rows, LANES), jnp.float32)
+        acc_h = jnp.zeros((rows, LANES), jnp.float32)
+        for a in range(taps):
+            table = table_ref[i, a]
+            both = jnp.concatenate([table, jnp.concatenate([table[samples:], table[:samples]], axis=0)], axis=1)
+            moved = scr_ref[pl.ds(a + 8 - reach, rows), :].astype(jnp.bfloat16)
+            part = jnp.dot(moved, both, preferred_element_type=jnp.float32)
+            acc = acc + part[:, :samples]
+            acc_h = acc_h + part[:, samples:]
+        c = step * per + i
+        out_ref[:, :, pl.ds(pl.multiple_of(c * samples, samples), samples)] = (acc * keep).astype(out_ref.dtype).reshape(rows // 2, 2, samples)
+        for k in range(i, comps, per):
+            @pl.when(c == k)
+            def _():
+                moved = pltpu.roll(acc_h, reach + 2 * reach * k, 1)
+                mine = jnp.where((lane >= 2 * reach * k) & (lane < 2 * reach * (k + 1)), moved, 0.0)
+                if k == 0:
+                    halo_ref[...] = mine
+                else:
+                    halo_ref[...] += mine
 
-    @pl.when(c == comps - 1)
+    @pl.when(step == pl.num_programs(0) - 1)
     def _():
         out_ref[:, :, comps * samples:(comps + 1) * samples] = (halo_ref[...] * keep * edge_ref[...]).astype(out_ref.dtype).reshape(rows // 2, 2, samples)
 
@@ -109,12 +113,12 @@
     kernel = functools.partial(fan_kernel, taps=taps, live_col=live_col, comps=comps)
     return pl.pallas_call(
         kernel,
-        grid=(comps,),
+        grid=(comps // 2,),
         in_specs=[
             pl.BlockSpec((1, rows), lambda c: (0, 0)),
             pl.BlockSpec((1, LANES), lambda c: (0, 0)),
-            pl.BlockSpec((1, rows, EXT), lambda c: (c, 0, 0)),
-            pl.BlockSpec((1, taps, EXT, LANES), lambda c: (c, 0, 0, 0)),
+            pl.BlockSpec((2, rows, EXT), lambda c: (c, 0, 0)),
+            pl.BlockSpec((2, taps, EXT, LANES), lambda c: (c, 0, 0, 0)),
         ],
         out_specs=pl.BlockSpec((rows // 2, 2, (comps + 1) * LANES), lambda c: (0, 0, 0)),
         out_shape=jax.ShapeDtypeStruct((rows // 2, 2, (comps + 1) * LANES), jnp.bfloat16),

time: 63.7 us -> 65.4 us (1.027)
  Pallas kernels: 11.1 us -> 12.8 us
    pallas_call x1, Pallas kernels: 6.25 us -> 7.97 us  [fan_call(): pl.pallas_call(kernel, grid=(comps // 2,), in_specs=[pl.BlockSpec((1, row...]
where the time goes in v18:
time: 65.4 us; the launch traced here: 65.1 us
  starting transfers between devices  24.4 us (37%)
  waiting for transfers between devices  13.9 us (21%)
  Pallas kernels  12.8 us (20%)
  local copies, waits for them, and re-layouts  9.92 us (15%)
  matrix products  2.58 us (4%)
  other arithmetic  1.37 us (2%)
    all_to_all x1, starting transfers between devices, on_device(): lax.all_to_all(packed, 'shot', split_axis=0, concat_axis=0, tiled=True)  18.5 us
    all_to_all x1, waiting for transfers between devices, on_device(): lax.all_to_all(packed, 'shot', split_axis=0, concat_axis=0, tiled=True)  13.9 us
    pallas_call x1, Pallas kernels, fan_call(): pl.pallas_call(kernel, grid=(comps // 2,), in_specs=[pl.BlockSpec((1, row...  7.97 us
    dot_general x2, local copies, waits for them, and re-layouts, circulant(): jnp.einsum('gab,jtb->gajt', tap_set, onehot, preferred_element_type=jnp.f...  5.76 us
    pallas_call x1, Pallas kernels, dip_call(): pl.pallas_call(kernel, out_shape=jax.ShapeDtypeStruct((rows * comps, LANE...  4.81 us
    ppermute x1, starting transfers between devices, time_halo(): lax.ppermute(lax.slice_in_dim(block, samples - width, None, axis=-1), axi...  4.59 us
    dot_general x2, matrix products, circulant(): jnp.einsum('gab,jtb->gajt', tap_set, onehot, preferred_element_type=jnp.f...  2.58 us
    concatenate x1, local copies, waits for them, and re-layouts, on_device(): ext = jnp.concatenate([block, high, gap1, live, gap2, low], axis=-1)  1.36 us
  transfers between devices with their start and end apart: 3, of which 1 were waited for; matrix products, arithmetic and copies ran while one was open for 16% of the time, Pallas kernels for 0%

profile of v18, /device:TPU:1, one launch (start us, length us, event | category | flops | bytes accessed | tf_op | source)
XLA Modules:
  0.0 65.1 jit_solution(17342116596061357685)
XLA Ops:
  0.0 0.0 copy-start
  0.0 1.2 %fusion.12 = (bf16[4,256,14]{2,1,0:T(8,128)(2,1)S(1)}, bf16[4,256,14]{2,1,0:T(8,128)(2,1)S(1)}) fusion(bf16[4,256,128]{2,1,0:T(8,128)(2,1)} %bitcast.24), kind=kLoop, calls=%fused_computation.22 | loop fusion | bytes 114688 | tf_op jit(solution)/shard_map/slice | solution.py:19
  1.2 1.3 %collective-permute-start = (bf16[4,256,14]{2,1,0:T(8,128)(2,1)S(1)}, bf16[4,256,14]{2,1,0:T(8,128)(2,1)S(1)}, u32[]{:S(2)}, u32[]{:S(2)}) collective-permute-start(bf16[4,256,14]{2,1,0:T(8,128)(2,1)S(1)} %get-tuple-element.6), channel_id=1, source_target_pairs={{1,0},{2,1},{3,2},{5,4},{6,5},{7,6},{9,8},{10,9},{11,10},{13,12},{... | collective-permute-start | bytes 86024 | tf_op jit(solution)/shard_map/ppermute | solution.py:20
  2.5 4.6 %collective-permute-start.1 = (bf16[4,256,14]{2,1,0:T(8,128)(2,1)S(1)}, bf16[4,256,14]{2,1,0:T(8,128)(2,1)S(1)}, u32[]{:S(2)}, u32[]{:S(2)}) collective-permute-start(bf16[4,256,14]{2,1,0:T(8,128)(2,1)S(1)} %get-tuple-element.5), channel_id=1, source_target_pairs={{0,1},{1,2},{2,3},{4,5},{5,6},{6,7},{8,9},{9,10},{10,11},{12,13},{... | collective-permute-start | bytes 86024 | tf_op jit(solution)/shard_map/ppermute | solution.py:19
  7.1 0.1 add_select_fusion
  7.1 0.7 %convert_reduce_fusion = bf16[256]{0:T(256)(128)(2,1)S(1)} fusion(s32[1,256]{1,0:T(1,128)} %param.9), kind=kLoop, calls=%fused_computation.20 | loop fusion | flops 256 | bytes 1536 | tf_op jit(solution)/shard_map/convert_element_type | solution.py:150
  7.8 2.0 %fusion.3 = bf16[256,128,4,15]{1,3,2,0:T(8,128)(2,1)S(1)} fusion(s32[256,128]{1,0:T(8,128)S(1)} %add_select_fusion, bf16[4,15,15]{2,0,1:T(4,128)(2,1)} %param.7), kind=kOutput, calls=%fused_computation.5 | convolution fusion | flops 59473920 | bytes 4065032 | tf_op jit(solution)/shard_map/gab,jtb->gajt/dot_general | solution.py:31
  9.8 0.5 select_convert_fusion.edge_ref
  10.3 0.0 copy-start.1
  10.3 4.5 %copy.24 = bf16[256,128,4,15]{1,0,3,2:T(8,128)(2,1)} copy(bf16[256,128,4,15]{1,3,2,0:T(8,128)(2,1)S(1)} %fusion.3) | data formatting | bytes 7864320 | tf_op jit(solution)/shard_map/gab,jtb->gajt/dot_general | solution.py:31
  14.9 0.0 collective-permute-done
  14.9 0.0 collective-permute-done.1
  14.9 0.1 broadcast_in_dim.42
  15.1 0.0 copy-done.1
  15.1 1.4 %concatenate.3.ext_ref = bf16[4,256,256]{2,1,0:T(8,128)(2,1)} concatenate(bf16[4,256,128]{2,1,0:T(8,128)(2,1)S(1)} %bitcast.25, bf16[4,256,14]{2,1,0:T(8,128)(2,1)S(1)} %collective-permute-done, bf16[4,256,18]{2,1,0:T(8,128)(2,1)S(1)} %broadcast_in_dim.22, bf16[4,256,1]{2,1,0:T(8,128)(2,1)S(1)} %broadcast_in_dim.42, bf16[4,256,81]{2,1,0:T(8,128)(2,1)S(1)} %broadcast_in_dim.43, ...), dimensions={2} | concatenate | bytes 1048576 | tf_op jit(solution)/shard_map/concatenate | solution.py:153
  16.4 8.0 %shard_map.64 = bf16[128,2,640]{2,1,0:T(2,128)(2,1)} custom-call(s32[1,256]{1,0:T(1,128)} %bitcast.26, f32[1,128]{1,0:T(1,128)} %select_convert_fusion.edge_ref, bf16[4,256,256]{2,1,0:T(8,128)(2,1)} %concatenate.3.ext_ref, bf16[4,15,256,128]{3,2,1,0:T(8,128)(2,1)} %bitcast.22), custom_call_target="tpu_custom_call" | custom-call | tf_op jit(solution)/shard_map/pallas_call | solution.py:114
  24.4 0.0 copy-start.3
  24.4 18.5 %all-to-all-start = ((bf16[128,2,640]{2,1,0:T(2,128)(2,1)}), bf16[128,2,640]{2,1,0:T(2,128)(2,1)S(1)}, u32[]{:S(2)}, u32[]{:S(2)}) async-start(bf16[128,2,640]{2,1,0:T(2,128)(2,1)} %shard_map.64), calls=%async_computation | async-start | bytes 655360 | tf_op jit(solution)/shard_map/all_to_all | solution.py:159
  43.0 0.0 copy-done
  43.0 0.6 fusion.1
  43.6 1.2 %copy.25 = bf16[256,128,15]{1,0,2:T(8,128)(2,1)} copy(bf16[256,128,15]{1,2,0:T(8,128)(2,1)S(1)} %fusion.1) | data formatting | bytes 1966080 | tf_op jit(solution)/shard_map/gab,jtb->gajt/dot_general | solution.py:31
  44.8 0.0 copy-done.3
  44.8 0.1 iota_add_fusion
  44.9 0.7 %add.51.target_ref = s32[1,256]{1,0:T(1,128)} reshape(s32[128,2]{1,0:T(8,128)S(1)} %iota_add_fusion) | data formatting | bytes 2048 | tf_op jit(solution)/shard_map/add | solution.py:161
  45.6 13.9 %all-to-all-done.data_ref = bf16[128,2,640]{2,1,0:T(2,128)(2,1)S(1)} async-done(((bf16[128,2,640]{2,1,0:T(2,128)(2,1)}), bf16[128,2,640]{2,1,0:T(2,128)(2,1)S(1)}, u32[]{:S(2)}, u32[]{:S(2)}) %all-to-all-start) | async-done | bytes 327712 | tf_op jit(solution)/shard_map/all_to_all | solution.py:159
  59.5 0.0 copy-start.2
  59.5 0.7 %copy-done.2 = bf16[128,2,640]{2,1,0:T(2,128)(2,1)} copy-done((bf16[128,2,640]{2,1,0:T(2,128)(2,1)}, bf16[128,2,640]{2,1,0:T(2,128)(2,1)S(1)}, u32[]{:S(2)}) %copy-start.2) | copy-done | bytes 327704
  60.3 4.8 %shard_map.65 = bf16[1024,128]{1,0:T(8,128)(2,1)} custom-call(s32[1,256]{1,0:T(1,128)} %add.51.target_ref, bf16[128,2,640]{2,1,0:T(2,128)(2,1)} %copy-done.2, bf16[1,15,256,128]{3,2,1,0:T(8,128)(2,1)} %bitcast.23), custom_call_target="tpu_custom_call" | custom-call | tf_op jit(solution)/shard_map/pallas_call | solution.py:133
  (3 shorter events, 0.1 us)
Async XLA Ops:
  0.0 43.0 %copy-start = (bf16[15,15]{1,0:T(8,128)(2,1)S(1)}, bf16[15,15]{1,0:T(8,128)(2,1)}, u32[]{:S(2)}) copy-start(bf16[15,15]{1,0:T(8,128)(2,1)} %param.8) | copy-start | bytes 1354
  1.2 13.7 %collective-permute-start = (bf16[4,256,14]{2,1,0:T(8,128)(2,1)S(1)}, bf16[4,256,14]{2,1,0:T(8,128)(2,1)S(1)}, u32[]{:S(2)}, u32[]{:S(2)}) collective-permute-start(bf16[4,256,14]{2,1,0:T(8,128)(2,1)S(1)} %get-tuple-element.6), channel_id=1, source_target_pairs={{1,0},{2,1},{3,2},{5,4},{6,5},{7,6},{9,8},{10,9},{11,10},{13,12},{... | collective-permute-start | bytes 86024 | tf_op jit(solution)/shard_map/ppermute | solution.py:20
  2.5 12.4 %collective-permute-start.1 = (bf16[4,256,14]{2,1,0:T(8,128)(2,1)S(1)}, bf16[4,256,14]{2,1,0:T(8,128)(2,1)S(1)}, u32[]{:S(2)}, u32[]{:S(2)}) collective-permute-start(bf16[4,256,14]{2,1,0:T(8,128)(2,1)S(1)} %get-tuple-element.5), channel_id=1, source_target_pairs={{0,1},{1,2},{2,3},{4,5},{5,6},{6,7},{8,9},{9,10},{10,11},{12,13},{... | collective-permute-start | bytes 86024 | tf_op jit(solution)/shard_map/ppermute | solution.py:19
  10.3 4.7 %copy-start.1 = (bf16[1,4,256,128]{3,2,1,0:T(8,128)(2,1)S(1)}, bf16[1,4,256,128]{3,2,1,0:T(8,128)(2,1)}, u32[]{:S(2)}) copy-start(bf16[1,4,256,128]{3,2,1,0:T(8,128)(2,1)} %param.6) | copy-start | bytes 786436
  24.4 20.4 %copy-start.3 = (s32[128]{0:T(128)S(1)}, s32[128]{0:T(128)}, u32[]{:S(2)}) copy-start(s32[128]{0:T(128)} %param.11) | copy-start | bytes 1540
  24.4 35.1 %all-to-all-start = ((bf16[128,2,640]{2,1,0:T(2,128)(2,1)}), bf16[128,2,640]{2,1,0:T(2,128)(2,1)S(1)}, u32[]{:S(2)}, u32[]{:S(2)}) async-start(bf16[128,2,640]{2,1,0:T(2,128)(2,1)} %shard_map.64), calls=%async_computation | async-start | bytes 655360 | tf_op jit(solution)/shard_map/all_to_all | solution.py:159
  59.5 0.7 %copy-start.2 = (bf16[128,2,640]{2,1,0:T(2,128)(2,1)}, bf16[128,2,640]{2,1,0:T(2,128)(2,1)S(1)}, u32[]{:S(2)}) copy-start(bf16[128,2,640]{2,1,0:T(2,128)(2,1)S(1)} %all-to-all-done.data_ref) | copy-start | bytes 983044
